TPU v7x, 128 devices: a whole 4x4x4 slice. The times are simulated.
128 devices in a mesh: alpha: 8 (over y, x_lo), beta: 16 (over x_hi, z, core).
Axes of the slice: x: 4 (x_hi: 2, x_lo: 2; x = x_hi * 2 + x_lo), y: 4, z: 4, core: 2. Of those that a mesh axis runs over, the one named last changes fastest.
Arguments:
- coefficients: bfloat16 [2048, 4096], P('alpha', 'beta'), may hold values from -6 to 6
- diagonal: float32 [2048, 4096], P('alpha', 'beta'), may hold values from 0.3 to 3
- integrals: bfloat16 [324, 324], replicated, may hold values from -0.02734375 to 0.02734375
- alpha_row: int32 [324, 2048], replicated, may hold values from 0 to 2047
- alpha_sign: int32 [324, 2048], replicated, may hold values from -1 to 1
- beta_block: int32 [64, 324], P('beta'), may hold values from 0 to 63
- beta_sign: int32 [64, 20736], P('beta'), may hold values from -1 to 1
- block_irrep: int32 [32], replicated, may hold values from 0 to 7, as said below
Outputs:
- sigma: float32 [2048, 4096], P('alpha', 'beta')
Inputs may be any that keep to these rules, and one draw needn't show every extreme that they name: `block_irrep`: irrep 0 is the window's. The 4 blocks held by one index of alpha include 1 to 4 blocks of irrep 0, and some index holds 4 of them.
All inputs are finite; a program needn't handle non-finite values.
Results may differ from a plain program's by a relative error of at most 0.0003.
Values may be sent and summed in bfloat16 or wider, within the bound.
A program may use at most 128 MiB of HBM per device.

v0:
```python
import jax
import jax.numpy as jnp
from jax import lax
from jax.sharding import PartitionSpec as P


def locate(target_rank, live_flags, per_device):
    block_iota = jnp.arange(live_flags.shape[0], dtype=jnp.int32)
    ranks_all = jnp.cumsum(live_flags) - live_flags
    matches = (live_flags == 1) & (ranks_all == target_rank)
    block_id = jnp.sum(jnp.where(matches, block_iota, 0))
    owner_id = block_id // per_device
    before = jnp.sum(jnp.where(block_iota < owner_id * per_device, live_flags, 0))
    return (block_id, owner_id, target_rank - before)


def block_terms(
    block_id,
    coeff_blocks,
    alpha_row,
    alpha_sign,
    integrals,
    target_table,
    beta_signs,
    block_len,
    total_blocks,
):
    src_blocks = coeff_blocks.shape[0]
    pair_count = integrals.shape[0]
    step_rows = min(16, block_len)
    pieces = []
    for sub_step in range(block_len // step_rows):
        first_row = block_id * block_len + sub_step * step_rows
        row_ids = lax.dynamic_slice_in_dim(alpha_row, first_row, step_rows, 1)
        sign_vals = lax.dynamic_slice_in_dim(alpha_sign, first_row, step_rows, 1).astype(
            jnp.bfloat16
        )
        picked = coeff_blocks[:, row_ids, :] * sign_vals[None, :, :, None]
        picked = picked.reshape(src_blocks, pair_count, step_rows * block_len)
        mixed_rows = jnp.einsum(
            "qp,spx->sqx", integrals, picked, preferred_element_type=jnp.float32
        )
        weighted = (
            mixed_rows.reshape(src_blocks, pair_count, step_rows, block_len)
            * beta_signs[:, :, None, :]
        )
        summed = jnp.dot(
            target_table,
            weighted.reshape(src_blocks * pair_count, step_rows * block_len),
            precision=lax.Precision.HIGHEST,
            preferred_element_type=jnp.float32,
        )
        pieces.append(
            summed.reshape(total_blocks, step_rows, block_len)
            .transpose(1, 0, 2)
            .reshape(step_rows, total_blocks * block_len)
        )
    return jnp.concatenate(pieces, axis=0)


def on_device(
    coefficients, diagonal, integrals, alpha_row, alpha_sign, beta_block, beta_sign, block_irrep
):
    alpha_rank = lax.axis_index("alpha")
    pair_count = integrals.shape[0]
    local_rows, local_cols = coefficients.shape
    block_len = beta_sign.shape[1] // pair_count
    per_device = local_rows // block_len
    src_blocks = local_cols // block_len
    total_blocks = lax.axis_size("beta") * src_blocks
    gathered = lax.all_gather(coefficients, "alpha", axis=0, tiled=True)
    live_flags = (block_irrep == 0).astype(jnp.int32)
    live_rows = jnp.repeat(live_flags, block_len)
    gathered = gathered * live_rows[:, None].astype(jnp.bfloat16)
    window_rows = gathered.shape[0]
    coeff_blocks = gathered.reshape(window_rows, src_blocks, block_len).transpose(1, 0, 2)
    beta_ids = beta_block.reshape(-1)
    target_iota = jnp.arange(total_blocks, dtype=jnp.int32)
    target_table = (target_iota[:, None] == beta_ids[None, :]).astype(jnp.float32)
    beta_signs = beta_sign.reshape(src_blocks, pair_count, block_len).astype(jnp.float32)
    block_iota = jnp.arange(live_flags.shape[0], dtype=jnp.int32)
    base_own = jnp.sum(jnp.where(block_iota < alpha_rank * per_device, live_flags, 0))
    own_flags = lax.dynamic_slice_in_dim(live_flags, alpha_rank * per_device, per_device, 0)
    own_count = jnp.sum(own_flags)

    def rank_of(slot_idx):
        return base_own + slot_idx

    empty = jnp.zeros((per_device, block_len, total_blocks * block_len), jnp.float32)

    def one_task(slot_idx, buffer):
        block_id, owner_id, live_pos = locate(rank_of(slot_idx), live_flags, per_device)
        rows_out = block_terms(
            block_id,
            coeff_blocks,
            alpha_row,
            alpha_sign,
            integrals,
            target_table,
            beta_signs,
            block_len,
            total_blocks,
        )
        return lax.dynamic_update_index_in_dim(buffer, rows_out, slot_idx, 0)

    buffer = lax.fori_loop(0, own_count, one_task, empty)
    whole = lax.psum(buffer, "beta")
    summed = lax.dynamic_slice_in_dim(whole, lax.axis_index("beta") * local_cols, local_cols, 2)
    own_pos = jnp.cumsum(own_flags) - own_flags
    placed = summed[own_pos]
    placed = jnp.where(own_flags[:, None, None] == 1, placed, jnp.zeros_like(placed)).reshape(
        local_rows, local_cols
    )
    own_live_rows = jnp.repeat(own_flags, block_len)
    total = diagonal * coefficients.astype(jnp.float32) + placed
    return jnp.where(own_live_rows[:, None] == 1, total, jnp.zeros_like(total))


def solution(mesh):
    return jax.shard_map(
        on_device,
        mesh=mesh,
        in_specs=(
            P("alpha", "beta"),
            P("alpha", "beta"),
            P(),
            P(),
            P(),
            P("beta", None),
            P("beta", None),
            P(),
        ),
        out_specs=P("alpha", "beta"),
        check_vma=False,
    )
```

profile of v0, /device:TPU:1, one launch (start us, length us, event | category | flops | bytes accessed | tf_op | source)
XLA Modules:
  0.0 1145.5 jit_solution(6576279985161262132)
XLA Ops:
  10.2 3.5 copy.33
  16.9 31.4 %all-gather.2.cloned.1.call-done = bf16[2048,256]{0,1:T(8,128)(2,1)} async-done(((bf16[256,256]{0,1:T(8,128)(2,1)}), bf16[2048,256]{0,1:T(8,128)(2,1)}) %all-gather.2.cloned.1.call-update) | async-done | bytes 1048592 | tf_op jit(solution)/shard_map/all_gather | solution.py:71
  50.9 2.5 broadcast_in_dim.82
  53.4 464.3 %while.13 = (s32[]{:T(128)}, f32[4,64,4096]{2,1,0:T(8,128)}, s32[]{:T(128)}, s32[32]{0:T(128)S(1)}, s32[]{:T(128)}, /*index=5*/s32[32]{0:T(128)S(1)}, s32[324,20...) while((s32[]{:T(128)}, f32[4,64,4096]{2,1,0:T(8,128)}, ...), condition=%wide.region_5.6_spmd.clone, body=%wide.region_3.5_spmd.clone.sunk | while | flops 7528891392 | bytes 255579248 | solution.py:106
  55.9 2.3 compare_select_fusion.7
  58.3 15.2 %gather_fusion.1 = bf16[5184,4,64]{2,1,0:T(4,128)(2,1)} fusion(bf16[4,2048,64]{2,0,1:T(4,128)(2,1)S(1)} %get-tuple-element.379, s32[6144]{0:T(1024)S(1)} %pad_clamp_fusion.10), kind=kCustom, calls=%fused_computation.2.clone.clone.1 | custom fusion | bytes 5329152 | tf_op jit(solution)/shard_map/while/body/gather | solution.py:38
  73.6 10.7 copy.54
  85.2 2.2 bitcast_multiply_fusion.9
  87.4 4.0 convolution_bitcast_fusion.9
  91.4 4.4 reshape.331
  95.8 6.1 copy.55
  101.9 4.9 mul.224
  106.8 8.0 mul.225
  114.7 8.8 fusion.86
  125.8 15.2 %gather_fusion.2 = bf16[5184,4,64]{2,1,0:T(4,128)(2,1)} fusion(bf16[4,2048,64]{2,0,1:T(4,128)(2,1)S(1)} %get-tuple-element.379, s32[6144]{0:T(1024)S(1)} %pad_clamp_fusion.11), kind=kCustom, calls=%fused_computation.1.clone.clone.1 | custom fusion | bytes 5329152 | tf_op jit(solution)/shard_map/while/body/gather | solution.py:38
  141.0 10.7 copy.57
  151.8 2.2 bitcast_multiply_fusion.10
  154.0 4.0 convolution_bitcast_fusion.10
  158.0 4.3 reshape.335
  162.3 6.1 copy.58
  168.5 8.8 fusion.87
  179.5 15.2 %gather_fusion = bf16[5184,4,64]{2,1,0:T(4,128)(2,1)} fusion(bf16[4,2048,64]{2,0,1:T(4,128)(2,1)S(1)} %get-tuple-element.379, s32[6144]{0:T(1024)S(1)} %pad_clamp_fusion.9), kind=kCustom, calls=%fused_computation.3.clone.clone.1 | custom fusion | bytes 5329152 | tf_op jit(solution)/shard_map/while/body/gather | solution.py:38
  194.8 10.7 copy.51
  205.5 2.2 bitcast_multiply_fusion.8
  207.8 4.0 convolution_bitcast_fusion.8
  211.8 4.3 reshape.327
  216.1 6.1 copy.52
  222.2 8.8 fusion.85
  233.2 15.2 %gather_fusion.3 = bf16[5184,4,64]{2,1,0:T(4,128)(2,1)} fusion(bf16[4,2048,64]{2,0,1:T(4,128)(2,1)S(1)} %get-tuple-element.379, s32[6144]{0:T(1024)S(1)} %pad_clamp_fusion.12), kind=kCustom, calls=%fused_computation.clone.clone.1 | custom fusion | bytes 5329152 | tf_op jit(solution)/shard_map/while/body/gather | solution.py:38
  248.5 10.7 copy.60
  259.3 2.2 bitcast_multiply_fusion.11
  261.5 4.0 convolution_bitcast_fusion.11
  265.5 4.3 reshape.339
  269.8 6.1 copy.61
  275.9 6.6 fusion.88
  287.7 2.5 compare_select_fusion.7
  290.3 15.2 %gather_fusion.1 = bf16[5184,4,64]{2,1,0:T(4,128)(2,1)} fusion(bf16[4,2048,64]{2,0,1:T(4,128)(2,1)S(1)} %get-tuple-element.379, s32[6144]{0:T(1024)S(1)} %pad_clamp_fusion.10), kind=kCustom, calls=%fused_computation.2.clone.clone.1 | custom fusion | bytes 5329152 | tf_op jit(solution)/shard_map/while/body/gather | solution.py:38
  305.5 10.7 copy.54
  317.1 2.2 bitcast_multiply_fusion.9
  319.3 4.0 convolution_bitcast_fusion.9
  323.3 4.4 reshape.331
  327.7 6.1 copy.55
  333.8 4.9 mul.224
  338.7 8.0 mul.225
  346.7 8.8 fusion.86
  357.7 15.2 %gather_fusion.2 = bf16[5184,4,64]{2,1,0:T(4,128)(2,1)} fusion(bf16[4,2048,64]{2,0,1:T(4,128)(2,1)S(1)} %get-tuple-element.379, s32[6144]{0:T(1024)S(1)} %pad_clamp_fusion.11), kind=kCustom, calls=%fused_computation.1.clone.clone.1 | custom fusion | bytes 5329152 | tf_op jit(solution)/shard_map/while/body/gather | solution.py:38
  373.0 10.7 copy.57
  386.0 4.0 convolution_bitcast_fusion.10
  389.9 4.3 reshape.335
  394.3 6.1 copy.58
  400.4 8.8 fusion.87
  411.5 15.2 %gather_fusion = bf16[5184,4,64]{2,1,0:T(4,128)(2,1)} fusion(bf16[4,2048,64]{2,0,1:T(4,128)(2,1)S(1)} %get-tuple-element.379, s32[6144]{0:T(1024)S(1)} %pad_clamp_fusion.9), kind=kCustom, calls=%fused_computation.3.clone.clone.1 | custom fusion | bytes 5329152 | tf_op jit(solution)/shard_map/while/body/gather | solution.py:38
  426.7 10.7 copy.51
  439.7 4.0 convolution_bitcast_fusion.8
  443.7 4.3 reshape.327
  448.0 6.1 copy.52
  454.2 8.8 fusion.85
  465.2 15.2 %gather_fusion.3 = bf16[5184,4,64]{2,1,0:T(4,128)(2,1)} fusion(bf16[4,2048,64]{2,0,1:T(4,128)(2,1)S(1)} %get-tuple-element.379, s32[6144]{0:T(1024)S(1)} %pad_clamp_fusion.12), kind=kCustom, calls=%fused_computation.clone.clone.1 | custom fusion | bytes 5329152 | tf_op jit(solution)/shard_map/while/body/gather | solution.py:38
  480.4 10.7 copy.60
  493.4 4.0 convolution_bitcast_fusion.11
  497.4 4.3 reshape.339
  501.7 6.1 copy.61
  507.9 6.6 fusion.88
  518.0 618.4 %all-reduce.2.cloned.1.call-done = f32[4,64,4096]{2,1,0:T(8,128)} async-done(((f32[4,64,4096]{2,1,0:T(8,128)}), f32[4,64,4096]{2,1,0:T(8,128)}) %all-reduce.2.cloned.1.call-update) | async-done | bytes 4194320 | tf_op jit(solution)/shard_map/psum | solution.py:107
  (100 shorter events, 41.2 us)
Async XLA Ops:
  6.5 9.7 copy-start.5
  6.5 7.1 copy-start.2
  6.5 8.4 copy-start.4
  6.5 41.7 %all-gather.2.cloned.1.call-start = ((), (), s32[]{:S(2)}) async-start(), calls=%async_computation | async-start | bytes 1179648 | tf_op jit(solution)/shard_map/all_gather | solution.py:71
  8.3 1128.0 %all-reduce.2.cloned.1.call-start = ((), (), s32[]{:S(2)}) async-start(), calls=%async_computation.1 | async-start | bytes 8388608 | tf_op jit(solution)/shard_map/psum | solution.py:107
  13.9 39.5 %copy-start = (bf16[324,324]{1,0:T(8,128)(2,1)S(1)}, bf16[324,324]{1,0:T(8,128)(2,1)}, u32[]{:S(2)}) copy-start(bf16[324,324]{1,0:T(8,128)(2,1)} %param.12) | copy-start | bytes 629860
  53.4 464.4 %copy-start.7 = (pred[4]{0:T(512)(128)(4,1)S(1)}, pred[4]{0:T(512)(128)(4,1)}, u32[]{:S(2)}) copy-start(pred[4]{0:T(512)(128)(4,1)} %get-tuple-element.219) | copy-start | bytes 16
  53.4 464.5 %copy-start.6 = (s32[4]{0:T(128)S(1)}, s32[4]{0:T(128)}, u32[]{:S(2)}) copy-start(s32[4]{0:T(128)} %get-tuple-element.229) | copy-start | bytes 52
  517.7 620.1 %copy-start.1 = (bf16[256,256]{1,0:T(8,128)(2,1)S(1)}, bf16[256,256]{1,0:T(8,128)(2,1)}, u32[]{:S(2)}) copy-start(bf16[256,256]{1,0:T(8,128)(2,1)} %param.10) | copy-start | bytes 393220
  517.7 620.1 %copy-start.3 = (f32[256,256]{1,0:T(8,128)S(1)}, f32[256,256]{1,0:T(8,128)}, u32[]{:S(2)}) copy-start(f32[256,256]{1,0:T(8,128)} %param.11) | copy-start | bytes 786436
Sparse Core Ops, SparseCore 0:
  8.9 39.2 all-gather.1
  517.9 618.3 all-reduce.1
where the time goes:
time: 1150 us
  waiting for transfers between devices  650 us (57%)
  local copies, waits for them, and re-layouts  344 us (30%)
  matrix products  97.6 us (8%)
  other arithmetic  35.6 us (3%)
  between operations  13.5 us (1%)
    psum x1, waiting for transfers between devices, on_device(): whole = lax.psum(buffer, 'beta')  618 us
    gather x16, local copies, waits for them, and re-layouts, block_terms(): picked = coeff_blocks[:, row_ids, :] * sign_vals[None, :, :, None]  207 us
    reshape x14, local copies, waits for them, and re-layouts, block_terms(): mixed_rows.reshape(src_blocks, pair_count, step_rows, block_len)  71.5 us
    dot_general x8, matrix products, block_terms(): jnp.dot(target_table, weighted.reshape(src_blocks * pair_count, step_rows...  65.9 us
    mul x6, local copies, waits for them, and re-layouts, block_terms(): mixed_rows.reshape(src_blocks, pair_count, step_rows, block_len)  38 us
    dot_general x8, matrix products, block_terms(): jnp.einsum('qp,spx->sqx', integrals, picked, preferred_element_type=jnp.f...  31.8 us
    all_gather x1, waiting for transfers between devices, on_device(): gathered = lax.all_gather(coefficients, 'alpha', axis=0, tiled=True)  31.4 us
  transfers between devices with their start and end apart: 2, of which 2 were waited for; matrix products, arithmetic and copies ran while one was open for 1% of the time, Pallas kernels for 0%

commit v1 on v0

v1 whole, which is shorter than its diff:
```python
import jax
import jax.numpy as jnp
from jax import lax
from jax.sharding import PartitionSpec as P


def split_bf16(values):
    rounded = lax.reduce_precision(values, exponent_bits=8, mantissa_bits=7)
    return rounded.astype(jnp.bfloat16), (values - rounded).astype(jnp.bfloat16)


def on_device(
    coefficients, diagonal, integrals, alpha_row, alpha_sign, beta_block, beta_sign, block_irrep
):
    alpha_rank = lax.axis_index("alpha")
    pair_count = integrals.shape[0]
    local_rows, local_cols = coefficients.shape
    block_len = beta_sign.shape[1] // pair_count
    per_device = local_rows // block_len
    src_blocks = local_cols // block_len
    total_blocks = lax.axis_size("beta") * src_blocks

    gathered = lax.all_gather(coefficients, "alpha", axis=0, tiled=True)
    live_flags = (block_irrep == 0).astype(jnp.int32)
    live_rows = jnp.repeat(live_flags, block_len)
    gathered = gathered * live_rows[:, None].astype(jnp.bfloat16)
    window_rows = gathered.shape[0]
    coeff3 = gathered.reshape(window_rows, src_blocks, block_len)

    beta_ids = beta_block.T.reshape(-1)
    target_iota = jnp.arange(total_blocks, dtype=jnp.int32)
    target_table = (target_iota[:, None] == beta_ids[None, :]).astype(jnp.bfloat16)
    signs_qs = (
        beta_sign.reshape(src_blocks, pair_count, block_len).transpose(1, 0, 2).astype(jnp.float32)
    )

    own_flags = lax.dynamic_slice_in_dim(live_flags, alpha_rank * per_device, per_device, 0)
    own_count = jnp.sum(own_flags)
    own_pos = jnp.cumsum(own_flags) - own_flags
    local_iota = jnp.arange(per_device, dtype=jnp.int32)

    dims = lax.GatherDimensionNumbers(
        offset_dims=(1, 3), collapsed_slice_dims=(0,), start_index_map=(0,)
    )

    def one_block(slot_idx, buffer):
        local_blk = jnp.sum(jnp.where((own_flags == 1) & (own_pos == slot_idx), local_iota, 0))
        first_row = (alpha_rank * per_device + local_blk) * block_len
        row_ids = lax.dynamic_slice_in_dim(alpha_row, first_row, block_len, 1)
        sign_vals = lax.dynamic_slice_in_dim(alpha_sign, first_row, block_len, 1).astype(
            jnp.bfloat16
        )
        picked = lax.gather(
            coeff3,
            row_ids[:, :, None],
            dims,
            slice_sizes=(1, src_blocks, block_len),
            mode=lax.GatherScatterMode.PROMISE_IN_BOUNDS,
        )
        picked = picked * sign_vals[:, None, :, None]
        mixed = jnp.dot(
            integrals,
            picked.reshape(pair_count, src_blocks * block_len * block_len),
            preferred_element_type=jnp.float32,
        ).reshape(pair_count, src_blocks, block_len, block_len)
        weighted = mixed * signs_qs[:, :, None, :]
        high, low = split_bf16(
            weighted.reshape(pair_count * src_blocks, block_len * block_len)
        )
        summed = jnp.dot(target_table, high, preferred_element_type=jnp.float32) + jnp.dot(
            target_table, low, preferred_element_type=jnp.float32
        )
        rows_out = (
            summed.reshape(total_blocks, block_len, block_len)
            .transpose(1, 0, 2)
            .reshape(block_len, total_blocks * block_len)
        )
        return lax.dynamic_update_index_in_dim(buffer, rows_out, local_blk, 0)

    empty = jnp.zeros((per_device, block_len, total_blocks * block_len), jnp.float32)
    buffer = lax.fori_loop(0, own_count, one_block, empty)
    summed = lax.psum_scatter(buffer, "beta", scatter_dimension=2, tiled=True)
    placed = summed.reshape(local_rows, local_cols)
    own_live_rows = jnp.repeat(own_flags, block_len)
    total = diagonal * coefficients.astype(jnp.float32) + placed
    return jnp.where(own_live_rows[:, None] == 1, total, jnp.zeros_like(total))


def solution(mesh):
    return jax.shard_map(
        on_device,
        mesh=mesh,
        in_specs=(
            P("alpha", "beta"),
            P("alpha", "beta"),
            P(),
            P(),
            P(),
            P("beta", None),
            P("beta", None),
            P(),
        ),
        out_specs=P("alpha", "beta"),
        check_vma=False,
    )
```

time: 1150 us -> 1100 us (0.957)
  waiting for transfers between devices: 650 us -> 819 us
  local copies, waits for them, and re-layouts: 344 us -> 192 us
  matrix products: 97.6 us -> 43.4 us
  other arithmetic: 35.6 us -> 14.5 us
    reduce_scatter x0 -> x1, waiting for transfers between devices: none -> 789 us  [on_device(): summed = lax.psum_scatter(buffer, 'beta', scatter_dimension=2, tiled=True)]
    psum x1 -> x0, waiting for transfers between devices: 618 us -> none  [on_device(): whole = lax.psum(buffer, 'beta')]
    gather x17 -> x2, local copies, waits for them, and re-layouts: 208 us -> 95 us  [one_block(): lax.gather(coeff3, row_ids[:, :, None], dims, slice_sizes=(1, src_blocks,...]
    dot_general x16 -> x3, matrix products: 97.6 us -> 43.4 us  [the longest x1 17.2 us: one_block(): jnp.dot(target_table, low, preferred_element_type=jnp.float32)]
    reshape x30 -> x2, local copies, waits for them, and re-layouts: 78.3 us -> 26.8 us  [the longest x1 24.6 us: one_block(): mixed = jnp.dot(integrals, picked.reshape(pair_count, src_blocks * block_...]
    mul x14 -> x2, local copies, waits for them, and re-layouts: 38.6 us -> 49.8 us  [one_block(): weighted = mixed * signs_qs[:, :, None, :]]
where the time goes in v1:
time: 1100 us; the launch traced here: 1090 us
  waiting for transfers between devices  819 us (74%)
  local copies, waits for them, and re-layouts  192 us (17%)
  matrix products  43.4 us (4%)
  other arithmetic  14.5 us (1%)
  between operations  13.5 us (1%)
    reduce_scatter x1, waiting for transfers between devices, on_device(): summed = lax.psum_scatter(buffer, 'beta', scatter_dimension=2, tiled=True)  789 us
    gather x2, local copies, waits for them, and re-layouts, one_block(): lax.gather(coeff3, row_ids[:, :, None], dims, slice_sizes=(1, src_blocks,...  95 us
    mul x2, local copies, waits for them, and re-layouts, one_block(): weighted = mixed * signs_qs[:, :, None, :]  49.8 us
    all_gather x1, waiting for transfers between devices, on_device(): gathered = lax.all_gather(coefficients, 'alpha', axis=0, tiled=True)  30.8 us
    reshape x1, local copies, waits for them, and re-layouts, one_block(): mixed = jnp.dot(integrals, picked.reshape(pair_count, src_blocks * block_...  24.6 us
  transfers between devices with their start and end apart: 2, of which 2 were waited for; matrix products, arithmetic and copies ran while one was open for 1% of the time, Pallas kernels for 0%

profile of v1, /device:TPU:1, one launch (start us, length us, event | category | flops | bytes accessed | tf_op | source)
XLA Modules:
  0.0 1086.5 jit_solution(7168128574325689797)
XLA Ops:
  6.5 0.0 copy-start
  6.5 0.0 all-gather.2.cloned.1.call-start
  6.5 1.7 copy.12
  8.2 0.0 all-gather.2.cloned.1.call-update
  8.3 0.0 reduce-scatter.2.cloned.1.call-start
  8.3 0.7 fusion.19
  9.0 0.7 broadcast_compare_fusion
  9.6 0.2 reduce-window.9
  9.8 0.1 broadcast_in_dim.43
  9.9 0.1 convert_element_type.48
  10.0 0.8 copy.13
  10.8 0.1 eq.57
  10.9 1.0 convert_element_type.49
  12.0 0.3 convert_element_type.50
  12.2 1.0 copy.16
  13.3 3.4 copy.15
  16.7 0.7 bitcast_subtract_fusion
  17.4 30.8 %all-gather.2.cloned.1.call-done = bf16[2048,256]{0,1:T(8,128)(2,1)} async-done(((bf16[256,256]{0,1:T(8,128)(2,1)}), bf16[2048,256]{0,1:T(8,128)(2,1)}) %all-gather.2.cloned.1.call-update) | async-done | bytes 1048592 | tf_op jit(solution)/shard_map/all_gather | solution.py:23
  48.2 1.3 broadcast_multiply_fusion.1
  49.5 1.4 copy.14
  50.9 2.5 broadcast_in_dim.42
  53.5 0.0 copy-done
  53.5 0.0 copy-start.2
  53.5 0.0 copy-start.1
  53.5 235.6 %while.13 = (s32[]{:T(128)}, f32[4,64,4096]{2,1,0:T(8,128)}, s32[]{:T(128)}, s32[4]{0:T(128)S(1)}, s32[4]{0:T(128)S(1)}, /*index=5*/s32[]{:T(128)}, s32[324,2048...) while((s32[]{:T(128)}, f32[4,64,4096]{2,1,0:T(8,128)}, ...), condition=%wide.region_4.5_spmd.clone, body=%wide.region_2.4_spmd.clone.sunk | while | flops 4841911296 | bytes 299490720 | solution.py:81
  54.2 0.6 fusion.35
  57.4 0.9 dynamic-slice_convert_fusion.2
  58.3 1.0 constant_dynamic-slice_fusion.2
  59.4 0.1 reshape.106
  59.5 55.8 %gather_fusion = bf16[20736,4,64]{2,1,0:T(4,128)(2,1)} fusion(bf16[2048,4,64]{2,1,0:T(4,128)(2,1)S(1)} %get-tuple-element.344, s32[21504]{0:T(1024)S(1)} %pad_clamp_fusion.2), kind=kCustom, calls=%fused_computation.clone.clone.1 | custom fusion | bytes 21316608 | tf_op jit(solution)/shard_map/while/body/gather | solution.py:53
  115.2 39.2 %copy.19 = bf16[324,64,4,64]{0,3,1,2:T(8,128)(2,1)} copy(bf16[324,64,4,64]{3,2,1,0:T(4,128)(2,1)} %bitcast.37) | data formatting | bytes 21233664 | tf_op jit(solution)/shard_map/while/body/gather | solution.py:53
  154.5 6.6 broadcast_multiply_fusion.3
  161.1 10.3 convolution_bitcast_fusion.2
  171.3 24.6 %reshape.107 = f32[1296,4096]{1,0:T(8,128)} reshape(f32[324,16384]{1,0:T(8,128)} %convolution_bitcast_fusion.2) | data formatting | bytes 42467328 | tf_op jit(solution)/shard_map/while/body/reshape | solution.py:65
  196.0 14.6 %mul.86 = f32[324,4,64,64]{3,2,1,0:T(8,128)} broadcast(f32[324,4,64]{2,1,0:T(4,128)} %get-tuple-element.347), dimensions={0,1,3} | broadcast | bytes 21565440 | tf_op jit(solution)/shard_map/while/body/mul | solution.py:66
  210.5 35.2 %mul.87 = f32[1296,4096]{1,0:T(8,128)} reshape(f32[324,4,64,64]{3,2,1,0:T(8,128)} %mul.86) | data formatting | bytes 42467328 | tf_op jit(solution)/shard_map/while/body/mul | solution.py:66
  245.7 17.2 %fusion.36 = f32[4096,64]{0,1:T(8,128)} fusion(f32[1296,4096]{1,0:T(8,128)} %reshape.107, f32[1296,4096]{1,0:T(8,128)} %mul.87, s32[1296]{0:T(1024)S(1)} %get-tuple-element.348), kind=kOutput, calls=%fused_computation.7.clone.1 | convolution fusion | flops 700876800 | bytes 43521088 | tf_op jit(solution)/shard_map/while/body/dot_general | solution.py:70
  262.9 16.0 %fusion.37 = f32[64,4096]{1,0:T(8,128)S(1)} fusion(f32[4096,64]{0,1:T(8,128)} %fusion.36, f32[1296,4096]{1,0:T(8,128)} %reshape.107, f32[1296,4096]{1,0:T(8,128)} %mul.87, s32[1296]{0:T(1024)S(1)} %get-tuple-element.348), kind=kOutput, calls=%fused_computation.13.clone.1 | convolution fusion | flops 695830528 | bytes 44569664 | tf_op jit(solution)/shard_map/while/body/dot_general | solution.py:70
  278.9 2.2 reshape.108
  281.1 4.1 copy.20
  285.2 2.1 broadcast_in_dim.53
  287.3 1.1 constant_dynamic-update-slice_fusion.2
  289.1 0.0 reduce-scatter.2.cloned.1.call-update
  289.1 0.0 copy-done.2
  289.1 0.1 broadcast_in_dim.40
  289.2 0.1 eq.55
  289.3 788.5 %reduce-scatter.2.cloned.1.call-done = f32[4,64,256]{2,1,0:T(8,128)} async-done(((f32[4,64,4096]{2,1,0:T(8,128)}), f32[4,64,256]{2,1,0:T(8,128)}) %reduce-scatter.2.cloned.1.call-update) | async-done | bytes 262160 | tf_op jit(solution)/shard_map/reduce_scatter | solution.py:82
  1077.8 0.0 copy-done.1
  1077.8 1.8 fusion.18
  (1 shorter events, 0.0 us)
Async XLA Ops:
  6.5 46.9 %copy-start = (bf16[324,324]{1,0:T(8,128)(2,1)S(1)}, bf16[324,324]{1,0:T(8,128)(2,1)}, u32[]{:S(2)}) copy-start(bf16[324,324]{1,0:T(8,128)(2,1)} %param.12) | copy-start | bytes 629860
  6.5 41.7 %all-gather.2.cloned.1.call-start = ((), (), s32[]{:S(2)}) async-start(), calls=%async_computation.1 | async-start | bytes 1179648 | tf_op jit(solution)/shard_map/all_gather | solution.py:23
  8.3 1069.5 %reduce-scatter.2.cloned.1.call-start = ((), (), s32[]{:S(2)}) async-start(), calls=%async_computation.2 | async-start | bytes 4456448 | tf_op jit(solution)/shard_map/reduce_scatter | solution.py:82
  53.5 235.6 %copy-start.2 = (pred[4]{0:T(512)(128)(4,1)S(1)}, pred[4]{0:T(512)(128)(4,1)}, u32[]{:S(2)}) copy-start(pred[4]{0:T(512)(128)(4,1)} %get-tuple-element.223) | copy-start | bytes 16
  53.5 1024.3 %copy-start.1 = (bf16[256,256]{1,0:T(8,128)(2,1)S(1)}, bf16[256,256]{1,0:T(8,128)(2,1)}, u32[]{:S(2)}) copy-start(bf16[256,256]{1,0:T(8,128)(2,1)} %param.10) | copy-start | bytes 393220
Sparse Core Ops, SparseCore 0:
  8.9 39.2 all-gather.1
  289.2 788.5 reduce-scatter.1

commit v2 on v1

--- a/solution.py
+++ b/solution.py
@@ -1,12 +1,50 @@
 import jax
 import jax.numpy as jnp
 from jax import lax
+from jax.experimental import pallas as pl
+from jax.experimental.pallas import tpu as pltpu
 from jax.sharding import PartitionSpec as P
 
+TILE = 1024
 
-def split_bf16(values):
-    rounded = lax.reduce_precision(values, exponent_bits=8, mantissa_bits=7)
-    return rounded.astype(jnp.bfloat16), (values - rounded).astype(jnp.bfloat16)
+
+def mix_kernel(integ_ref, picked_ref, sign_ref, table_ref, out_ref):
+    step_s = pl.program_id(1)
+    mixed = jnp.dot(integ_ref[...], picked_ref[...], preferred_element_type=jnp.float32)
+    weighted = mixed * sign_ref[0].astype(jnp.float32)
+    high = weighted.astype(jnp.bfloat16)
+    low = (weighted - high.astype(jnp.float32)).astype(jnp.bfloat16)
+    table = table_ref[0]
+    part = jnp.dot(table, high, preferred_element_type=jnp.float32) + jnp.dot(
+        table, low, preferred_element_type=jnp.float32
+    )
+
+    @pl.when(step_s == 0)
+    def _():
+        out_ref[...] = part
+
+    @pl.when(step_s > 0)
+    def _():
+        out_ref[...] += part
+
+
+def mix_block(integrals, picked, sign_tiled, tables, src_blocks, block_len, total_blocks):
+    pair_count = integrals.shape[0]
+    cols = block_len * block_len
+    tiles = cols // TILE
+    return pl.pallas_call(
+        mix_kernel,
+        out_shape=jax.ShapeDtypeStruct((total_blocks, cols), jnp.float32),
+        grid=(tiles, src_blocks),
+        in_specs=[
+            pl.BlockSpec((pair_count, pair_count), lambda r, s: (0, 0)),
+            pl.BlockSpec((pair_count, TILE), lambda r, s: (0, s * tiles + r)),
+            pl.BlockSpec((1, pair_count, TILE), lambda r, s: (s, 0, 0)),
+            pl.BlockSpec((1, total_blocks, pair_count), lambda r, s: (s, 0, 0)),
+        ],
+        out_specs=pl.BlockSpec((total_blocks, TILE), lambda r, s: (0, r)),
+        compiler_params=pltpu.CompilerParams(dimension_semantics=("arbitrary", "arbitrary")),
+    )(integrals, picked, sign_tiled, tables)
 
 
 def on_device(
@@ -27,12 +65,12 @@
     window_rows = gathered.shape[0]
     coeff3 = gathered.reshape(window_rows, src_blocks, block_len)
 
-    beta_ids = beta_block.T.reshape(-1)
     target_iota = jnp.arange(total_blocks, dtype=jnp.int32)
-    target_table = (target_iota[:, None] == beta_ids[None, :]).astype(jnp.bfloat16)
-    signs_qs = (
-        beta_sign.reshape(src_blocks, pair_count, block_len).transpose(1, 0, 2).astype(jnp.float32)
-    )
+    tables = (target_iota[None, :, None] == beta_block[:, None, :]).astype(jnp.bfloat16)
+    signs = beta_sign.reshape(src_blocks, pair_count, 1, block_len).astype(jnp.bfloat16)
+    sign_tiled = jnp.broadcast_to(
+        signs, (src_blocks, pair_count, TILE // block_len, block_len)
+    ).reshape(src_blocks, pair_count, TILE)
 
     own_flags = lax.dynamic_slice_in_dim(live_flags, alpha_rank * per_device, per_device, 0)
     own_count = jnp.sum(own_flags)
@@ -58,17 +96,14 @@
             mode=lax.GatherScatterMode.PROMISE_IN_BOUNDS,
         )
         picked = picked * sign_vals[:, None, :, None]
-        mixed = jnp.dot(
+        summed = mix_block(
             integrals,
             picked.reshape(pair_count, src_blocks * block_len * block_len),
-            preferred_element_type=jnp.float32,
-        ).reshape(pair_count, src_blocks, block_len, block_len)
-        weighted = mixed * signs_qs[:, :, None, :]
-        high, low = split_bf16(
-            weighted.reshape(pair_count * src_blocks, block_len * block_len)
-        )
-        summed = jnp.dot(target_table, high, preferred_element_type=jnp.float32) + jnp.dot(
-            target_table, low, preferred_element_type=jnp.float32
+            sign_tiled,
+            tables,
+            src_blocks,
+            block_len,
+            total_blocks,
         )
         rows_out = (
             summed.reshape(total_blocks, block_len, block_len)

time: 1100 us -> 811 us (0.74)
  waiting for transfers between devices: 819 us -> 115 us
  local copies, waits for them, and re-layouts: 192 us -> 524 us
  Pallas kernels: 0 us -> 79.6 us
  matrix products: 43.4 us -> 0 us
  other arithmetic: 14.5 us -> 56.8 us
    reduce_scatter x1, waiting for transfers between devices: 789 us -> 81.5 us  [on_device(): summed = lax.psum_scatter(buffer, 'beta', scatter_dimension=2, tiled=True)]
    gather x2 -> x8, local copies, waits for them, and re-layouts: 95 us -> 380 us  [one_block(): lax.gather(coeff3, row_ids[:, :, None], dims, slice_sizes=(1, src_blocks,...]
    pallas_call x0 -> x4, Pallas kernels: none -> 79.6 us  [mix_block(): pl.pallas_call(mix_kernel, out_shape=jax.ShapeDtypeStruct((total_blocks,...]
    dot_general x3 -> x0, matrix products: 43.4 us -> none  [the longest x1 17.2 us: one_block(): jnp.dot(target_table, low, preferred_element_type=jnp.float32)]
    mul x1 -> x4, other arithmetic: 6.56 us -> 42.4 us  [one_block(): picked = picked * sign_vals[:, None, :, None]]
    transpose x1 -> x4, local copies, waits for them, and re-layouts: 4.11 us -> 16.5 us  [one_block(): rows_out = summed.reshape(total_blocks, block_len, block_len).transpose(1...]
    mul x2 -> x4, local copies, waits for them, and re-layouts: 49.8 us -> 60.3 us  [one_block(): picked = picked * sign_vals[:, None, :, None]]
    reshape x1 -> x4, local copies, waits for them, and re-layouts: 24.6 us -> 18.2 us  [on_device(): sign_tiled = jnp.broadcast_to(signs, (src_blocks, pair_count, TILE // blo...]
where the time goes in v2:
time: 811 us; the launch traced here: 802 us
  local copies, waits for them, and re-layouts  524 us (65%)
  waiting for transfers between devices  115 us (14%)
  Pallas kernels  79.6 us (10%)
  other arithmetic  56.8 us (7%)
  between operations  13.5 us (2%)
  loops' own time  13.2 us (2%)
    gather x8, local copies, waits for them, and re-layouts, one_block(): lax.gather(coeff3, row_ids[:, :, None], dims, slice_sizes=(1, src_blocks,...  380 us
    reduce_scatter x1, waiting for transfers between devices, on_device(): summed = lax.psum_scatter(buffer, 'beta', scatter_dimension=2, tiled=True)  81.5 us
    pallas_call x4, Pallas kernels, mix_block(): pl.pallas_call(mix_kernel, out_shape=jax.ShapeDtypeStruct((total_blocks,...  79.6 us
    mul x4, local copies, waits for them, and re-layouts, one_block(): picked = picked * sign_vals[:, None, :, None]  60.3 us
    mul x4, other arithmetic, one_block(): picked = picked * sign_vals[:, None, :, None]  42.4 us
    all_gather x1, waiting for transfers between devices, on_device(): gathered = lax.all_gather(coefficients, 'alpha', axis=0, tiled=True)  33.8 us
    reshape x4, local copies, waits for them, and re-layouts, on_device(): sign_tiled = jnp.broadcast_to(signs, (src_blocks, pair_count, TILE // blo...  18.2 us
    transpose x4, local copies, waits for them, and re-layouts, one_block(): rows_out = summed.reshape(total_blocks, block_len, block_len).transpose(1...  16.5 us
  transfers between devices with their start and end apart: 2, of which 2 were waited for; matrix products, arithmetic and copies ran while one was open for 1% of the time, Pallas kernels for 0%

profile of v2, /device:TPU:1, one launch (start us, length us, event | category | flops | bytes accessed | tf_op | source)
XLA Modules:
  0.0 802.1 jit_solution(5872656954410614258)
XLA Ops:
  6.5 1.7 copy.15
  9.9 3.4 copy.17
  14.4 33.8 %all-gather.2.cloned.1.call-done = bf16[2048,256]{0,1:T(8,128)(2,1)} async-done(((bf16[256,256]{0,1:T(8,128)(2,1)}), bf16[2048,256]{0,1:T(8,128)(2,1)}) %all-gather.2.cloned.1.call-update) | async-done | bytes 1048592 | tf_op jit(solution)/shard_map/all_gather | solution.py:61
  48.2 1.3 broadcast_multiply_fusion.1
  49.6 1.4 copy.16
  51.0 2.6 broadcast_in_dim.47
  53.5 657.8 %while.13 = (s32[]{:T(128)}, f32[4,64,4096]{2,1,0:T(8,128)}, s32[]{:T(128)}, s32[4]{0:T(128)S(1)}, s32[4]{0:T(128)S(1)}, /*index=5*/s32[]{:T(128)}, s32[324,2048...) while((s32[]{:T(128)}, f32[4,64,4096]{2,1,0:T(8,128)}, ...), condition=%wide.region_4.5_spmd.clone, body=%wide.region_2.4_spmd.clone.sunk | while | flops 5516573 | bytes 102372704 | solution.py:116
  55.4 1.0 constant_dynamic-slice_fusion.2
  56.6 55.7 %gather_fusion = bf16[20736,4,64]{2,1,0:T(4,128)(2,1)} fusion(bf16[2048,4,64]{2,1,0:T(4,128)(2,1)S(1)} %get-tuple-element.343, s32[21504]{0:T(1024)S(1)} %pad_clamp_fusion.2), kind=kCustom, calls=%fused_computation.clone.clone.1 | custom fusion | bytes 21316608 | tf_op jit(solution)/shard_map/while/body/gather | solution.py:91
  112.2 39.2 %copy.23 = bf16[324,64,4,64]{0,3,1,2:T(8,128)(2,1)} copy(bf16[324,64,4,64]{3,2,1,0:T(4,128)(2,1)} %bitcast.22) | data formatting | bytes 21233664 | tf_op jit(solution)/shard_map/while/body/gather | solution.py:91
  151.5 0.9 dynamic-slice_convert_fusion.2
  152.4 10.6 %broadcast_multiply_fusion.3 = bf16[324,64,4,64]{0,3,1,2:T(8,128)(2,1)} fusion(bf16[324,64,4,64]{0,3,1,2:T(8,128)(2,1)} %copy.23, bf16[324,64]{0,1:T(8,128)(2,1)S(1)} %dynamic-slice_convert_fusion.2), kind=kLoop, calls=%fused_computation.4.clone.1 | loop fusion | flops 5308416 | bytes 21275136 | tf_op jit(solution)/shard_map/while/body/mul | solution.py:98
  163.0 15.1 %copy.24.picked_ref = bf16[324,16384]{1,0:T(8,128)(2,1)} copy(bf16[324,16384]{0,1:T(8,128)(2,1)} %bitcast.23) | data formatting | bytes 21233664 | tf_op jit(solution)/shard_map/while/body/mul | solution.py:98
  178.0 2.3 broadcast_in_dim.64
  180.3 4.6 copy.25.sign_ref
  184.9 0.7 fusion.13.table_ref
  185.6 19.9 %body.3 = f32[64,4096]{1,0:T(8,128)} custom-call(bf16[324,324]{1,0:T(8,128)(2,1)} %get-tuple-element.345.integ_ref, bf16[324,16384]{1,0:T(8,128)(2,1)} %copy.24.picked_ref, bf16[4,324,1024]{2,1,0:T(8,128)(2,1)} %copy.25.sign_ref, bf16[4,64,324]{2,1,0:T(8,128)(2,1)} %fusion.13.table_ref), custom_call_target="tpu_custom_call" | custom-call | tf_op jit(solution)/shard_map/while/body/pallas_call | solution.py:35
  205.5 3.1 reshape.109
  208.6 4.1 copy.26
  212.7 2.1 broadcast_in_dim.65
  216.8 1.1 constant_dynamic-update-slice_fusion.2
  219.7 1.0 constant_dynamic-slice_fusion.2
  220.9 55.7 %gather_fusion = bf16[20736,4,64]{2,1,0:T(4,128)(2,1)} fusion(bf16[2048,4,64]{2,1,0:T(4,128)(2,1)S(1)} %get-tuple-element.343, s32[21504]{0:T(1024)S(1)} %pad_clamp_fusion.2), kind=kCustom, calls=%fused_computation.clone.clone.1 | custom fusion | bytes 21316608 | tf_op jit(solution)/shard_map/while/body/gather | solution.py:91
  276.6 39.2 %copy.23 = bf16[324,64,4,64]{0,3,1,2:T(8,128)(2,1)} copy(bf16[324,64,4,64]{3,2,1,0:T(4,128)(2,1)} %bitcast.22) | data formatting | bytes 21233664 | tf_op jit(solution)/shard_map/while/body/gather | solution.py:91
  315.8 0.9 dynamic-slice_convert_fusion.2
  316.7 10.6 %broadcast_multiply_fusion.3 = bf16[324,64,4,64]{0,3,1,2:T(8,128)(2,1)} fusion(bf16[324,64,4,64]{0,3,1,2:T(8,128)(2,1)} %copy.23, bf16[324,64]{0,1:T(8,128)(2,1)S(1)} %dynamic-slice_convert_fusion.2), kind=kLoop, calls=%fused_computation.4.clone.1 | loop fusion | flops 5308416 | bytes 21275136 | tf_op jit(solution)/shard_map/while/body/mul | solution.py:98
  327.3 15.1 %copy.24.picked_ref = bf16[324,16384]{1,0:T(8,128)(2,1)} copy(bf16[324,16384]{0,1:T(8,128)(2,1)} %bitcast.23) | data formatting | bytes 21233664 | tf_op jit(solution)/shard_map/while/body/mul | solution.py:98
  342.4 2.3 broadcast_in_dim.64
  344.6 4.6 copy.25.sign_ref
  349.9 19.9 %body.3 = f32[64,4096]{1,0:T(8,128)} custom-call(bf16[324,324]{1,0:T(8,128)(2,1)} %get-tuple-element.345.integ_ref, bf16[324,16384]{1,0:T(8,128)(2,1)} %copy.24.picked_ref, bf16[4,324,1024]{2,1,0:T(8,128)(2,1)} %copy.25.sign_ref, bf16[4,64,324]{2,1,0:T(8,128)(2,1)} %fusion.13.table_ref), custom_call_target="tpu_custom_call" | custom-call | tf_op jit(solution)/shard_map/while/body/pallas_call | solution.py:35
  369.8 3.1 reshape.109
  372.9 4.1 copy.26
  377.0 2.1 broadcast_in_dim.65
  381.0 1.1 constant_dynamic-update-slice_fusion.2
  384.0 1.0 constant_dynamic-slice_fusion.2
  385.1 55.7 %gather_fusion = bf16[20736,4,64]{2,1,0:T(4,128)(2,1)} fusion(bf16[2048,4,64]{2,1,0:T(4,128)(2,1)S(1)} %get-tuple-element.343, s32[21504]{0:T(1024)S(1)} %pad_clamp_fusion.2), kind=kCustom, calls=%fused_computation.clone.clone.1 | custom fusion | bytes 21316608 | tf_op jit(solution)/shard_map/while/body/gather | solution.py:91
  440.8 39.2 %copy.23 = bf16[324,64,4,64]{0,3,1,2:T(8,128)(2,1)} copy(bf16[324,64,4,64]{3,2,1,0:T(4,128)(2,1)} %bitcast.22) | data formatting | bytes 21233664 | tf_op jit(solution)/shard_map/while/body/gather | solution.py:91
  480.1 0.9 dynamic-slice_convert_fusion.2
  481.0 10.6 %broadcast_multiply_fusion.3 = bf16[324,64,4,64]{0,3,1,2:T(8,128)(2,1)} fusion(bf16[324,64,4,64]{0,3,1,2:T(8,128)(2,1)} %copy.23, bf16[324,64]{0,1:T(8,128)(2,1)S(1)} %dynamic-slice_convert_fusion.2), kind=kLoop, calls=%fused_computation.4.clone.1 | loop fusion | flops 5308416 | bytes 21275136 | tf_op jit(solution)/shard_map/while/body/mul | solution.py:98
  491.6 15.1 %copy.24.picked_ref = bf16[324,16384]{1,0:T(8,128)(2,1)} copy(bf16[324,16384]{0,1:T(8,128)(2,1)} %bitcast.23) | data formatting | bytes 21233664 | tf_op jit(solution)/shard_map/while/body/mul | solution.py:98
  506.6 2.3 broadcast_in_dim.64
  508.9 4.6 copy.25.sign_ref
  513.5 0.7 fusion.13.table_ref
  514.2 19.9 %body.3 = f32[64,4096]{1,0:T(8,128)} custom-call(bf16[324,324]{1,0:T(8,128)(2,1)} %get-tuple-element.345.integ_ref, bf16[324,16384]{1,0:T(8,128)(2,1)} %copy.24.picked_ref, bf16[4,324,1024]{2,1,0:T(8,128)(2,1)} %copy.25.sign_ref, bf16[4,64,324]{2,1,0:T(8,128)(2,1)} %fusion.13.table_ref), custom_call_target="tpu_custom_call" | custom-call | tf_op jit(solution)/shard_map/while/body/pallas_call | solution.py:35
  534.1 3.1 reshape.109
  537.2 4.1 copy.26
  541.3 2.1 broadcast_in_dim.65
  545.3 1.1 constant_dynamic-update-slice_fusion.2
  548.3 1.0 constant_dynamic-slice_fusion.2
  549.4 55.7 %gather_fusion = bf16[20736,4,64]{2,1,0:T(4,128)(2,1)} fusion(bf16[2048,4,64]{2,1,0:T(4,128)(2,1)S(1)} %get-tuple-element.343, s32[21504]{0:T(1024)S(1)} %pad_clamp_fusion.2), kind=kCustom, calls=%fused_computation.clone.clone.1 | custom fusion | bytes 21316608 | tf_op jit(solution)/shard_map/while/body/gather | solution.py:91
  605.1 39.2 %copy.23 = bf16[324,64,4,64]{0,3,1,2:T(8,128)(2,1)} copy(bf16[324,64,4,64]{3,2,1,0:T(4,128)(2,1)} %bitcast.22) | data formatting | bytes 21233664 | tf_op jit(solution)/shard_map/while/body/gather | solution.py:91
  644.3 0.9 dynamic-slice_convert_fusion.2
  645.2 10.6 %broadcast_multiply_fusion.3 = bf16[324,64,4,64]{0,3,1,2:T(8,128)(2,1)} fusion(bf16[324,64,4,64]{0,3,1,2:T(8,128)(2,1)} %copy.23, bf16[324,64]{0,1:T(8,128)(2,1)S(1)} %dynamic-slice_convert_fusion.2), kind=kLoop, calls=%fused_computation.4.clone.1 | loop fusion | flops 5308416 | bytes 21275136 | tf_op jit(solution)/shard_map/while/body/mul | solution.py:98
  655.8 15.1 %copy.24.picked_ref = bf16[324,16384]{1,0:T(8,128)(2,1)} copy(bf16[324,16384]{0,1:T(8,128)(2,1)} %bitcast.23) | data formatting | bytes 21233664 | tf_op jit(solution)/shard_map/while/body/mul | solution.py:98
  670.9 2.3 broadcast_in_dim.64
  673.2 4.6 copy.25.sign_ref
  677.8 0.7 fusion.13.table_ref
  678.5 19.9 %body.3 = f32[64,4096]{1,0:T(8,128)} custom-call(bf16[324,324]{1,0:T(8,128)(2,1)} %get-tuple-element.345.integ_ref, bf16[324,16384]{1,0:T(8,128)(2,1)} %copy.24.picked_ref, bf16[4,324,1024]{2,1,0:T(8,128)(2,1)} %copy.25.sign_ref, bf16[4,64,324]{2,1,0:T(8,128)(2,1)} %fusion.13.table_ref), custom_call_target="tpu_custom_call" | custom-call | tf_op jit(solution)/shard_map/while/body/pallas_call | solution.py:35
  698.4 3.1 reshape.109
  701.5 4.1 copy.26
  705.6 2.1 broadcast_in_dim.65
  709.6 1.1 constant_dynamic-update-slice_fusion.2
  712.1 81.5 %reduce-scatter.2.cloned.1.call-done = f32[4,64,256]{2,1,0:T(8,128)} async-done(((f32[4,64,4096]{2,1,0:T(8,128)}), f32[4,64,256]{2,1,0:T(8,128)}) %reduce-scatter.2.cloned.1.call-update) | async-done | bytes 262160 | tf_op jit(solution)/shard_map/reduce_scatter | solution.py:117
  793.5 1.8 fusion.8
  (38 shorter events, 7.2 us)
Async XLA Ops:
  6.5 6.8 copy-start.1
  6.5 41.7 %all-gather.2.cloned.1.call-start = ((), (), s32[]{:S(2)}) async-start(), calls=%async_computation.1 | async-start | bytes 1179648 | tf_op jit(solution)/shard_map/all_gather | solution.py:61
  8.3 785.3 %reduce-scatter.2.cloned.1.call-start = ((), (), s32[]{:S(2)}) async-start(), calls=%async_computation.2 | async-start | bytes 4456448 | tf_op jit(solution)/shard_map/reduce_scatter | solution.py:117
  49.5 4.0 copy-start.3
  711.3 0.6 copy-start.4
  711.3 82.2 %copy-start = (bf16[256,256]{1,0:T(8,128)(2,1)S(1)}, bf16[256,256]{1,0:T(8,128)(2,1)}, u32[]{:S(2)}) copy-start(bf16[256,256]{1,0:T(8,128)(2,1)} %param.10) | copy-start | bytes 393220
  711.3 82.2 %copy-start.2 = (f32[256,256]{1,0:T(8,128)S(1)}, f32[256,256]{1,0:T(8,128)}, u32[]{:S(2)}) copy-start(f32[256,256]{1,0:T(8,128)} %param.11) | copy-start | bytes 786436
Sparse Core Ops, SparseCore 0:
  8.9 39.2 all-gather.1
  711.5 82.0 reduce-scatter.1

commit v3 on v1

v3 whole, which is shorter than its diff:
```python
import jax
import jax.numpy as jnp
from jax import lax
from jax.experimental import pallas as pl
from jax.experimental.pallas import tpu as pltpu
from jax.sharding import PartitionSpec as P

ROWS = 8


def mix_kernel(integ_ref, picked_ref, sign_ref, table_ref, out_ref):
    width = sign_ref.shape[1]
    targets = out_ref.shape[1]
    block_len = out_ref.shape[2]
    src_blocks = width // block_len
    lane = lax.broadcasted_iota(jnp.int32, (targets, 2 * block_len), 1)
    upper = lane >= block_len
    integ = integ_ref[...]
    table = table_ref[...]
    sign = sign_ref[...].astype(jnp.float32)
    for row in range(picked_ref.shape[0]):
        mixed = jnp.dot(integ, picked_ref[row], preferred_element_type=jnp.float32)
        weighted = mixed * sign
        high = weighted.astype(jnp.bfloat16)
        low = (weighted - high.astype(jnp.float32)).astype(jnp.bfloat16)
        res = jnp.dot(table, high, preferred_element_type=jnp.float32) + jnp.dot(
            table, low, preferred_element_type=jnp.float32
        )
        folded = jnp.zeros((targets, 2 * block_len), jnp.float32)
        for s in range(src_blocks):
            lanes = (s // 2) * 2 * block_len
            piece = res[s * targets : (s + 1) * targets, lanes : lanes + 2 * block_len]
            keep = upper if s % 2 else jnp.logical_not(upper)
            folded = folded + jnp.where(keep, piece, 0.0)
        folded = folded + pltpu.roll(folded, block_len, 1)
        out_ref[row] = folded[:, :block_len]


def mix_block(integ_pad, picked, sign_q, table_all, targets, block_len):
    rows, pairs, width = picked.shape
    return pl.pallas_call(
        mix_kernel,
        out_shape=jax.ShapeDtypeStruct((rows, targets, block_len), jnp.float32),
        grid=(rows // ROWS,),
        in_specs=[
            pl.BlockSpec((pairs, pairs), lambda i: (0, 0)),
            pl.BlockSpec((ROWS, pairs, width), lambda i: (i, 0, 0)),
            pl.BlockSpec((pairs, width), lambda i: (0, 0)),
            pl.BlockSpec(table_all.shape, lambda i: (0, 0)),
        ],
        out_specs=pl.BlockSpec((ROWS, targets, block_len), lambda i: (i, 0, 0)),
        compiler_params=pltpu.CompilerParams(dimension_semantics=("arbitrary",)),
    )(integ_pad, picked, sign_q, table_all)


def on_device(
    coefficients, diagonal, integrals, alpha_row, alpha_sign, beta_block, beta_sign, block_irrep
):
    alpha_rank = lax.axis_index("alpha")
    pair_count = integrals.shape[0]
    local_rows, local_cols = coefficients.shape
    block_len = beta_sign.shape[1] // pair_count
    per_device = local_rows // block_len
    src_blocks = local_cols // block_len
    total_blocks = lax.axis_size("beta") * src_blocks
    pairs = -(-pair_count // 16) * 16
    extra = pairs - pair_count

    gathered = lax.all_gather(coefficients, "alpha", axis=0, tiled=True)
    live_flags = (block_irrep == 0).astype(jnp.int32)
    live_rows = jnp.repeat(live_flags, block_len)
    gathered = gathered * live_rows[:, None].astype(jnp.bfloat16)
    window_rows = gathered.shape[0]
    coeff_ext = jnp.concatenate(
        [gathered, -gathered, jnp.zeros((16, local_cols), jnp.bfloat16)], axis=0
    )
    zero_row = 2 * window_rows
    row_ext = jnp.where(
        alpha_sign == 0, zero_row, jnp.where(alpha_sign < 0, alpha_row + window_rows, alpha_row)
    )
    row_ext = jnp.pad(row_ext, ((0, extra), (0, 0)), constant_values=zero_row).T

    integ_pad = jnp.pad(integrals, ((0, extra), (0, extra)))
    sign_q = (
        beta_sign.reshape(src_blocks, pair_count, block_len)
        .transpose(1, 0, 2)
        .reshape(pair_count, local_cols)
    )
    sign_q = jnp.pad(sign_q, ((0, extra), (0, 0))).astype(jnp.bfloat16)
    target_iota = jnp.arange(total_blocks, dtype=jnp.int32)
    table_all = (target_iota[None, :, None] == beta_block[:, None, :]).astype(jnp.bfloat16)
    table_all = jnp.pad(
        table_all.reshape(src_blocks * total_blocks, pair_count), ((0, 0), (0, extra))
    )

    own_flags = lax.dynamic_slice_in_dim(live_flags, alpha_rank * per_device, per_device, 0)
    own_count = jnp.sum(own_flags)
    own_pos = jnp.cumsum(own_flags) - own_flags
    local_iota = jnp.arange(per_device, dtype=jnp.int32)

    dims = lax.GatherDimensionNumbers(
        offset_dims=(2,), collapsed_slice_dims=(0,), start_index_map=(0,)
    )

    def one_block(slot_idx, buffer):
        local_blk = jnp.sum(jnp.where((own_flags == 1) & (own_pos == slot_idx), local_iota, 0))
        first_row = (alpha_rank * per_device + local_blk) * block_len
        row_ids = lax.dynamic_slice_in_dim(row_ext, first_row, block_len, 0)
        picked = lax.gather(
            coeff_ext,
            row_ids[:, :, None],
            dims,
            slice_sizes=(1, local_cols),
            mode=lax.GatherScatterMode.PROMISE_IN_BOUNDS,
        )
        summed = mix_block(integ_pad, picked, sign_q, table_all, total_blocks, block_len)
        rows_out = summed.reshape(block_len, total_blocks * block_len)
        return lax.dynamic_update_index_in_dim(buffer, rows_out, local_blk, 0)

    empty = jnp.zeros((per_device, block_len, total_blocks * block_len), jnp.float32)
    buffer = lax.fori_loop(0, own_count, one_block, empty)
    summed = lax.psum_scatter(buffer, "beta", scatter_dimension=2, tiled=True)
    placed = summed.reshape(local_rows, local_cols)
    own_live_rows = jnp.repeat(own_flags, block_len)
    total = diagonal * coefficients.astype(jnp.float32) + placed
    return jnp.where(own_live_rows[:, None] == 1, total, jnp.zeros_like(total))


def solution(mesh):
    return jax.shard_map(
        on_device,
        mesh=mesh,
        in_specs=(
            P("alpha", "beta"),
            P("alpha", "beta"),
            P(),
            P(),
            P(),
            P("beta", None),
            P("beta", None),
            P(),
        ),
        out_specs=P("alpha", "beta"),
        check_vma=False,
    )
```

time: 1100 us -> 621 us (0.56); the launches traced: 1090 us -> 620 us
  waiting for transfers between devices: 819 us -> 458 us
  local copies, waits for them, and re-layouts: 192 us -> 102 us
  matrix products: 43.4 us -> 0 us
  Pallas kernels: 0 us -> 25 us
    reduce_scatter x1, waiting for transfers between devices: 789 us -> 433 us  [on_device(): summed = lax.psum_scatter(buffer, 'beta', scatter_dimension=2, tiled=True)]
    mul x2 -> x0, local copies, waits for them, and re-layouts: 49.8 us -> none  [one_block(): weighted = mixed * signs_qs[:, :, None, :]]
    dot_general x3 -> x0, matrix products: 43.4 us -> none  [the longest x1 17.2 us: one_block(): jnp.dot(target_table, low, preferred_element_type=jnp.float32)]
    reshape x2 -> x1, local copies, waits for them, and re-layouts: 26.8 us -> 0.21 us  [on_device(): beta_sign.reshape(src_blocks, pair_count, block_len).transpose(1, 0, 2)]
    pallas_call x0 -> x1, Pallas kernels: none -> 25 us  [mix_block(): pl.pallas_call(mix_kernel, out_shape=jax.ShapeDtypeStruct((rows, targets,...]
    gather x2 -> x1, local copies, waits for them, and re-layouts: 95 us -> 84.8 us  [one_block(): lax.gather(coeff_ext, row_ids[:, :, None], dims, slice_sizes=(1, local_co...]
  transfers between devices with their start and end apart: 2 -> 2, of which waited for: 2 -> 2; matrix products, arithmetic and copies ran while one was open for 1% -> 3% of each run, Pallas kernels for 0% -> 0%
where the time goes in v3:
time: 621 us; the launch traced here: 620 us
  waiting for transfers between devices  458 us (74%)
  local copies, waits for them, and re-layouts  102 us (16%)
  Pallas kernels  25 us (4%)
  other arithmetic  16.4 us (3%)
  between operations  13.5 us (2%)
    reduce_scatter x1, waiting for transfers between devices, on_device(): summed = lax.psum_scatter(buffer, 'beta', scatter_dimension=2, tiled=True)  433 us
    gather x1, local copies, waits for them, and re-layouts, one_block(): lax.gather(coeff_ext, row_ids[:, :, None], dims, slice_sizes=(1, local_co...  84.8 us
    pallas_call x1, Pallas kernels, mix_block(): pl.pallas_call(mix_kernel, out_shape=jax.ShapeDtypeStruct((rows, targets,...  25 us
    all_gather x1, waiting for transfers between devices, on_device(): gathered = lax.all_gather(coefficients, 'alpha', axis=0, tiled=True)  24.1 us
  transfers between devices with their start and end apart: 2, of which 2 were waited for; matrix products, arithmetic and copies ran while one was open for 3% of the time, Pallas kernels for 0%

profile of v3, /device:TPU:1, one launch (start us, length us, event | category | flops | bytes accessed | tf_op | source)
XLA Modules:
  0.0 619.6 jit_solution(10215973802559829097)
XLA Ops:
  6.5 0.0 all-gather.2.cloned.1.call-start
  6.5 0.7 all-gather.2.cloned.1.call-update
  7.3 0.0 reduce-scatter.2.cloned.1.call-start
  7.3 0.7 fusion.5
  8.0 0.6 broadcast_compare_fusion
  8.6 0.2 reduce-window.9
  8.8 0.1 eq.66
  8.9 0.1 broadcast_in_dim.50
  8.9 0.1 convert_element_type.28
  9.0 1.0 convert.9
  10.1 0.2 reshape.62
  10.3 0.2 copy.18
  10.5 0.1 copy.20
  10.6 0.7 pad.22.clone
  11.3 1.0 pad.21
  12.3 2.3 copy.16
  14.6 0.0 copy-start.2
  14.6 3.5 copy.14
  18.1 0.0 copy-done.2
  18.1 0.1 bitcast_compare_fusion
  18.2 0.7 pad_convert_fusion
  18.9 0.7 bitcast_subtract_fusion
  19.5 2.5 fusion.3
  22.0 1.9 pad_bitcast_fusion
  23.9 24.1 %all-gather.2.cloned.1.call-done = bf16[2048,256]{1,0:T(8,128)(2,1)} async-done(((bf16[256,256]{1,0:T(8,128)(2,1)}), bf16[2048,256]{1,0:T(8,128)(2,1)}) %all-gather.2.cloned.1.call-update) | async-done | bytes 1048592 | tf_op jit(solution)/shard_map/all_gather | solution.py:69
  48.0 1.6 fusion.6
  49.5 5.9 maximum_maximum_fusion
  55.4 2.5 broadcast_in_dim.48
  58.0 118.8 %while.13 = (s32[]{:T(128)}, f32[4,64,4096]{2,1,0:T(8,128)}, s32[]{:T(128)}, s32[4]{0:T(128)S(1)}, s32[4]{0:T(128)S(1)}, /*index=5*/s32[]{:T(128)}, s32[2048,336...) while((s32[]{:T(128)}, f32[4,64,4096]{2,1,0:T(8,128)}, ...), condition=%wide.region_4.5_spmd.clone, body=%wide.region_2.4_spmd.clone.sunk | while | flops 21533 | bytes 26816808 | solution.py:121
  58.6 0.7 fusion.8
  62.1 0.9 constant_dynamic-slice_fusion.2
  63.0 0.1 reshape.84
  63.2 84.8 %gather_fusion = bf16[21504,256]{1,0:T(8,128)(2,1)} fusion(bf16[4112,256]{1,0:T(8,128)(2,1)S(1)} %get-tuple-element.317, s32[21504]{0:T(1024)S(1)} %broadcast_clamp_fusion.2), kind=kCustom, calls=%fused_computation.clone.clone.1 | custom fusion | bytes 22106112 | tf_op jit(solution)/shard_map/while/body/gather | solution.py:109
  148.0 25.0 %body.3 = f32[64,64,64]{2,1,0:T(8,128)} custom-call(bf16[336,336]{1,0:T(8,128)(2,1)S(1)} %get-tuple-element.318.integ_ref, bf16[64,336,256]{2,1,0:T(8,128)(2,1)} %bitcast.16, bf16[336,256]{1,0:T(8,128)(2,1)} %get-tuple-element.319.sign_ref, bf16[256,336]{1,0:T(8,128)(2,1)} %get-tuple-element.320.table_ref), custom_call_target="tpu_custom_call" | custom-call | tf_op jit(solution)/shard_map/while/body/pallas_call | solution.py:41
  172.9 2.1 broadcast_in_dim.62
  175.1 1.1 constant_dynamic-update-slice_fusion.2
  176.8 0.0 copy-start.3
  176.8 0.0 copy-start
  176.8 0.0 copy-start.1
  176.8 0.0 reduce-scatter.2.cloned.1.call-update
  176.8 0.6 copy-done.3
  177.4 0.1 broadcast_in_dim.46
  177.5 0.1 eq.63
  177.6 433.4 %reduce-scatter.2.cloned.1.call-done = f32[4,64,256]{2,1,0:T(8,128)} async-done(((f32[4,64,4096]{2,1,0:T(8,128)}), f32[4,64,256]{2,1,0:T(8,128)}) %reduce-scatter.2.cloned.1.call-update) | async-done | bytes 262160 | tf_op jit(solution)/shard_map/reduce_scatter | solution.py:122
  611.0 0.0 copy-done
  611.0 0.0 copy-done.1
  611.0 1.8 fusion.4
  (4 shorter events, 0.0 us)
Async XLA Ops:
  6.5 41.4 %all-gather.2.cloned.1.call-start = ((), (), s32[]{:S(2)}) async-start(), calls=%async_computation.1 | async-start | bytes 1179648 | tf_op jit(solution)/shard_map/all_gather | solution.py:69
  7.3 603.7 %reduce-scatter.2.cloned.1.call-start = ((), (), s32[]{:S(2)}) async-start(), calls=%async_computation.2 | async-start | bytes 4456448 | tf_op jit(solution)/shard_map/reduce_scatter | solution.py:122
  14.6 3.5 copy-start.2
  176.8 0.7 copy-start.3
  176.8 434.2 %copy-start = (bf16[256,256]{1,0:T(8,128)(2,1)S(1)}, bf16[256,256]{1,0:T(8,128)(2,1)}, u32[]{:S(2)}) copy-start(bf16[256,256]{1,0:T(8,128)(2,1)} %param.10) | copy-start | bytes 393220
  176.8 434.2 %copy-start.1 = (f32[256,256]{1,0:T(8,128)S(1)}, f32[256,256]{1,0:T(8,128)}, u32[]{:S(2)}) copy-start(f32[256,256]{1,0:T(8,128)} %param.11) | copy-start | bytes 786436
Sparse Core Ops, SparseCore 0:
  9.0 38.9 all-gather.1
  177.0 433.9 reduce-scatter.1

commit v4 on v3

v4 whole, which is shorter than its diff:
```python
import jax
import jax.numpy as jnp
from jax import lax
from jax.experimental import pallas as pl
from jax.experimental.pallas import tpu as pltpu
from jax.sharding import Mesh
from jax.sharding import PartitionSpec as P

ROWS = 8
PAIR = 2


def mix_kernel(integ_ref, picked_ref, sign_ref, table_ref, out_ref):
    halves, _, width = sign_ref.shape
    targets = out_ref.shape[1]
    block_len = out_ref.shape[2]
    src_blocks = width // block_len
    lane = lax.broadcasted_iota(jnp.int32, (targets, 2 * block_len), 1)
    upper = lane >= block_len
    integ = integ_ref[...]
    for row in range(picked_ref.shape[0]):
        mixed = jnp.dot(integ, picked_ref[row], preferred_element_type=jnp.float32)
        folded = jnp.zeros((targets, 2 * block_len), jnp.float32)
        for half in range(halves):
            weighted = mixed[:, half * width : (half + 1) * width] * sign_ref[half].astype(
                jnp.float32
            )
            high = weighted.astype(jnp.bfloat16)
            low = (weighted - high.astype(jnp.float32)).astype(jnp.bfloat16)
            table = table_ref[half]
            res = jnp.dot(table, high, preferred_element_type=jnp.float32) + jnp.dot(
                table, low, preferred_element_type=jnp.float32
            )
            for s in range(src_blocks):
                lanes = (s // 2) * 2 * block_len
                piece = res[s * targets : (s + 1) * targets, lanes : lanes + 2 * block_len]
                keep = upper if s % 2 else jnp.logical_not(upper)
                folded = folded + jnp.where(keep, piece, 0.0)
        folded = folded + pltpu.roll(folded, block_len, 1)
        out_ref[row] = folded[:, :block_len]


def mix_block(integ_pad, picked, sign_q, table_all, targets, block_len):
    rows, pairs, width = picked.shape
    return pl.pallas_call(
        mix_kernel,
        out_shape=jax.ShapeDtypeStruct((rows, targets, block_len), jnp.float32),
        grid=(rows // ROWS,),
        in_specs=[
            pl.BlockSpec((pairs, pairs), lambda i: (0, 0)),
            pl.BlockSpec((ROWS, pairs, width), lambda i: (i, 0, 0)),
            pl.BlockSpec(sign_q.shape, lambda i: (0, 0, 0)),
            pl.BlockSpec(table_all.shape, lambda i: (0, 0, 0)),
        ],
        out_specs=pl.BlockSpec((ROWS, targets, block_len), lambda i: (i, 0, 0)),
        compiler_params=pltpu.CompilerParams(dimension_semantics=("arbitrary",)),
    )(integ_pad, picked, sign_q, table_all)


def on_device(
    coefficients, diagonal, integrals, alpha_row, alpha_sign, beta_block, beta_sign, block_irrep
):
    alpha_rank = lax.axis_index("alpha")
    member = lax.axis_index("m")
    pair_count = integrals.shape[0]
    local_rows, local_cols = coefficients.shape
    block_len = beta_sign.shape[1] // pair_count
    per_device = local_rows // block_len
    src_blocks = local_cols // block_len
    total_blocks = lax.axis_size("g") * PAIR * src_blocks
    pairs = -(-pair_count // 16) * 16
    extra = pairs - pair_count
    sub_rows = block_len // PAIR

    gathered = lax.all_gather(coefficients, "alpha", axis=0, tiled=True)
    live_flags = (block_irrep == 0).astype(jnp.int32)
    live_rows = jnp.repeat(live_flags, block_len)
    gathered = gathered * live_rows[:, None].astype(jnp.bfloat16)
    gathered = lax.all_gather(gathered, "m", axis=1, tiled=True)
    window_rows, wide_cols = gathered.shape
    coeff_ext = jnp.concatenate(
        [gathered, -gathered, jnp.zeros((16, wide_cols), jnp.bfloat16)], axis=0
    )
    zero_row = 2 * window_rows
    row_ext = jnp.where(
        alpha_sign == 0, zero_row, jnp.where(alpha_sign < 0, alpha_row + window_rows, alpha_row)
    )
    row_ext = jnp.pad(row_ext, ((0, extra), (0, 0)), constant_values=zero_row).T

    integ_pad = jnp.pad(integrals, ((0, extra), (0, extra)))
    beta_block2 = lax.all_gather(beta_block, "m", axis=0, tiled=True)
    beta_sign2 = lax.all_gather(beta_sign, "m", axis=0, tiled=True)
    sign_q = (
        beta_sign2.reshape(PAIR, src_blocks, pair_count, block_len)
        .transpose(0, 2, 1, 3)
        .reshape(PAIR, pair_count, local_cols)
    )
    sign_q = jnp.pad(sign_q, ((0, 0), (0, extra), (0, 0))).astype(jnp.bfloat16)
    target_iota = jnp.arange(total_blocks, dtype=jnp.int32)
    table_all = (target_iota[None, :, None] == beta_block2[:, None, :]).astype(jnp.bfloat16)
    table_all = jnp.pad(
        table_all.reshape(PAIR, src_blocks * total_blocks, pair_count),
        ((0, 0), (0, 0), (0, extra)),
    )

    own_flags = lax.dynamic_slice_in_dim(live_flags, alpha_rank * per_device, per_device, 0)
    own_count = jnp.sum(own_flags)
    own_pos = jnp.cumsum(own_flags) - own_flags
    local_iota = jnp.arange(per_device, dtype=jnp.int32)

    dims = lax.GatherDimensionNumbers(
        offset_dims=(2,), collapsed_slice_dims=(0,), start_index_map=(0,)
    )

    def one_block(slot_idx, buffer):
        local_blk = jnp.sum(jnp.where((own_flags == 1) & (own_pos == slot_idx), local_iota, 0))
        first_row = (alpha_rank * per_device + local_blk) * block_len + member * sub_rows
        row_ids = lax.dynamic_slice_in_dim(row_ext, first_row, sub_rows, 0)
        picked = lax.gather(
            coeff_ext,
            row_ids[:, :, None],
            dims,
            slice_sizes=(1, wide_cols),
            mode=lax.GatherScatterMode.PROMISE_IN_BOUNDS,
        )
        summed = mix_block(integ_pad, picked, sign_q, table_all, total_blocks, block_len)
        rows_out = summed.reshape(sub_rows, total_blocks * block_len)
        return lax.dynamic_update_index_in_dim(buffer, rows_out, local_blk, 0)

    empty = jnp.zeros((per_device, sub_rows, total_blocks * block_len), jnp.float32)
    buffer = lax.fori_loop(0, own_count, one_block, empty)
    summed = lax.psum_scatter(buffer, "g", scatter_dimension=2, tiled=True)
    summed = lax.all_to_all(summed, "m", 2, 1, tiled=True)
    placed = summed.reshape(local_rows, local_cols)
    own_live_rows = jnp.repeat(own_flags, block_len)
    total = diagonal * coefficients.astype(jnp.float32) + placed
    return jnp.where(own_live_rows[:, None] == 1, total, jnp.zeros_like(total))


def solution(mesh):
    alpha_size, beta_size = mesh.devices.shape
    split_mesh = Mesh(
        mesh.devices.reshape(alpha_size, beta_size // PAIR, PAIR), ("alpha", "g", "m")
    )
    beta = ("g", "m")
    return jax.shard_map(
        on_device,
        mesh=split_mesh,
        in_specs=(
            P("alpha", beta),
            P("alpha", beta),
            P(),
            P(),
            P(),
            P(beta, None),
            P(beta, None),
            P(),
        ),
        out_specs=P("alpha", beta),
        check_vma=False,
    )
```

time: 621 us -> 553 us (0.89)
  waiting for transfers between devices: 458 us -> 349 us
  Pallas kernels: 25 us -> 44.3 us
  blocking collectives: 0 us -> 13.5 us
    reduce_scatter x1 -> x0, waiting for transfers between devices: 433 us -> none  [on_device(): summed = lax.psum_scatter(buffer, 'beta', scatter_dimension=2, tiled=True)]
    unnamed x2 -> x4, waiting for transfers between devices: 0.73 us -> 310 us
    pallas_call x1 -> x2, Pallas kernels: 25 us -> 44.3 us  [mix_block(): pl.pallas_call(mix_kernel, out_shape=jax.ShapeDtypeStruct((rows, targets,...]
    gather x1 -> x2, local copies, waits for them, and re-layouts: 84.8 us -> 67.6 us  [one_block(): lax.gather(coeff_ext, row_ids[:, :, None], dims, slice_sizes=(1, wide_col...]
    all_gather x1, waiting for transfers between devices: 24.1 us -> 39.8 us  [on_device(): gathered = lax.all_gather(coefficients, 'alpha', axis=0, tiled=True)]
    all_gather x0 -> x2, blocking collectives: none -> 9.21 us  [the longest x1 7.35 us: on_device(): beta_sign2 = lax.all_gather(beta_sign, 'm', axis=0, tiled=True)]
    while x0 -> x1, local copies, waits for them, and re-layouts: none -> 7.25 us  [on_device(): buffer = lax.fori_loop(0, own_count, one_block, empty)]
  transfers between devices with their start and end apart: 2 -> 3, of which waited for: 2 -> 2; matrix products, arithmetic and copies ran while one was open for 3% -> 4% of each run, Pallas kernels for 0% -> 0%
where the time goes in v4:
time: 553 us; the launch traced here: 552 us
  waiting for transfers between devices  349 us (63%)
  local copies, waits for them, and re-layouts  103 us (19%)
  Pallas kernels  44.3 us (8%)
  other arithmetic  20.1 us (4%)
  between operations  13.9 us (3%)
  blocking collectives  13.5 us (2%)
  loops' own time  7.35 us (1%)
    unnamed x4, waiting for transfers between devices  310 us
    gather x2, local copies, waits for them, and re-layouts, one_block(): lax.gather(coeff_ext, row_ids[:, :, None], dims, slice_sizes=(1, wide_col...  67.6 us
    pallas_call x2, Pallas kernels, mix_block(): pl.pallas_call(mix_kernel, out_shape=jax.ShapeDtypeStruct((rows, targets,...  44.3 us
    all_gather x1, waiting for transfers between devices, on_device(): gathered = lax.all_gather(coefficients, 'alpha', axis=0, tiled=True)  39.8 us
  transfers between devices with their start and end apart: 3, of which 2 were waited for; matrix products, arithmetic and copies ran while one was open for 4% of the time, Pallas kernels for 0%

profile of v4, /device:TPU:1, one launch (start us, length us, event | category | flops | bytes accessed | tf_op | source)
XLA Modules:
  0.0 551.6 jit_solution(4383216553758981738)
XLA Ops:
  6.5 0.7 all-gather.5.cloned.1.call-update
  7.3 0.0 all-gather.7.cloned.1.call-start
  7.3 0.7 fusion.5
  8.0 0.1 broadcast_in_dim.50
  8.0 0.1 convert_element_type.28
  8.1 39.8 %all-gather.5.cloned.1.call-done = bf16[2048,256]{1,0:T(8,128)(2,1)} async-done(((bf16[256,256]{1,0:T(8,128)(2,1)}), bf16[2048,256]{1,0:T(8,128)(2,1)}) %all-gather.5.cloned.1.call-update) | async-done | bytes 1048592 | tf_op jit(solution)/shard_map/all_gather | solution.py:75
  48.0 2.6 broadcast_multiply_fusion
  50.5 0.0 all-gather.7.cloned.1.call-update
  50.6 0.0 all-reduce.7.cloned.1.call-start
  50.6 0.6 broadcast_compare_fusion
  51.2 0.8 reduce-window.9
  51.9 2.3 copy.30
  54.2 0.0 copy-start.5
  54.3 3.5 copy.32
  57.7 7.4 %all-gather = s32[2,4,20736]{2,1,0:T(4,128)S(1)} all-gather(s32[1,4,20736]{2,1,0:T(4,128)S(1)} %bitcast.31), channel_id=1, replica_groups=mesh['alpha'=8,'g'=8,'m'=2] {'m'}, dimensions={0}, use_global_device_ids=true | all-gather | bytes 995328 | tf_op jit(solution)/shard_map/all_gather | solution.py:92
  65.1 0.1 convert.10
  65.2 1.3 reshape.64
  66.5 1.4 copy.34
  67.9 0.9 copy.38
  68.9 1.9 all-gather.1
  70.7 0.1 eq.66
  70.8 1.9 pad.22.clone
  72.7 1.7 pad.21
  74.4 0.1 eq.68
  74.4 0.2 bitcast_compare_fusion
  74.6 0.1 pad_convert_fusion
  74.7 1.9 bitcast_subtract_fusion
  76.6 0.5 fusion.3
  77.1 1.8 pad_bitcast_fusion
  79.0 2.1 neg.3
  81.1 0.1 copy-done.3
  81.2 7.2 %maximum_maximum_fusion = bf16[4112,512]{1,0:T(8,128)(2,1)} fusion(bf16[2048,512]{1,0:T(8,128)(2,1)S(1)} %neg.3, bf16[2048,512]{1,0:T(8,128)(2,1)S(1)} %copy-done.3, bf16[4112]{0:T(1024)(128)(2,1)S(1)} %pad.27.clone), kind=kLoop, calls=%fused_computation.8 | loop fusion | flops 12632064 | bytes 8413216 | tf_op jit(solution)/shard_map/concatenate | solution.py:81
  88.4 1.6 broadcast_in_dim.48
  89.9 127.2 %while.13 = (s32[]{:T(128)}, f32[4,32,4096]{2,1,0:T(8,128)}, s32[]{:T(128)}, s32[4]{0:T(128)S(1)}, s32[4]{0:T(128)S(1)}, /*index=5*/s32[]{:T(128)}, s32[]{:T(128...) while((s32[]{:T(128)}, f32[4,32,4096]{2,1,0:T(8,128)}, ...), condition=%wide.region_4.5_spmd.clone, body=%wide.region_2.4_spmd.clone.sunk | while | flops 11294 | bytes 24420660 | solution.py:131
  90.8 0.6 fusion.8
  92.0 0.8 constant_dynamic-slice_fusion.3
  92.9 0.1 reshape.95
  93.0 33.8 %gather_fusion = bf16[10752,512]{1,0:T(8,128)(2,1)} fusion(bf16[4112,512]{1,0:T(8,128)(2,1)} %get-tuple-element.366, s32[11264]{0:T(1024)S(1)} %pad_clamp_fusion.2), kind=kCustom, calls=%fused_computation.clone.clone.1 | custom fusion | bytes 22063104 | tf_op jit(solution)/shard_map/while/body/gather | solution.py:119
  126.8 22.2 %body.3 = f32[32,64,64]{2,1,0:T(8,128)} custom-call(bf16[336,336]{1,0:T(8,128)(2,1)S(1)} %get-tuple-element.367.integ_ref, bf16[32,336,512]{2,1,0:T(8,128)(2,1)} %bitcast.26, bf16[2,336,256]{2,1,0:T(8,128)(2,1)S(1)} %get-tuple-element.368.sign_ref, bf16[2,256,336]{2,1,0:T(8,128)(2,1)S(1)} %get-tuple-element.369.table_ref), custom_call_target="tpu_custom_call" | custom-call | tf_op jit(solution)/shard_map/while/body/pallas_call | solution.py:45
  148.9 1.6 broadcast_in_dim.62
  152.4 0.8 constant_dynamic-update-slice_fusion.2
  153.9 0.6 fusion.8
  155.2 0.8 constant_dynamic-slice_fusion.3
  156.0 0.1 reshape.95
  156.1 33.8 %gather_fusion = bf16[10752,512]{1,0:T(8,128)(2,1)} fusion(bf16[4112,512]{1,0:T(8,128)(2,1)} %get-tuple-element.366, s32[11264]{0:T(1024)S(1)} %pad_clamp_fusion.2), kind=kCustom, calls=%fused_computation.clone.clone.1 | custom fusion | bytes 22063104 | tf_op jit(solution)/shard_map/while/body/gather | solution.py:119
  189.9 22.2 %body.3 = f32[32,64,64]{2,1,0:T(8,128)} custom-call(bf16[336,336]{1,0:T(8,128)(2,1)S(1)} %get-tuple-element.367.integ_ref, bf16[32,336,512]{2,1,0:T(8,128)(2,1)} %bitcast.26, bf16[2,336,256]{2,1,0:T(8,128)(2,1)S(1)} %get-tuple-element.368.sign_ref, bf16[2,256,336]{2,1,0:T(8,128)(2,1)S(1)} %get-tuple-element.369.table_ref), custom_call_target="tpu_custom_call" | custom-call | tf_op jit(solution)/shard_map/while/body/pallas_call | solution.py:45
  212.1 1.6 broadcast_in_dim.62
  215.6 0.8 constant_dynamic-update-slice_fusion.2
  217.1 7.3 %copy.36 = f32[4,32,4096]{1,0,2:T(4,128)} copy(f32[4,32,4096]{2,1,0:T(8,128)} %get-tuple-element.156) | data formatting | bytes 4194304 | tf_op jit(solution)/shard_map/while | solution.py:131
  224.4 0.0 all-reduce.7.cloned.1.call-update
  224.4 0.5 copy-done.9
  224.9 0.1 broadcast_in_dim.46
  225.0 0.1 eq.63
  225.1 0.6 dynamic-slice
  226.3 0.0 copy-start.4
  226.4 308.8 %all-reduce.7.cloned.1.call-done = f32[4,32,4096]{1,0,2:T(4,128)} async-done(((f32[4,32,4096]{1,0,2:T(4,128)}), f32[4,32,4096]{1,0,2:T(4,128)}) %all-reduce.7.cloned.1.call-update) | async-done | bytes 2097168
  535.1 1.3 fusion.6
  536.4 0.7 reshape.88
  537.1 4.3 all_to_all.15
  541.3 0.5 broadcast.43
  541.8 1.4 reduce
  543.3 0.6 reshape.89
  543.9 0.3 copy.37
  544.2 0.8 fusion.4
  (26 shorter events, 0.1 us)
Async XLA Ops:
  6.5 41.4 %all-gather.5.cloned.1.call-start = ((), (), s32[]{:S(2)}) async-start(), calls=%async_computation.1 | async-start | bytes 1179648 | tf_op jit(solution)/shard_map/all_gather | solution.py:75
  7.3 71.7 %all-gather.7.cloned.1.call-start = ((), (), s32[]{:S(2)}) async-start(), calls=%async_computation.2 | async-start | bytes 3145728 | tf_op jit(solution)/shard_map/all_gather | solution.py:79
  50.6 484.6 %all-reduce.7.cloned.1.call-start = ((), (), s32[]{:S(2)}) async-start(), calls=%async_computation.3 | async-start | bytes 16777216
  54.2 3.5 copy-start.5
  57.7 11.1 %copy-start.8 = (s32[4,324]{1,0:T(4,128)S(1)}, s32[4,324]{1,0:T(4,128)}, u32[]{:S(2)}) copy-start(s32[4,324]{1,0:T(4,128)} %param.15) | copy-start | bytes 15556
  70.8 5.8 %copy-start = (s32[324,2048]{0,1:T(8,128)S(1)}, s32[324,2048]{0,1:T(8,128)}, u32[]{:S(2)}) copy-start(s32[324,2048]{0,1:T(8,128)} %copy.32) | copy-start | bytes 7962628
  79.0 2.2 copy-start.3
  81.2 8.7 %copy-start.1 = (bf16[2,336,256]{2,1,0:T(8,128)(2,1)S(1)}, bf16[2,336,256]{2,1,0:T(8,128)(2,1)}, u32[]{:S(2)}) copy-start(bf16[2,336,256]{2,1,0:T(8,128)(2,1)} %pad.22.clone) | copy-start | bytes 1032196
  81.2 8.7 %copy-start.2 = (bf16[336,336]{1,0:T(8,128)(2,1)S(1)}, bf16[336,336]{1,0:T(8,128)(2,1)}, u32[]{:S(2)}) copy-start(bf16[336,336]{1,0:T(8,128)(2,1)} %pad.21) | copy-start | bytes 677380
  81.2 8.7 %copy-start.7 = (s32[4]{0:T(128)S(1)}, s32[4]{0:T(128)}, u32[]{:S(2)}) copy-start(s32[4]{0:T(128)} %get-tuple-element.328) | copy-start | bytes 52
  224.4 0.6 copy-start.9
  224.4 0.7 copy-start.10
  226.3 317.9 %copy-start.4 = (bf16[256,256]{1,0:T(8,128)(2,1)S(1)}, bf16[256,256]{1,0:T(8,128)(2,1)}, u32[]{:S(2)}) copy-start(bf16[256,256]{1,0:T(8,128)(2,1)} %param.10) | copy-start | bytes 393220
  226.3 317.9 %copy-start.6 = (f32[256,256]{1,0:T(8,128)S(1)}, f32[256,256]{1,0:T(8,128)}, u32[]{:S(2)}) copy-start(f32[256,256]{1,0:T(8,128)} %param.11) | copy-start | bytes 786436
Sparse Core Ops, SparseCore 0:
  9.0 38.9 all-gather.4
  50.7 17.6 all-gather.6
  224.5 310.5 all-reduce.6

commit v5 on v4

--- a/solution.py
+++ b/solution.py
@@ -125,12 +125,13 @@
         )
         summed = mix_block(integ_pad, picked, sign_q, table_all, total_blocks, block_len)
         rows_out = summed.reshape(sub_rows, total_blocks * block_len)
-        return lax.dynamic_update_index_in_dim(buffer, rows_out, local_blk, 0)
+        return lax.dynamic_update_slice(
+            buffer, rows_out[None], (local_blk, member * sub_rows, 0)
+        )
 
-    empty = jnp.zeros((per_device, sub_rows, total_blocks * block_len), jnp.float32)
+    empty = jnp.zeros((per_device, block_len, total_blocks * block_len), jnp.float32)
     buffer = lax.fori_loop(0, own_count, one_block, empty)
-    summed = lax.psum_scatter(buffer, "g", scatter_dimension=2, tiled=True)
-    summed = lax.all_to_all(summed, "m", 2, 1, tiled=True)
+    summed = lax.psum_scatter(buffer, ("g", "m"), scatter_dimension=2, tiled=True)
     placed = summed.reshape(local_rows, local_cols)
     own_live_rows = jnp.repeat(own_flags, block_len)
     total = diagonal * coefficients.astype(jnp.float32) + placed

time: 553 us -> 430 us (0.78)
  waiting for transfers between devices: 349 us -> 118 us
  local copies, waits for them, and re-layouts: 103 us -> 163 us
  Pallas kernels: 44.3 us -> 88.6 us
  loops' own time: 7.35 us -> 13.7 us
    unnamed x4 -> x3, waiting for transfers between devices: 310 us -> 0.74 us
    reduce_scatter x0 -> x1, waiting for transfers between devices: none -> 76.9 us  [on_device(): lax.psum_scatter(buffer, ('g', 'm'), scatter_dimension=2, tiled=True)]
    gather x2 -> x4, local copies, waits for them, and re-layouts: 67.6 us -> 135 us  [one_block(): lax.gather(coeff_ext, row_ids[:, :, None], dims, slice_sizes=(1, wide_col...]
    pallas_call x2 -> x4, Pallas kernels: 44.3 us -> 88.6 us  [mix_block(): pl.pallas_call(mix_kernel, out_shape=jax.ShapeDtypeStruct((rows, targets,...]
    while x1 -> x0, local copies, waits for them, and re-layouts: 7.25 us -> none  [on_device(): buffer = lax.fori_loop(0, own_count, one_block, empty)]
    another operation x1, loops' own time: 7.35 us -> 13.7 us  [on_device(): buffer = lax.fori_loop(0, own_count, one_block, empty)]
    reshape x0 -> x4, local copies, waits for them, and re-layouts: none -> 6.32 us  [one_block(): rows_out[None]]
where the time goes in v5:
time: 430 us; the launch traced here: 428 us
  local copies, waits for them, and re-layouts  163 us (38%)
  waiting for transfers between devices  118 us (27%)
  Pallas kernels  88.6 us (21%)
  other arithmetic  22.3 us (5%)
  loops' own time  13.7 us (3%)
  between operations  13.3 us (3%)
  blocking collectives  9.5 us (2%)
    gather x4, local copies, waits for them, and re-layouts, one_block(): lax.gather(coeff_ext, row_ids[:, :, None], dims, slice_sizes=(1, wide_col...  135 us
    pallas_call x4, Pallas kernels, mix_block(): pl.pallas_call(mix_kernel, out_shape=jax.ShapeDtypeStruct((rows, targets,...  88.6 us
    reduce_scatter x1, waiting for transfers between devices, on_device(): lax.psum_scatter(buffer, ('g', 'm'), scatter_dimension=2, tiled=True)  76.9 us
    all_gather x1, waiting for transfers between devices, on_device(): gathered = lax.all_gather(coefficients, 'alpha', axis=0, tiled=True)  39.8 us
    another operation x1, loops' own time, on_device(): buffer = lax.fori_loop(0, own_count, one_block, empty)  13.7 us
  transfers between devices with their start and end apart: 3, of which 2 were waited for; matrix products, arithmetic and copies ran while one was open for 4% of the time, Pallas kernels for 0%

profile of v5, /device:TPU:1, one launch (start us, length us, event | category | flops | bytes accessed | tf_op | source)
XLA Modules:
  0.0 428.4 jit_solution(12226674364081971237)
XLA Ops:
  6.5 0.7 all-gather.5.cloned.1.call-update
  7.3 0.7 fusion.5
  8.0 0.1 broadcast_in_dim.44
  8.0 0.1 convert_element_type.28
  8.1 39.8 %all-gather.5.cloned.1.call-done = bf16[2048,256]{1,0:T(8,128)(2,1)} async-done(((bf16[256,256]{1,0:T(8,128)(2,1)}), bf16[2048,256]{1,0:T(8,128)(2,1)}) %all-gather.5.cloned.1.call-update) | async-done | bytes 1048592 | tf_op jit(solution)/shard_map/all_gather | solution.py:75
  48.0 2.6 broadcast_multiply_fusion
  50.6 0.6 broadcast_compare_fusion
  51.2 0.7 reduce-window.9
  52.0 0.7 eq.66
  52.6 7.0 %all-gather.1 = s32[2,4,324]{2,1,0:T(4,128)S(1)} all-gather(s32[1,4,324]{2,1,0:T(4,128)} %bitcast.25), channel_id=1, replica_groups=mesh['alpha'=8,'g'=8,'m'=2] {'m'}, dimensions={0}, use_global_device_ids=true | all-gather | bytes 15552 | tf_op jit(solution)/shard_map/all_gather | solution.py:91
  59.7 2.5 all-gather
  62.1 0.1 convert.10
  62.3 0.4 reshape.66
  62.7 0.3 copy.24
  63.0 0.2 copy.26
  63.2 0.7 pad.21
  63.9 0.8 pad.22.clone
  64.7 2.5 copy.22
  67.2 3.4 copy.20
  70.6 0.6 pad.27.clone
  71.2 0.1 eq.68
  71.3 0.2 bitcast_compare_fusion
  71.5 0.1 pad_convert_fusion
  71.5 1.3 bitcast_subtract_fusion
  72.9 2.4 fusion.3
  75.3 1.9 pad_bitcast_fusion
  77.2 2.1 neg.3
  79.3 0.1 copy-done.2
  79.4 7.1 %maximum_maximum_fusion = bf16[4112,512]{1,0:T(8,128)(2,1)} fusion(bf16[2048,512]{1,0:T(8,128)(2,1)S(1)} %neg.3, bf16[2048,512]{1,0:T(8,128)(2,1)S(1)} %copy-done.2, bf16[4112]{0:T(1024)(128)(2,1)S(1)} %copy-done.6), kind=kLoop, calls=%fused_computation.8 | loop fusion | flops 12632064 | bytes 8413216 | tf_op jit(solution)/shard_map/concatenate | solution.py:81
  86.6 2.5 broadcast_in_dim.42
  89.0 253.4 %while.13 = (s32[]{:T(128)}, f32[4,64,4096]{2,1,0:T(8,128)}, s32[]{:T(128)}, s32[4]{0:T(128)S(1)}, s32[4]{0:T(128)S(1)}, /*index=5*/s32[]{:T(128)}, s32[]{:T(128...) while((s32[]{:T(128)}, f32[4,64,4096]{2,1,0:T(8,128)}, ...), condition=%wide.region_4.5_spmd.clone, body=%wide.region_2.4_spmd.clone.sunk | while | flops 11294 | bytes 24421188 | solution.py:133
  89.8 0.6 fusion.7
  93.1 0.8 constant_dynamic-slice_fusion.2
  93.9 0.1 reshape.96
  94.0 33.8 %gather_fusion = bf16[10752,512]{1,0:T(8,128)(2,1)} fusion(bf16[4112,512]{1,0:T(8,128)(2,1)} %get-tuple-element.375, s32[11264]{0:T(1024)S(1)} %pad_clamp_fusion.2), kind=kCustom, calls=%fused_computation.clone.clone.1 | custom fusion | bytes 22063104 | tf_op jit(solution)/shard_map/while/body/gather | solution.py:119
  127.8 22.1 %body.3 = f32[32,64,64]{2,1,0:T(8,128)} custom-call(bf16[336,336]{1,0:T(8,128)(2,1)S(1)} %get-tuple-element.376.integ_ref, bf16[32,336,512]{2,1,0:T(8,128)(2,1)} %bitcast.19, bf16[2,336,256]{2,1,0:T(8,128)(2,1)S(1)} %get-tuple-element.377.sign_ref, bf16[2,256,336]{2,1,0:T(8,128)(2,1)S(1)} %get-tuple-element.378.table_ref), custom_call_target="tpu_custom_call" | custom-call | tf_op jit(solution)/shard_map/while/body/pallas_call | solution.py:45
  149.9 1.6 reshape.97
  151.5 0.9 constant_dynamic-update-slice_fusion.2
  153.0 0.6 fusion.7
  156.2 0.8 constant_dynamic-slice_fusion.2
  157.0 0.1 reshape.96
  157.2 33.8 %gather_fusion = bf16[10752,512]{1,0:T(8,128)(2,1)} fusion(bf16[4112,512]{1,0:T(8,128)(2,1)} %get-tuple-element.375, s32[11264]{0:T(1024)S(1)} %pad_clamp_fusion.2), kind=kCustom, calls=%fused_computation.clone.clone.1 | custom fusion | bytes 22063104 | tf_op jit(solution)/shard_map/while/body/gather | solution.py:119
  190.9 22.1 %body.3 = f32[32,64,64]{2,1,0:T(8,128)} custom-call(bf16[336,336]{1,0:T(8,128)(2,1)S(1)} %get-tuple-element.376.integ_ref, bf16[32,336,512]{2,1,0:T(8,128)(2,1)} %bitcast.19, bf16[2,336,256]{2,1,0:T(8,128)(2,1)S(1)} %get-tuple-element.377.sign_ref, bf16[2,256,336]{2,1,0:T(8,128)(2,1)S(1)} %get-tuple-element.378.table_ref), custom_call_target="tpu_custom_call" | custom-call | tf_op jit(solution)/shard_map/while/body/pallas_call | solution.py:45
  213.1 1.6 reshape.97
  214.7 0.8 constant_dynamic-update-slice_fusion.2
  216.1 0.6 fusion.7
  219.4 0.8 constant_dynamic-slice_fusion.2
  220.2 0.1 reshape.96
  220.3 33.8 %gather_fusion = bf16[10752,512]{1,0:T(8,128)(2,1)} fusion(bf16[4112,512]{1,0:T(8,128)(2,1)} %get-tuple-element.375, s32[11264]{0:T(1024)S(1)} %pad_clamp_fusion.2), kind=kCustom, calls=%fused_computation.clone.clone.1 | custom fusion | bytes 22063104 | tf_op jit(solution)/shard_map/while/body/gather | solution.py:119
  254.1 22.1 %body.3 = f32[32,64,64]{2,1,0:T(8,128)} custom-call(bf16[336,336]{1,0:T(8,128)(2,1)S(1)} %get-tuple-element.376.integ_ref, bf16[32,336,512]{2,1,0:T(8,128)(2,1)} %bitcast.19, bf16[2,336,256]{2,1,0:T(8,128)(2,1)S(1)} %get-tuple-element.377.sign_ref, bf16[2,256,336]{2,1,0:T(8,128)(2,1)S(1)} %get-tuple-element.378.table_ref), custom_call_target="tpu_custom_call" | custom-call | tf_op jit(solution)/shard_map/while/body/pallas_call | solution.py:45
  276.2 1.6 reshape.97
  277.8 0.9 constant_dynamic-update-slice_fusion.2
  279.3 0.6 fusion.7
  282.5 0.8 constant_dynamic-slice_fusion.2
  283.3 0.1 reshape.96
  283.5 33.8 %gather_fusion = bf16[10752,512]{1,0:T(8,128)(2,1)} fusion(bf16[4112,512]{1,0:T(8,128)(2,1)} %get-tuple-element.375, s32[11264]{0:T(1024)S(1)} %pad_clamp_fusion.2), kind=kCustom, calls=%fused_computation.clone.clone.1 | custom fusion | bytes 22063104 | tf_op jit(solution)/shard_map/while/body/gather | solution.py:119
  317.2 22.1 %body.3 = f32[32,64,64]{2,1,0:T(8,128)} custom-call(bf16[336,336]{1,0:T(8,128)(2,1)S(1)} %get-tuple-element.376.integ_ref, bf16[32,336,512]{2,1,0:T(8,128)(2,1)} %bitcast.19, bf16[2,336,256]{2,1,0:T(8,128)(2,1)S(1)} %get-tuple-element.377.sign_ref, bf16[2,256,336]{2,1,0:T(8,128)(2,1)S(1)} %get-tuple-element.378.table_ref), custom_call_target="tpu_custom_call" | custom-call | tf_op jit(solution)/shard_map/while/body/pallas_call | solution.py:45
  339.4 1.6 reshape.97
  341.0 0.8 constant_dynamic-update-slice_fusion.2
  342.5 0.5 copy-done.8
  343.0 0.1 broadcast_in_dim.40
  343.1 0.1 eq.63
  343.2 76.9 %reduce-scatter.2.cloned.1.call-done = f32[4,64,256]{2,1,0:T(8,128)} async-done(((f32[4,64,4096]{2,1,0:T(8,128)}), f32[4,64,256]{2,1,0:T(8,128)}) %reduce-scatter.2.cloned.1.call-update) | async-done | bytes 262160 | tf_op jit(solution)/shard_map/reduce_scatter | solution.py:134
  420.1 1.8 fusion.4
  (29 shorter events, 0.2 us)
Async XLA Ops:
  6.5 56.6 %copy-start.5 = (bf16[324,324]{1,0:T(8,128)(2,1)S(1)}, bf16[324,324]{1,0:T(8,128)(2,1)}, u32[]{:S(2)}) copy-start(bf16[324,324]{1,0:T(8,128)(2,1)} %param.12) | copy-start | bytes 629860
  6.5 41.4 %all-gather.5.cloned.1.call-start = ((), (), s32[]{:S(2)}) async-start(), calls=%async_computation.1 | async-start | bytes 1179648 | tf_op jit(solution)/shard_map/all_gather | solution.py:75
  7.3 69.9 %all-gather.7.cloned.1.call-start = ((), (), s32[]{:S(2)}) async-start(), calls=%async_computation.2 | async-start | bytes 3145728 | tf_op jit(solution)/shard_map/all_gather | solution.py:79
  50.6 369.5 %reduce-scatter.2.cloned.1.call-start = ((), (), s32[]{:S(2)}) async-start(), calls=%async_computation.3 | async-start | bytes 4456448 | tf_op jit(solution)/shard_map/reduce_scatter | solution.py:134
  67.2 4.1 copy-start.7
  75.3 4.1 copy-start.6
  77.2 2.2 copy-start.2
  86.5 2.5 copy-start
  86.5 2.5 copy-start.1
  342.4 0.6 copy-start.8
  342.4 77.7 %copy-start.3 = (bf16[256,256]{1,0:T(8,128)(2,1)S(1)}, bf16[256,256]{1,0:T(8,128)(2,1)}, u32[]{:S(2)}) copy-start(bf16[256,256]{1,0:T(8,128)(2,1)} %param.10) | copy-start | bytes 393220
  342.4 77.7 %copy-start.4 = (f32[256,256]{1,0:T(8,128)S(1)}, f32[256,256]{1,0:T(8,128)}, u32[]{:S(2)}) copy-start(f32[256,256]{1,0:T(8,128)} %param.11) | copy-start | bytes 786436
Sparse Core Ops, SparseCore 0:
  9.0 38.9 all-gather.4
  50.7 17.6 all-gather.6
  342.6 77.4 reduce-scatter.1

commit v6 on v5

--- a/solution.py
+++ b/solution.py
@@ -104,16 +104,13 @@
     )
 
     own_flags = lax.dynamic_slice_in_dim(live_flags, alpha_rank * per_device, per_device, 0)
-    own_count = jnp.sum(own_flags)
-    own_pos = jnp.cumsum(own_flags) - own_flags
-    local_iota = jnp.arange(per_device, dtype=jnp.int32)
 
     dims = lax.GatherDimensionNumbers(
         offset_dims=(2,), collapsed_slice_dims=(0,), start_index_map=(0,)
     )
 
-    def one_block(slot_idx, buffer):
-        local_blk = jnp.sum(jnp.where((own_flags == 1) & (own_pos == slot_idx), local_iota, 0))
+    parts = []
+    for local_blk in range(per_device):
         first_row = (alpha_rank * per_device + local_blk) * block_len + member * sub_rows
         row_ids = lax.dynamic_slice_in_dim(row_ext, first_row, sub_rows, 0)
         picked = lax.gather(
@@ -125,14 +122,13 @@
         )
         summed = mix_block(integ_pad, picked, sign_q, table_all, total_blocks, block_len)
         rows_out = summed.reshape(sub_rows, total_blocks * block_len)
-        return lax.dynamic_update_slice(
-            buffer, rows_out[None], (local_blk, member * sub_rows, 0)
+        full = lax.dynamic_update_slice(
+            jnp.zeros((block_len, total_blocks * block_len), jnp.float32),
+            rows_out,
+            (member * sub_rows, 0),
         )
-
-    empty = jnp.zeros((per_device, block_len, total_blocks * block_len), jnp.float32)
-    buffer = lax.fori_loop(0, own_count, one_block, empty)
-    summed = lax.psum_scatter(buffer, ("g", "m"), scatter_dimension=2, tiled=True)
-    placed = summed.reshape(local_rows, local_cols)
+        parts.append(lax.psum_scatter(full, ("g", "m"), scatter_dimension=1, tiled=True))
+    placed = jnp.concatenate(parts, axis=0)
     own_live_rows = jnp.repeat(own_flags, block_len)
     total = diagonal * coefficients.astype(jnp.float32) + placed
     return jnp.where(own_live_rows[:, None] == 1, total, jnp.zeros_like(total))

time: 430 us -> 423 us (0.984)
  waiting for transfers between devices: 118 us -> 141 us
  loops' own time: 13.7 us -> 0 us
  local copies, waits for them, and re-layouts: 163 us -> 150 us
  other arithmetic: 22.3 us -> 17.8 us
    reduce_scatter x1 -> x4, waiting for transfers between devices: 76.9 us -> 98 us  [on_device(): lax.psum_scatter(full, ('g', 'm'), scatter_dimension=1, tiled=True)]
    another operation x1 -> x0, loops' own time: 13.7 us -> none  [on_device(): buffer = lax.fori_loop(0, own_count, one_block, empty)]
    all_gather x1, blocking collectives: 7.02 us -> 1.87 us  [on_device(): beta_block2 = lax.all_gather(beta_block, 'm', axis=0, tiled=True)]
    all_gather x1, blocking collectives: 2.48 us -> 7.24 us  [on_device(): beta_sign2 = lax.all_gather(beta_sign, 'm', axis=0, tiled=True)]
  transfers between devices with their start and end apart: 3 -> 6, of which waited for: 2 -> 4; matrix products, arithmetic and copies ran while one was open for 4% -> 27% of each run, Pallas kernels for 0% -> 16%
where the time goes in v6:
time: 423 us; the launch traced here: 421 us
  local copies, waits for them, and re-layouts  150 us (35%)
  waiting for transfers between devices  141 us (33%)
  Pallas kernels  89.5 us (21%)
  other arithmetic  17.8 us (4%)
  between operations  13.7 us (3%)
  blocking collectives  9.1 us (2%)
    gather x4, local copies, waits for them, and re-layouts, on_device(): lax.gather(coeff_ext, row_ids[:, :, None], dims, slice_sizes=(1, wide_col...  135 us
    reduce_scatter x4, waiting for transfers between devices, on_device(): lax.psum_scatter(full, ('g', 'm'), scatter_dimension=1, tiled=True)  98 us
    pallas_call x4, Pallas kernels, mix_block(): pl.pallas_call(mix_kernel, out_shape=jax.ShapeDtypeStruct((rows, targets,...  89.5 us
    all_gather x1, waiting for transfers between devices, on_device(): gathered = lax.all_gather(coefficients, 'alpha', axis=0, tiled=True)  39.8 us
  transfers between devices with their start and end apart: 6, of which 4 were waited for; matrix products, arithmetic and copies ran while one was open for 27% of the time, Pallas kernels for 16%

profile of v6, /device:TPU:1, one launch (start us, length us, event | category | flops | bytes accessed | tf_op | source)
XLA Modules:
  0.0 421.3 jit_solution(15816104324919078787)
XLA Ops:
  6.5 0.7 all-gather.5.cloned.1.call-update
  7.3 0.0 all-gather.7.cloned.1.call-start
  7.3 0.7 compare_convert_fusion
  8.0 0.1 broadcast_in_dim.40
  8.1 0.1 convert_element_type.28
  8.2 39.8 %all-gather.5.cloned.1.call-done = bf16[2048,256]{1,0:T(8,128)(2,1)} async-done(((bf16[256,256]{1,0:T(8,128)(2,1)}), bf16[2048,256]{1,0:T(8,128)(2,1)}) %all-gather.5.cloned.1.call-update) | async-done | bytes 1048592 | tf_op jit(solution)/shard_map/all_gather | solution.py:75
  48.0 2.5 broadcast_multiply_fusion
  50.5 0.0 all-gather.7.cloned.1.call-update
  50.5 0.0 reduce-scatter.5.cloned.1.call-start
  50.6 2.3 fusion
  53.0 0.3 fusion.2
  53.2 0.1 copy.16
  53.3 0.1 reshape.50
  53.5 7.2 %all-gather = s32[2,4,20736]{2,1,0:T(4,128)S(1)} all-gather(s32[1,4,20736]{2,1,0:T(4,128)S(1)} %bitcast.26), channel_id=1, replica_groups=mesh['alpha'=8,'g'=8,'m'=2] {'m'}, dimensions={0}, use_global_device_ids=true | all-gather | bytes 995328 | tf_op jit(solution)/shard_map/all_gather | solution.py:92
  60.7 0.1 convert.10
  60.8 0.4 reshape.42
  61.2 0.3 copy.17
  61.5 0.2 copy.18
  61.7 1.9 all-gather.1
  63.6 0.1 eq.51
  63.7 0.8 pad.21.sign_ref
  64.5 0.7 pad.19.integ_ref
  65.2 0.1 eq.53
  65.3 0.2 bitcast_compare_fusion
  65.4 0.8 pad_convert_fusion.table_ref
  66.3 2.0 all-gather.7.cloned.1.call-done
  68.3 2.1 neg.3
  70.5 0.1 copy-done
  70.6 7.1 %maximum_maximum_fusion = bf16[4112,512]{1,0:T(8,128)(2,1)} fusion(bf16[2048,512]{1,0:T(8,128)(2,1)S(1)} %neg.3, bf16[2048,512]{1,0:T(8,128)(2,1)S(1)} %copy-done, bf16[4112]{0:T(1024)(128)(2,1)S(1)} %pad.30.clone), kind=kLoop, calls=%fused_computation.4 | loop fusion | flops 12632064 | bytes 8413216 | tf_op jit(solution)/shard_map/concatenate | solution.py:81
  77.7 33.8 %gather_fusion = bf16[10752,512]{1,0:T(8,128)(2,1)} fusion(bf16[4112,512]{1,0:T(8,128)(2,1)} %maximum_maximum_fusion, s32[11264]{0:T(1024)S(1)} %pad_clamp_fusion.3), kind=kCustom, calls=%fused_computation | custom fusion | bytes 22063104 | tf_op jit(solution)/shard_map/gather | solution.py:116
  111.5 22.3 %shard_map.82 = f32[32,64,64]{2,1,0:T(8,128)} custom-call(bf16[336,336]{1,0:T(8,128)(2,1)} %pad.19.integ_ref, bf16[32,336,512]{2,1,0:T(8,128)(2,1)} %bitcast.20, bf16[2,336,256]{2,1,0:T(8,128)(2,1)} %pad.21.sign_ref, bf16[2,256,336]{2,1,0:T(8,128)(2,1)} %pad_convert_fusion.table_ref), custom_call_target="tpu_custom_call" | custom-call | tf_op jit(solution)/shard_map/pallas_call | solution.py:45
  133.8 1.6 reshape.44
  135.4 0.1 broadcast.31.clone.3
  135.5 1.0 copy-done.2
  136.6 0.2 reduce-scatter.7.cloned.1.call-start
  136.8 0.1 copy.19
  136.9 0.1 reshape.58
  137.0 33.8 %gather_fusion.1 = bf16[10752,512]{1,0:T(8,128)(2,1)} fusion(bf16[4112,512]{1,0:T(8,128)(2,1)} %maximum_maximum_fusion, s32[11264]{0:T(1024)S(1)} %pad_clamp_fusion.2), kind=kCustom, calls=%fused_computation.1 | custom fusion | bytes 22063104 | tf_op jit(solution)/shard_map/gather | solution.py:116
  170.8 22.4 %shard_map.83 = f32[32,64,64]{2,1,0:T(8,128)} custom-call(bf16[336,336]{1,0:T(8,128)(2,1)} %pad.19.integ_ref, bf16[32,336,512]{2,1,0:T(8,128)(2,1)} %bitcast.21, bf16[2,336,256]{2,1,0:T(8,128)(2,1)} %pad.21.sign_ref, bf16[2,256,336]{2,1,0:T(8,128)(2,1)} %pad_convert_fusion.table_ref), custom_call_target="tpu_custom_call" | custom-call | tf_op jit(solution)/shard_map/pallas_call | solution.py:45
  193.2 1.6 reshape.45
  194.7 0.1 broadcast.31.clone.2
  194.9 1.0 copy-done.3
  195.9 0.0 reduce-scatter.9.cloned.1.call-start
  195.9 0.1 copy.20
  196.0 0.1 reshape.66
  196.2 33.8 %gather_fusion.2 = bf16[10752,512]{1,0:T(8,128)(2,1)} fusion(bf16[4112,512]{1,0:T(8,128)(2,1)} %maximum_maximum_fusion, s32[11264]{0:T(1024)S(1)} %pad_clamp_fusion.1), kind=kCustom, calls=%fused_computation.2 | custom fusion | bytes 22063104 | tf_op jit(solution)/shard_map/gather | solution.py:116
  230.0 22.3 %shard_map.84 = f32[32,64,64]{2,1,0:T(8,128)} custom-call(bf16[336,336]{1,0:T(8,128)(2,1)} %pad.19.integ_ref, bf16[32,336,512]{2,1,0:T(8,128)(2,1)} %bitcast.22, bf16[2,336,256]{2,1,0:T(8,128)(2,1)} %pad.21.sign_ref, bf16[2,256,336]{2,1,0:T(8,128)(2,1)} %pad_convert_fusion.table_ref), custom_call_target="tpu_custom_call" | custom-call | tf_op jit(solution)/shard_map/pallas_call | solution.py:45
  252.3 1.6 reshape.46
  253.9 0.1 broadcast.31.clone.1
  254.0 1.0 copy-done.4
  255.0 0.3 reduce-scatter.11.cloned.1.call-start
  255.3 0.1 copy.21
  255.4 0.1 reshape.74
  255.5 33.8 %gather_fusion.3 = bf16[10752,512]{1,0:T(8,128)(2,1)} fusion(bf16[4112,512]{1,0:T(8,128)(2,1)} %maximum_maximum_fusion, s32[11264]{0:T(1024)S(1)} %pad_clamp_fusion), kind=kCustom, calls=%fused_computation.3 | custom fusion | bytes 22063104 | tf_op jit(solution)/shard_map/gather | solution.py:116
  289.3 22.4 %shard_map.85 = f32[32,64,64]{2,1,0:T(8,128)} custom-call(bf16[336,336]{1,0:T(8,128)(2,1)} %pad.19.integ_ref, bf16[32,336,512]{2,1,0:T(8,128)(2,1)} %bitcast.19, bf16[2,336,256]{2,1,0:T(8,128)(2,1)} %pad.21.sign_ref, bf16[2,256,336]{2,1,0:T(8,128)(2,1)} %pad_convert_fusion.table_ref), custom_call_target="tpu_custom_call" | custom-call | tf_op jit(solution)/shard_map/pallas_call | solution.py:45
  311.7 1.6 reshape.47
  313.4 0.1 broadcast.31.clone
  313.5 1.0 copy-done.1
  314.5 0.1 dynamic-slice_compare_fusion
  314.6 0.1 broadcast_in_dim.38
  314.7 0.1 eq.48
  314.8 27.8 %reduce-scatter.9.cloned.1.call-done = f32[64,256]{1,0:T(8,128)} async-done(((f32[64,4096]{1,0:T(8,128)}), f32[64,256]{1,0:T(8,128)}) %reduce-scatter.9.cloned.1.call-update) | async-done | bytes 65552 | tf_op jit(solution)/shard_map/reduce_scatter | solution.py:130
  342.6 70.1 %reduce-scatter.11.cloned.1.call-done = f32[64,256]{1,0:T(8,128)} async-done(((f32[64,4096]{1,0:T(8,128)}), f32[64,256]{1,0:T(8,128)}) %reduce-scatter.11.cloned.1.call-update) | async-done | bytes 65552 | tf_op jit(solution)/shard_map/reduce_scatter | solution.py:130
  412.7 1.7 fusion.1
  (36 shorter events, 0.3 us)
Async XLA Ops:
  6.5 44.1 %copy-start.5 = (s32[324,2048]{1,0:T(8,128)S(1)}, s32[324,2048]{1,0:T(8,128)}, u32[]{:S(2)}) copy-start(s32[324,2048]{1,0:T(8,128)} %param.11) | copy-start | bytes 7962628
  6.5 41.4 %all-gather.5.cloned.1.call-start = ((), (), s32[]{:S(2)}) async-start(), calls=%async_computation.4 | async-start | bytes 1179648 | tf_op jit(solution)/shard_map/all_gather | solution.py:75
  7.3 61.1 %all-gather.7.cloned.1.call-start = ((), (), s32[]{:S(2)}) async-start(), calls=%async_computation.5 | async-start | bytes 3145728 | tf_op jit(solution)/shard_map/all_gather | solution.py:79
  50.5 264.2 %reduce-scatter.5.cloned.1.call-start = ((), (), s32[]{:S(2)}) async-start(), calls=%async_computation.6 | async-start | bytes 1114112 | tf_op jit(solution)/shard_map/reduce_scatter | solution.py:130
  50.6 2.8 copy-start.7
  52.9 8.8 %copy-start.10 = (s32[4,324]{1,0:T(4,128)S(1)}, s32[4,324]{1,0:T(4,128)}, u32[]{:S(2)}) copy-start(s32[4,324]{1,0:T(4,128)} %param.13) | copy-start | bytes 15556
  53.0 11.5 %copy-start.9 = (bf16[324,324]{1,0:T(8,128)(2,1)S(1)}, bf16[324,324]{1,0:T(8,128)(2,1)}, u32[]{:S(2)}) copy-start(bf16[324,324]{1,0:T(8,128)(2,1)} %param.10) | copy-start | bytes 629860
  68.3 2.2 copy-start
  135.5 1.0 copy-start.2
  136.6 178.2 %reduce-scatter.7.cloned.1.call-start = ((), (), s32[]{:S(2)}) async-start(), calls=%async_computation.7 | async-start | bytes 1114112 | tf_op jit(solution)/shard_map/reduce_scatter | solution.py:130
  194.9 1.0 copy-start.3
  195.9 146.7 %reduce-scatter.9.cloned.1.call-start = ((), (), s32[]{:S(2)}) async-start(), calls=%async_computation.8 | async-start | bytes 1114112 | tf_op jit(solution)/shard_map/reduce_scatter | solution.py:130
  254.0 1.0 copy-start.4
  255.0 157.7 %reduce-scatter.11.cloned.1.call-start = ((), (), s32[]{:S(2)}) async-start(), calls=%async_computation.9 | async-start | bytes 1114112 | tf_op jit(solution)/shard_map/reduce_scatter | solution.py:130
  311.7 101.0 %copy-start.6 = (bf16[256,256]{1,0:T(8,128)(2,1)S(1)}, bf16[256,256]{1,0:T(8,128)(2,1)}, u32[]{:S(2)}) copy-start(bf16[256,256]{1,0:T(8,128)(2,1)} %param.8) | copy-start | bytes 393220
  311.7 101.0 %copy-start.8 = (f32[256,256]{1,0:T(8,128)S(1)}, f32[256,256]{1,0:T(8,128)}, u32[]{:S(2)}) copy-start(f32[256,256]{1,0:T(8,128)} %param.9) | copy-start | bytes 786436
  313.5 1.0 copy-start.1
Sparse Core Ops, SparseCore 0:
  9.0 38.9 all-gather.4
  50.7 17.6 all-gather.6
  136.7 66.0 reduce-scatter.4
  206.9 65.9 reduce-scatter.6
  276.5 66.0 reduce-scatter.8
  346.7 65.9 reduce-scatter.10

commit v7 on v6

--- a/solution.py
+++ b/solution.py
@@ -57,6 +57,59 @@
     )(integ_pad, picked, sign_q, table_all)
 
 
+def exchange_kernel(send_ref, recv_ref, send_sem, recv_sem, local_sem):
+    groups = lax.axis_size("g")
+    count = groups * PAIR
+    alpha = lax.axis_index("alpha")
+    me = lax.axis_index("g") * PAIR + lax.axis_index("m")
+
+    def remote(slot, peer):
+        return pltpu.make_async_remote_copy(
+            src_ref=send_ref.at[slot],
+            dst_ref=recv_ref.at[slot],
+            send_sem=send_sem.at[slot],
+            recv_sem=recv_sem.at[slot],
+            device_id=(alpha, peer // PAIR, peer % PAIR),
+            device_id_type=pl.DeviceIdType.MESH,
+        )
+
+    for step in range(1, count):
+        dest = lax.rem(me + step, count)
+        pltpu.make_async_remote_copy(
+            src_ref=send_ref.at[dest],
+            dst_ref=recv_ref.at[me],
+            send_sem=send_sem.at[dest],
+            recv_sem=recv_sem.at[me],
+            device_id=(alpha, dest // PAIR, dest % PAIR),
+            device_id_type=pl.DeviceIdType.MESH,
+        ).start()
+    local = pltpu.make_async_copy(send_ref.at[me], recv_ref.at[me], local_sem)
+    local.start()
+    local.wait()
+    for step in range(1, count):
+        dest = lax.rem(me + step, count)
+        remote(dest, dest).wait_send()
+    for step in range(1, count):
+        src = lax.rem(me + count - step, count)
+        remote(src, src).wait_recv()
+
+
+def exchange(send):
+    count = send.shape[0]
+    return pl.pallas_call(
+        exchange_kernel,
+        out_shape=jax.ShapeDtypeStruct(send.shape, send.dtype),
+        in_specs=[pl.BlockSpec(memory_space=pl.ANY)],
+        out_specs=pl.BlockSpec(memory_space=pl.ANY),
+        scratch_shapes=[
+            pltpu.SemaphoreType.DMA((count,)),
+            pltpu.SemaphoreType.DMA((count,)),
+            pltpu.SemaphoreType.DMA,
+        ],
+        compiler_params=pltpu.CompilerParams(has_side_effects=True),
+    )(send)
+
+
 def on_device(
     coefficients, diagonal, integrals, alpha_row, alpha_sign, beta_block, beta_sign, block_irrep
 ):
@@ -121,14 +174,14 @@
             mode=lax.GatherScatterMode.PROMISE_IN_BOUNDS,
         )
         summed = mix_block(integ_pad, picked, sign_q, table_all, total_blocks, block_len)
-        rows_out = summed.reshape(sub_rows, total_blocks * block_len)
-        full = lax.dynamic_update_slice(
-            jnp.zeros((block_len, total_blocks * block_len), jnp.float32),
-            rows_out,
-            (member * sub_rows, 0),
+        parts.append(
+            summed.reshape(sub_rows, total_blocks // src_blocks, local_cols).transpose(1, 0, 2)
         )
-        parts.append(lax.psum_scatter(full, ("g", "m"), scatter_dimension=1, tiled=True))
-    placed = jnp.concatenate(parts, axis=0)
+    send = jnp.stack(parts, axis=1)
+    recv = exchange(send)
+    groups = recv.shape[0] // PAIR
+    recv = recv.reshape(groups, PAIR, per_device, sub_rows, local_cols).sum(axis=0)
+    placed = recv.transpose(1, 0, 2, 3).reshape(local_rows, local_cols)
     own_live_rows = jnp.repeat(own_flags, block_len)
     total = diagonal * coefficients.astype(jnp.float32) + placed
     return jnp.where(own_live_rows[:, None] == 1, total, jnp.zeros_like(total))

time: 423 us -> 362 us (0.86)
  waiting for transfers between devices: 141 us -> 37.1 us
  Pallas kernels: 89.5 us -> 124 us
    reduce_scatter x4 -> x0, waiting for transfers between devices: 98 us -> none  [on_device(): lax.psum_scatter(full, ('g', 'm'), scatter_dimension=1, tiled=True)]
    pallas_call x0 -> x1, Pallas kernels: none -> 34.9 us  [exchange(): pl.pallas_call(exchange_kernel, out_shape=jax.ShapeDtypeStruct(send.shape...]
    all_gather x1, blocking collectives: 1.87 us -> 6.81 us  [on_device(): beta_block2 = lax.all_gather(beta_block, 'm', axis=0, tiled=True)]
  transfers between devices with their start and end apart: 6 -> 2, of which waited for: 4 -> 1; matrix products, arithmetic and copies ran while one was open for 27% -> 4% of each run, Pallas kernels for 16% -> 0%
where the time goes in v7:
time: 362 us; the launch traced here: 357 us
  local copies, waits for them, and re-layouts  150 us (41%)
  Pallas kernels  124 us (34%)
  waiting for transfers between devices  37.1 us (10%)
  other arithmetic  21.2 us (6%)
  between operations  13.6 us (4%)
  blocking collectives  10.3 us (3%)
    gather x4, local copies, waits for them, and re-layouts, on_device(): lax.gather(coeff_ext, row_ids[:, :, None], dims, slice_sizes=(1, wide_col...  135 us
    pallas_call x4, Pallas kernels, mix_block(): pl.pallas_call(mix_kernel, out_shape=jax.ShapeDtypeStruct((rows, targets,...  89.5 us
    all_gather x1, waiting for transfers between devices, on_device(): gathered = lax.all_gather(coefficients, 'alpha', axis=0, tiled=True)  36.3 us
    pallas_call x1, Pallas kernels, exchange(): pl.pallas_call(exchange_kernel, out_shape=jax.ShapeDtypeStruct(send.shape...  34.9 us
    concatenate x1, other arithmetic, on_device(): jnp.concatenate([gathered, -gathered, jnp.zeros((16, wide_cols), jnp.bflo...  7.29 us
  transfers between devices with their start and end apart: 2, of which 1 were waited for; matrix products, arithmetic and copies ran while one was open for 4% of the time, Pallas kernels for 0%

profile of v7, /device:TPU:1, one launch (start us, length us, event | category | flops | bytes accessed | tf_op | source)
XLA Modules:
  0.0 356.8 jit_solution(5534979415998168667)
XLA Ops:
  6.5 0.0 copy-start.4
  6.5 0.0 all-gather.5.cloned.1.call-start
  6.5 0.7 all-gather.5.cloned.1.call-update
  7.3 0.0 all-gather.7.cloned.1.call-start
  7.3 0.7 compare_convert_fusion
  8.0 0.1 broadcast_in_dim.40
  8.0 0.1 convert_element_type.28
  8.1 3.5 all-gather
  11.7 0.0 copy-start.1
  11.7 36.3 %all-gather.5.cloned.1.call-done = bf16[2048,256]{1,0:T(8,128)(2,1)} async-done(((bf16[256,256]{1,0:T(8,128)(2,1)}), bf16[2048,256]{1,0:T(8,128)(2,1)}) %all-gather.5.cloned.1.call-update) | async-done | bytes 1048592 | tf_op jit(solution)/shard_map/all_gather | solution.py:128
  48.0 2.5 broadcast_multiply_fusion
  50.5 0.0 all-gather.7.cloned.1.call-update
  50.5 0.1 dynamic-slice_compare_fusion
  50.6 0.1 broadcast_in_dim.38
  50.7 0.1 eq.48
  50.8 0.1 eq.51
  50.9 0.0 copy-done.4
  50.9 6.8 %all-gather.1 = s32[2,4,324]{2,1,0:T(4,128)S(1)} all-gather(s32[1,4,324]{2,1,0:T(4,128)S(1)} %bitcast.51), channel_id=1, replica_groups=mesh['alpha'=8,'g'=8,'m'=2] {'m'}, dimensions={0}, use_global_device_ids=true | all-gather | bytes 15552 | tf_op jit(solution)/shard_map/all_gather | solution.py:144
  57.7 0.8 convert.10
  58.5 1.4 reshape.48
  60.0 1.0 copy.31
  61.0 1.2 copy.32
  62.1 1.7 pad.19.integ_ref
  63.8 0.8 pad.21.sign_ref
  64.6 0.0 copy-done.1
  64.6 2.5 fusion
  67.1 0.3 fusion.2
  67.4 0.1 copy.30
  67.5 0.1 reshape.58
  67.6 0.1 copy.34
  67.7 0.1 reshape.66
  67.8 0.1 copy.36
  67.9 0.1 reshape.74
  68.0 0.1 copy.38
  68.1 0.1 reshape.82
  68.3 0.1 eq.53
  68.3 0.2 bitcast_compare_fusion
  68.5 0.8 pad_convert_fusion.table_ref
  69.4 0.0 all-gather.7.cloned.1.call-done
  69.4 0.0 copy-start
  69.4 2.1 neg.3
  71.6 0.1 copy-done
  71.7 7.3 %maximum_maximum_fusion = bf16[4112,512]{1,0:T(8,128)(2,1)} fusion(bf16[2048,512]{1,0:T(8,128)(2,1)S(1)} %neg.3, bf16[2048,512]{1,0:T(8,128)(2,1)S(1)} %copy-done, bf16[4112]{0:T(1024)(128)(2,1)S(1)} %pad.30.clone), kind=kLoop, calls=%fused_computation.4 | loop fusion | flops 12632064 | bytes 8413216 | tf_op jit(solution)/shard_map/concatenate | solution.py:134
  78.9 33.8 %gather_fusion.3 = bf16[10752,512]{1,0:T(8,128)(2,1)} fusion(bf16[4112,512]{1,0:T(8,128)(2,1)} %maximum_maximum_fusion, s32[11264]{0:T(1024)S(1)} %pad_clamp_fusion), kind=kCustom, calls=%fused_computation.3 | custom fusion | bytes 22063104 | tf_op jit(solution)/shard_map/gather | solution.py:169
  112.8 22.4 %shard_map.85 = f32[32,64,64]{2,1,0:T(8,128)} custom-call(bf16[336,336]{1,0:T(8,128)(2,1)} %pad.19.integ_ref, bf16[32,336,512]{2,1,0:T(8,128)(2,1)} %bitcast.42, bf16[2,336,256]{2,1,0:T(8,128)(2,1)} %pad.21.sign_ref, bf16[2,256,336]{2,1,0:T(8,128)(2,1)} %pad_convert_fusion.table_ref), custom_call_target="tpu_custom_call" | custom-call | tf_op jit(solution)/shard_map/pallas_call | solution.py:45
  135.1 1.5 reshape.53
  136.6 33.8 %gather_fusion.2 = bf16[10752,512]{1,0:T(8,128)(2,1)} fusion(bf16[4112,512]{1,0:T(8,128)(2,1)} %maximum_maximum_fusion, s32[11264]{0:T(1024)S(1)} %pad_clamp_fusion.1), kind=kCustom, calls=%fused_computation.2 | custom fusion | bytes 22063104 | tf_op jit(solution)/shard_map/gather | solution.py:169
  170.4 22.4 %shard_map.84 = f32[32,64,64]{2,1,0:T(8,128)} custom-call(bf16[336,336]{1,0:T(8,128)(2,1)} %pad.19.integ_ref, bf16[32,336,512]{2,1,0:T(8,128)(2,1)} %bitcast.43, bf16[2,336,256]{2,1,0:T(8,128)(2,1)} %pad.21.sign_ref, bf16[2,256,336]{2,1,0:T(8,128)(2,1)} %pad_convert_fusion.table_ref), custom_call_target="tpu_custom_call" | custom-call | tf_op jit(solution)/shard_map/pallas_call | solution.py:45
  192.8 1.5 reshape.52
  194.3 33.8 %gather_fusion.1 = bf16[10752,512]{1,0:T(8,128)(2,1)} fusion(bf16[4112,512]{1,0:T(8,128)(2,1)} %maximum_maximum_fusion, s32[11264]{0:T(1024)S(1)} %pad_clamp_fusion.2), kind=kCustom, calls=%fused_computation.1 | custom fusion | bytes 22063104 | tf_op jit(solution)/shard_map/gather | solution.py:169
  228.1 22.4 %shard_map.83 = f32[32,64,64]{2,1,0:T(8,128)} custom-call(bf16[336,336]{1,0:T(8,128)(2,1)} %pad.19.integ_ref, bf16[32,336,512]{2,1,0:T(8,128)(2,1)} %bitcast.44, bf16[2,336,256]{2,1,0:T(8,128)(2,1)} %pad.21.sign_ref, bf16[2,256,336]{2,1,0:T(8,128)(2,1)} %pad_convert_fusion.table_ref), custom_call_target="tpu_custom_call" | custom-call | tf_op jit(solution)/shard_map/pallas_call | solution.py:45
  250.5 1.5 reshape.51
  252.0 33.8 %gather_fusion = bf16[10752,512]{1,0:T(8,128)(2,1)} fusion(bf16[4112,512]{1,0:T(8,128)(2,1)} %maximum_maximum_fusion, s32[11264]{0:T(1024)S(1)} %pad_clamp_fusion.3), kind=kCustom, calls=%fused_computation | custom fusion | bytes 22063104 | tf_op jit(solution)/shard_map/gather | solution.py:169
  285.8 22.4 %shard_map.82 = f32[32,64,64]{2,1,0:T(8,128)} custom-call(bf16[336,336]{1,0:T(8,128)(2,1)} %pad.19.integ_ref, bf16[32,336,512]{2,1,0:T(8,128)(2,1)} %bitcast.41, bf16[2,336,256]{2,1,0:T(8,128)(2,1)} %pad.21.sign_ref, bf16[2,256,336]{2,1,0:T(8,128)(2,1)} %pad_convert_fusion.table_ref), custom_call_target="tpu_custom_call" | custom-call | tf_op jit(solution)/shard_map/pallas_call | solution.py:45
  308.2 1.5 reshape.50
  309.7 0.6 copy_bitcast_fusion
  310.3 0.6 copy_bitcast_fusion.2
  310.9 1.5 pad_maximum_fusion.send_ref
  312.4 0.0 copy-start.2
  312.4 34.9 %shard_map.86 = f32[16,4,32,256]{3,2,1,0:T(8,128)} custom-call(f32[16,4,32,256]{3,2,1,0:T(8,128)} %pad_maximum_fusion.send_ref), custom_call_target="tpu_custom_call" | custom-call | tf_op jit(solution)/shard_map/pallas_call | solution.py:99
  347.3 1.8 reduce_sum.9
  349.1 0.0 copy-done.2
  349.2 0.0 copy-done.3
  349.2 0.8 fusion.1
  (10 shorter events, 0.1 us)
Async XLA Ops:
  6.5 44.3 %copy-start.4 = (s32[4,324]{1,0:T(4,128)S(1)}, s32[4,324]{1,0:T(4,128)}, u32[]{:S(2)}) copy-start(s32[4,324]{1,0:T(4,128)} %param.13) | copy-start | bytes 15556
  6.5 41.4 %all-gather.5.cloned.1.call-start = ((), (), s32[]{:S(2)}) async-start(), calls=%async_computation | async-start | bytes 1179648 | tf_op jit(solution)/shard_map/all_gather | solution.py:128
  7.3 62.2 %all-gather.7.cloned.1.call-start = ((), (), s32[]{:S(2)}) async-start(), calls=%async_computation.1 | async-start | bytes 3145728 | tf_op jit(solution)/shard_map/all_gather | solution.py:132
  11.7 52.9 %copy-start.1 = (s32[324,2048]{1,0:T(8,128)S(1)}, s32[324,2048]{1,0:T(8,128)}, u32[]{:S(2)}) copy-start(s32[324,2048]{1,0:T(8,128)} %param.11) | copy-start | bytes 7962628
  69.4 2.2 copy-start
  312.4 36.7 %copy-start.2 = (bf16[256,256]{1,0:T(8,128)(2,1)S(1)}, bf16[256,256]{1,0:T(8,128)(2,1)}, u32[]{:S(2)}) copy-start(bf16[256,256]{1,0:T(8,128)(2,1)} %param.8) | copy-start | bytes 393220
  312.4 36.7 %copy-start.3 = (f32[256,256]{1,0:T(8,128)S(1)}, f32[256,256]{1,0:T(8,128)}, u32[]{:S(2)}) copy-start(f32[256,256]{1,0:T(8,128)} %param.9) | copy-start | bytes 786436
Sparse Core Ops, SparseCore 0:
  9.0 38.9 all-gather.4
  50.7 17.6 all-gather.6

commit v8 on v7

--- a/solution.py
+++ b/solution.py
@@ -110,6 +110,50 @@
     )(send)
 
 
+def spread_kernel(own_ref, out_ref, send_sem, recv_sem, local_sem):
+    count = lax.axis_size("alpha") * PAIR
+    group = lax.axis_index("g")
+    me = lax.axis_index("alpha") * PAIR + lax.axis_index("m")
+
+    def remote(slot, sem_slot, peer):
+        return pltpu.make_async_remote_copy(
+            src_ref=own_ref,
+            dst_ref=out_ref.at[slot],
+            send_sem=send_sem.at[sem_slot],
+            recv_sem=recv_sem.at[slot],
+            device_id=(peer // PAIR, group, peer % PAIR),
+            device_id_type=pl.DeviceIdType.MESH,
+        )
+
+    for step in range(1, count):
+        dest = lax.rem(me + step, count)
+        remote(me, dest, dest).start()
+    local = pltpu.make_async_copy(own_ref, out_ref.at[me], local_sem)
+    local.start()
+    local.wait()
+    for step in range(1, count):
+        dest = lax.rem(me + step, count)
+        remote(me, dest, dest).wait_send()
+    for step in range(1, count):
+        src = lax.rem(me + count - step, count)
+        remote(src, src, src).wait_recv()
+
+
+def spread(own, count):
+    return pl.pallas_call(
+        spread_kernel,
+        out_shape=jax.ShapeDtypeStruct((count,) + own.shape, own.dtype),
+        in_specs=[pl.BlockSpec(memory_space=pl.ANY)],
+        out_specs=pl.BlockSpec(memory_space=pl.ANY),
+        scratch_shapes=[
+            pltpu.SemaphoreType.DMA((count,)),
+            pltpu.SemaphoreType.DMA((count,)),
+            pltpu.SemaphoreType.DMA,
+        ],
+        compiler_params=pltpu.CompilerParams(has_side_effects=True),
+    )(own)
+
+
 def on_device(
     coefficients, diagonal, integrals, alpha_row, alpha_sign, beta_block, beta_sign, block_irrep
 ):
@@ -125,11 +169,14 @@
     extra = pairs - pair_count
     sub_rows = block_len // PAIR
 
-    gathered = lax.all_gather(coefficients, "alpha", axis=0, tiled=True)
+    alpha_size = lax.axis_size("alpha")
+    gathered = spread(coefficients, alpha_size * PAIR).reshape(
+        alpha_size, PAIR, local_rows, local_cols
+    )
+    gathered = gathered.transpose(0, 2, 1, 3).reshape(alpha_size * local_rows, PAIR * local_cols)
     live_flags = (block_irrep == 0).astype(jnp.int32)
     live_rows = jnp.repeat(live_flags, block_len)
     gathered = gathered * live_rows[:, None].astype(jnp.bfloat16)
-    gathered = lax.all_gather(gathered, "m", axis=1, tiled=True)
     window_rows, wide_cols = gathered.shape
     coeff_ext = jnp.concatenate(
         [gathered, -gathered, jnp.zeros((16, wide_cols), jnp.bfloat16)], axis=0

time: 362 us -> 338 us (0.934)
  waiting for transfers between devices: 37.1 us -> 0 us
  Pallas kernels: 124 us -> 161 us
  between operations: 13.6 us -> 0.23 us
  other arithmetic: 21.2 us -> 14.2 us
  blocking collectives: 10.3 us -> 5.6 us
    pallas_call x0 -> x1, Pallas kernels: none -> 36.5 us  [spread(): pl.pallas_call(spread_kernel, out_shape=jax.ShapeDtypeStruct((count,) + o...]
    all_gather x2 -> x0, waiting for transfers between devices: 36.3 us -> none  [the longest x1 36.3 us: on_device(): gathered = lax.all_gather(coefficients, 'alpha', axis=0, tiled=True)]
    transpose x0 -> x1, local copies, waits for them, and re-layouts: none -> 3.75 us  [on_device(): gathered.transpose(0, 2, 1, 3)]
    all_gather x1, blocking collectives: 6.81 us -> 3.12 us  [on_device(): beta_block2 = lax.all_gather(beta_block, 'm', axis=0, tiled=True)]
  transfers between devices with their start and end apart: 2 -> 0, of which waited for: 1 -> 0; matrix products, arithmetic and copies ran while one was open for 4% -> 0% of each run, Pallas kernels for 0% -> 0%
where the time goes in v8:
time: 338 us; the launch traced here: 333 us
  Pallas kernels  161 us (48%)
  local copies, waits for them, and re-layouts  152 us (45%)
  other arithmetic  14.2 us (4%)
  blocking collectives  5.6 us (2%)
    gather x4, local copies, waits for them, and re-layouts, on_device(): lax.gather(coeff_ext, row_ids[:, :, None], dims, slice_sizes=(1, wide_col...  135 us
    pallas_call x4, Pallas kernels, mix_block(): pl.pallas_call(mix_kernel, out_shape=jax.ShapeDtypeStruct((rows, targets,...  89.4 us
    pallas_call x1, Pallas kernels, spread(): pl.pallas_call(spread_kernel, out_shape=jax.ShapeDtypeStruct((count,) + o...  36.5 us
    pallas_call x1, Pallas kernels, exchange(): pl.pallas_call(exchange_kernel, out_shape=jax.ShapeDtypeStruct(send.shape...  35.1 us
    concatenate x1, other arithmetic, on_device(): jnp.concatenate([gathered, -gathered, jnp.zeros((16, wide_cols), jnp.bflo...  7.36 us

profile of v8, /device:TPU:1, one launch (start us, length us, event | category | flops | bytes accessed | tf_op | source)
XLA Modules:
  0.0 332.7 jit_solution(17511610860436680406)
XLA Ops:
  0.0 0.7 compare_convert_fusion
  0.7 0.1 dynamic-slice_compare_fusion
  0.7 0.1 broadcast_in_dim.38
  0.8 0.1 eq.48
  0.9 0.1 eq.51
  1.0 0.1 broadcast_in_dim.40
  1.1 0.1 convert_element_type.28
  1.2 3.1 all-gather.1
  4.3 1.7 pad.19.integ_ref
  6.0 2.5 all-gather
  8.4 0.1 convert.10
  8.6 0.4 reshape.56
  9.0 0.3 copy.35
  9.3 0.2 copy.36
  9.5 0.7 pad.21.sign_ref
  10.2 0.1 eq.53
  10.3 0.2 bitcast_compare_fusion
  10.5 0.8 pad_convert_fusion.table_ref
  11.3 36.5 %shard_map.82 = bf16[16,256,256]{2,1,0:T(8,128)(2,1)} custom-call(bf16[256,256]{1,0:T(8,128)(2,1)} %own_ref.1), custom_call_target="tpu_custom_call" | custom-call | tf_op jit(solution)/shard_map/pallas_call | solution.py:143
  47.8 3.7 %copy.33 = bf16[8,256,2,256]{3,2,1,0:T(2,128)(2,1)S(1)} copy(bf16[8,256,2,256]{3,1,2,0:T(8,128)(2,1)} %bitcast.53) | data formatting | bytes 4194304 | tf_op jit(solution)/shard_map/transpose | solution.py:176
  51.6 0.5 copy.45
  52.1 0.3 fusion.7
  52.5 0.0 copy-start
  52.5 0.0 copy-start.1
  52.5 7.4 %maximum_maximum_fusion = bf16[4112,512]{1,0:T(8,128)(2,1)} fusion(bf16[2048,512]{1,0:T(8,128)(2,1)S(1)} %get-tuple-element.5, bf16[2048,512]{1,0:T(8,128)(2,1)S(1)} %get-tuple-element.6, bf16[4112]{0:T(1024)(128)(2,1)S(1)} %pad.30.clone), kind=kLoop, calls=%fused_computation.4 | loop fusion | flops 12632064 | bytes 8413216 | tf_op jit(solution)/shard_map/concatenate | solution.py:181
  59.9 0.0 copy-done
  59.9 0.0 copy-done.1
  59.9 0.5 fusion
  60.4 0.3 fusion.2
  60.6 0.1 copy.34
  60.7 0.1 reshape.66
  60.9 0.1 copy.38
  61.0 0.1 reshape.74
  61.1 0.1 copy.40
  61.2 0.1 reshape.82
  61.3 0.1 copy.42
  61.4 0.1 reshape.90
  61.6 33.8 %gather_fusion.3 = bf16[10752,512]{1,0:T(8,128)(2,1)} fusion(bf16[4112,512]{1,0:T(8,128)(2,1)} %maximum_maximum_fusion, s32[11264]{0:T(1024)S(1)} %pad_clamp_fusion), kind=kCustom, calls=%fused_computation.3 | custom fusion | bytes 22063104 | tf_op jit(solution)/shard_map/gather | solution.py:216
  95.4 22.3 %shard_map.86 = f32[32,64,64]{2,1,0:T(8,128)} custom-call(bf16[336,336]{1,0:T(8,128)(2,1)} %pad.19.integ_ref, bf16[32,336,512]{2,1,0:T(8,128)(2,1)} %bitcast.48, bf16[2,336,256]{2,1,0:T(8,128)(2,1)} %pad.21.sign_ref, bf16[2,256,336]{2,1,0:T(8,128)(2,1)} %pad_convert_fusion.table_ref), custom_call_target="tpu_custom_call" | custom-call | tf_op jit(solution)/shard_map/pallas_call | solution.py:45
  117.7 1.5 reshape.61
  119.2 33.8 %gather_fusion.2 = bf16[10752,512]{1,0:T(8,128)(2,1)} fusion(bf16[4112,512]{1,0:T(8,128)(2,1)} %maximum_maximum_fusion, s32[11264]{0:T(1024)S(1)} %pad_clamp_fusion.1), kind=kCustom, calls=%fused_computation.2 | custom fusion | bytes 22063104 | tf_op jit(solution)/shard_map/gather | solution.py:216
  153.0 22.3 %shard_map.85 = f32[32,64,64]{2,1,0:T(8,128)} custom-call(bf16[336,336]{1,0:T(8,128)(2,1)} %pad.19.integ_ref, bf16[32,336,512]{2,1,0:T(8,128)(2,1)} %bitcast.49, bf16[2,336,256]{2,1,0:T(8,128)(2,1)} %pad.21.sign_ref, bf16[2,256,336]{2,1,0:T(8,128)(2,1)} %pad_convert_fusion.table_ref), custom_call_target="tpu_custom_call" | custom-call | tf_op jit(solution)/shard_map/pallas_call | solution.py:45
  175.4 1.5 reshape.60
  176.9 0.6 copy_bitcast_fusion
  177.5 33.8 %gather_fusion.1 = bf16[10752,512]{1,0:T(8,128)(2,1)} fusion(bf16[4112,512]{1,0:T(8,128)(2,1)} %maximum_maximum_fusion, s32[11264]{0:T(1024)S(1)} %pad_clamp_fusion.2), kind=kCustom, calls=%fused_computation.1 | custom fusion | bytes 22063104 | tf_op jit(solution)/shard_map/gather | solution.py:216
  211.3 22.3 %shard_map.84 = f32[32,64,64]{2,1,0:T(8,128)} custom-call(bf16[336,336]{1,0:T(8,128)(2,1)} %pad.19.integ_ref, bf16[32,336,512]{2,1,0:T(8,128)(2,1)} %bitcast.50, bf16[2,336,256]{2,1,0:T(8,128)(2,1)} %pad.21.sign_ref, bf16[2,256,336]{2,1,0:T(8,128)(2,1)} %pad_convert_fusion.table_ref), custom_call_target="tpu_custom_call" | custom-call | tf_op jit(solution)/shard_map/pallas_call | solution.py:45
  233.7 1.5 reshape.59
  235.2 33.8 %gather_fusion = bf16[10752,512]{1,0:T(8,128)(2,1)} fusion(bf16[4112,512]{1,0:T(8,128)(2,1)} %maximum_maximum_fusion, s32[11264]{0:T(1024)S(1)} %pad_clamp_fusion.3), kind=kCustom, calls=%fused_computation | custom fusion | bytes 22063104 | tf_op jit(solution)/shard_map/gather | solution.py:216
  269.0 22.3 %shard_map.83 = f32[32,64,64]{2,1,0:T(8,128)} custom-call(bf16[336,336]{1,0:T(8,128)(2,1)} %pad.19.integ_ref, bf16[32,336,512]{2,1,0:T(8,128)(2,1)} %bitcast.47, bf16[2,336,256]{2,1,0:T(8,128)(2,1)} %pad.21.sign_ref, bf16[2,256,336]{2,1,0:T(8,128)(2,1)} %pad_convert_fusion.table_ref), custom_call_target="tpu_custom_call" | custom-call | tf_op jit(solution)/shard_map/pallas_call | solution.py:45
  291.3 1.5 reshape.58
  292.8 0.6 copy_bitcast_fusion.2
  293.4 1.5 pad_maximum_fusion.send_ref
  294.9 0.0 copy-start.2
  294.9 0.0 copy-start.3
  294.9 35.1 %shard_map.87 = f32[16,4,32,256]{3,2,1,0:T(8,128)} custom-call(f32[16,4,32,256]{3,2,1,0:T(8,128)} %pad_maximum_fusion.send_ref), custom_call_target="tpu_custom_call" | custom-call | tf_op jit(solution)/shard_map/pallas_call | solution.py:99
  330.0 1.8 reduce_sum.9
  331.8 0.0 copy-done.2
  331.8 0.0 copy-done.3
  331.9 0.8 fusion.1
  (9 shorter events, 0.1 us)
Async XLA Ops:
  52.5 7.4 %copy-start = (s32[324,2048]{1,0:T(8,128)S(1)}, s32[324,2048]{1,0:T(8,128)}, u32[]{:S(2)}) copy-start(s32[324,2048]{1,0:T(8,128)} %param.11) | copy-start | bytes 7962628
  52.5 7.4 %copy-start.1 = (s32[324,2048]{1,0:T(8,128)S(1)}, s32[324,2048]{1,0:T(8,128)}, u32[]{:S(2)}) copy-start(s32[324,2048]{1,0:T(8,128)} %param.12) | copy-start | bytes 7962628
  294.9 36.9 %copy-start.2 = (bf16[256,256]{1,0:T(8,128)(2,1)S(1)}, bf16[256,256]{1,0:T(8,128)(2,1)}, u32[]{:S(2)}) copy-start(bf16[256,256]{1,0:T(8,128)(2,1)} %own_ref.1) | copy-start | bytes 393220
  294.9 36.9 %copy-start.3 = (f32[256,256]{1,0:T(8,128)S(1)}, f32[256,256]{1,0:T(8,128)}, u32[]{:S(2)}) copy-start(f32[256,256]{1,0:T(8,128)} %param.9) | copy-start | bytes 786436

commit v9 on v8

--- a/solution.py
+++ b/solution.py
@@ -154,6 +154,51 @@
     )(own)
 
 
+def gather_alpha_kernel(own_ref, out_ref, send_sem, recv_sem, local_sem):
+    count = lax.axis_size("alpha")
+    group = lax.axis_index("g")
+    member = lax.axis_index("m")
+    me = lax.axis_index("alpha")
+
+    def remote(slot, sem_slot, peer):
+        return pltpu.make_async_remote_copy(
+            src_ref=own_ref,
+            dst_ref=out_ref.at[slot],
+            send_sem=send_sem.at[sem_slot],
+            recv_sem=recv_sem.at[slot],
+            device_id=(peer, group, member),
+            device_id_type=pl.DeviceIdType.MESH,
+        )
+
+    for step in range(1, count):
+        dest = lax.rem(me + step, count)
+        remote(me, dest, dest).start()
+    local = pltpu.make_async_copy(own_ref, out_ref.at[me], local_sem)
+    local.start()
+    local.wait()
+    for step in range(1, count):
+        dest = lax.rem(me + step, count)
+        remote(me, dest, dest).wait_send()
+    for step in range(1, count):
+        src = lax.rem(me + count - step, count)
+        remote(src, src, src).wait_recv()
+
+
+def gather_alpha(own, count):
+    return pl.pallas_call(
+        gather_alpha_kernel,
+        out_shape=jax.ShapeDtypeStruct((count,) + own.shape, own.dtype),
+        in_specs=[pl.BlockSpec(memory_space=pl.ANY)],
+        out_specs=pl.BlockSpec(memory_space=pl.ANY),
+        scratch_shapes=[
+            pltpu.SemaphoreType.DMA((count,)),
+            pltpu.SemaphoreType.DMA((count,)),
+            pltpu.SemaphoreType.DMA,
+        ],
+        compiler_params=pltpu.CompilerParams(has_side_effects=True),
+    )(own)
+
+
 def on_device(
     coefficients, diagonal, integrals, alpha_row, alpha_sign, beta_block, beta_sign, block_irrep
 ):
@@ -209,9 +254,24 @@
         offset_dims=(2,), collapsed_slice_dims=(0,), start_index_map=(0,)
     )
 
-    parts = []
-    for local_blk in range(per_device):
-        first_row = (alpha_rank * per_device + local_blk) * block_len + member * sub_rows
+    block_count = live_flags.shape[0]
+    block_iota = jnp.arange(block_count, dtype=jnp.int32)
+    live_rank = jnp.cumsum(live_flags) - live_flags
+    live_total = jnp.sum(live_flags)
+    block_of_rank = jnp.sum(
+        jnp.where(
+            (live_flags[None, :] == 1) & (live_rank[None, :] == block_iota[:, None]),
+            block_iota[None, :],
+            0,
+        ),
+        axis=1,
+    )
+    my_count = jnp.maximum(live_total - alpha_rank + alpha_size - 1, 0) // alpha_size
+    beta_size = total_blocks // src_blocks
+
+    def one_block(slot, buffer):
+        block_id = block_of_rank[slot * alpha_size + alpha_rank]
+        first_row = block_id * block_len + member * sub_rows
         row_ids = lax.dynamic_slice_in_dim(row_ext, first_row, sub_rows, 0)
         picked = lax.gather(
             coeff_ext,
@@ -221,14 +281,21 @@
             mode=lax.GatherScatterMode.PROMISE_IN_BOUNDS,
         )
         summed = mix_block(integ_pad, picked, sign_q, table_all, total_blocks, block_len)
-        parts.append(
-            summed.reshape(sub_rows, total_blocks // src_blocks, local_cols).transpose(1, 0, 2)
-        )
-    send = jnp.stack(parts, axis=1)
+        part = summed.reshape(sub_rows, beta_size, local_cols).transpose(1, 0, 2)
+        return lax.dynamic_update_slice(buffer, part[:, None], (0, slot, 0, 0))
+
+    empty = jnp.zeros((beta_size, per_device, sub_rows, local_cols), jnp.float32)
+    send = lax.fori_loop(0, my_count, one_block, empty)
     recv = exchange(send)
     groups = recv.shape[0] // PAIR
     recv = recv.reshape(groups, PAIR, per_device, sub_rows, local_cols).sum(axis=0)
-    placed = recv.transpose(1, 0, 2, 3).reshape(local_rows, local_cols)
+    done = recv.transpose(1, 0, 2, 3).reshape(per_device, block_len, local_cols)
+    everyone = gather_alpha(done, alpha_size).reshape(
+        alpha_size * per_device, block_len, local_cols
+    )
+    own_rank = lax.dynamic_slice_in_dim(live_rank, alpha_rank * per_device, per_device, 0)
+    pick = (own_rank % alpha_size) * per_device + jnp.minimum(own_rank // alpha_size, per_device - 1)
+    placed = everyone[pick].reshape(local_rows, local_cols)
     own_live_rows = jnp.repeat(own_flags, block_len)
     total = diagonal * coefficients.astype(jnp.float32) + placed
     return jnp.where(own_live_rows[:, None] == 1, total, jnp.zeros_like(total))

time: 338 us -> 273 us (0.81); the launches traced: 333 us -> 273 us
  local copies, waits for them, and re-layouts: 152 us -> 93.8 us
  Pallas kernels: 161 us -> 157 us
    gather x4 -> x3, local copies, waits for them, and re-layouts: 135 us -> 69.7 us  [the longest x2 67.6 us: one_block(): lax.gather(coeff_ext, row_ids[:, :, None], dims, slice_sizes=(1, wide_col...]
    pallas_call x4 -> x2, Pallas kernels: 89.4 us -> 44.3 us  [mix_block(): pl.pallas_call(mix_kernel, out_shape=jax.ShapeDtypeStruct((rows, targets,...]
    pallas_call x0 -> x1, Pallas kernels: none -> 39.6 us  [gather_alpha(): pl.pallas_call(gather_alpha_kernel, out_shape=jax.ShapeDtypeStruct((count...]
    unnamed x10 -> x21, local copies, waits for them, and re-layouts: 0.56 us -> 6.53 us
where the time goes in v9:
time: 273 us
  Pallas kernels  157 us (58%)
  local copies, waits for them, and re-layouts  93.8 us (34%)
  other arithmetic  15.8 us (6%)
  blocking collectives  4.21 us (2%)
    gather x2, local copies, waits for them, and re-layouts, one_block(): lax.gather(coeff_ext, row_ids[:, :, None], dims, slice_sizes=(1, wide_col...  67.6 us
    pallas_call x2, Pallas kernels, mix_block(): pl.pallas_call(mix_kernel, out_shape=jax.ShapeDtypeStruct((rows, targets,...  44.3 us
    pallas_call x1, Pallas kernels, gather_alpha(): pl.pallas_call(gather_alpha_kernel, out_shape=jax.ShapeDtypeStruct((count...  39.6 us
    pallas_call x1, Pallas kernels, spread(): pl.pallas_call(spread_kernel, out_shape=jax.ShapeDtypeStruct((count,) + o...  37.6 us
    pallas_call x1, Pallas kernels, exchange(): pl.pallas_call(exchange_kernel, out_shape=jax.ShapeDtypeStruct(send.shape...  35.2 us
    concatenate x1, other arithmetic, on_device(): jnp.concatenate([gathered, -gathered, jnp.zeros((16, wide_cols), jnp.bflo...  7.18 us
    unnamed x21, local copies, waits for them, and re-layouts  6.53 us

profile of v9, /device:TPU:1, one launch (start us, length us, event | category | flops | bytes accessed | tf_op | source)
XLA Modules:
  0.0 272.6 jit_solution(11160629892797223474)
XLA Ops:
  0.0 1.1 compare_convert_fusion
  1.1 0.1 copy.36
  1.2 0.1 reduce-window.9
  1.3 0.1 reduce
  1.4 1.3 fusion.6
  3.4 0.1 broadcast_in_dim.64
  3.4 0.1 convert_element_type.28
  3.5 37.6 %shard_map.82 = bf16[16,256,256]{2,1,0:T(8,128)(2,1)} custom-call(bf16[256,256]{1,0:T(8,128)(2,1)} %own_ref.1), custom_call_target="tpu_custom_call" | custom-call | tf_op jit(solution)/shard_map/pallas_call | solution.py:143
  41.2 3.7 %copy.41 = bf16[8,256,2,256]{3,2,1,0:T(2,128)(2,1)S(1)} copy(bf16[8,256,2,256]{3,1,2,0:T(8,128)(2,1)} %bitcast.40) | data formatting | bytes 4194304 | tf_op jit(solution)/shard_map/transpose | solution.py:221
  44.9 0.5 copy.50
  45.5 0.3 fusion.9
  45.8 7.2 %maximum_maximum_fusion = bf16[4112,512]{1,0:T(8,128)(2,1)} fusion(bf16[2048,512]{1,0:T(8,128)(2,1)S(1)} %get-tuple-element.188, bf16[2048,512]{1,0:T(8,128)(2,1)S(1)} %get-tuple-element.189, bf16[4112]{0:T(1024)(128)(2,1)S(1)} %pad.27.clone), kind=kLoop, calls=%fused_computation.6 | loop fusion | flops 12632064 | bytes 8413216 | tf_op jit(solution)/shard_map/concatenate | solution.py:226
  53.0 0.0 copy-done.6
  53.0 0.1 select_reduce_fusion
  53.1 2.3 copy.37
  55.4 3.5 %copy.39 = s32[324,2048]{0,1:T(8,128)} copy(s32[324,2048]{1,0:T(8,128)} %param.13) | data formatting | bytes 5308416 | tf_op args[3]
  58.9 2.4 fusion
  61.3 0.0 copy-start.1
  61.3 1.8 pad_bitcast_fusion
  63.2 0.0 copy-done.1
  63.2 2.4 all-gather
  65.6 0.1 convert.10
  65.7 0.0 copy-start.3
  65.7 0.4 reshape.88
  66.1 0.3 copy.42
  66.4 0.2 copy.49
  66.7 0.0 copy-done.4
  66.7 1.8 all-gather.1
  68.5 0.1 eq.80
  68.6 0.1 eq.78
  68.6 0.2 bitcast_compare_fusion
  68.8 0.1 pad_convert_fusion
  68.9 0.0 copy-done.3
  68.9 1.6 broadcast_in_dim.60.clone
  70.5 121.3 %while.12 = (s32[]{:T(128)}, f32[16,4,32,256]{3,2,1,0:T(8,128)}, s32[]{:T(128)}, s32[]{:T(128)}, s32[32]{0:T(128)S(1)}, /*index=5*/s32[]{:T(128)}, s32[2048,336]...) while((s32[]{:T(128)}, f32[16,4,32,256]{3,2,1,0:T(8,128)}, ...), condition=%wide.region_4.5_spmd, body=%wide.region_3.4_spmd.sunk | while | flops 11279 | bytes 24420688 | solution.py:288
  70.5 0.6 dynamic_slice.24
  71.7 0.8 constant_dynamic-slice_fusion.2
  72.5 0.1 reshape.126
  72.6 33.8 %gather_fusion = bf16[10752,512]{1,0:T(8,128)(2,1)} fusion(bf16[4112,512]{1,0:T(8,128)(2,1)} %get-tuple-element.307, s32[11264]{0:T(1024)S(1)} %pad_clamp_fusion.3), kind=kCustom, calls=%fused_computation.clone.1 | custom fusion | bytes 22063104 | tf_op jit(solution)/shard_map/while/body/gather | solution.py:276
  106.4 22.1 %body.3 = f32[32,64,64]{2,1,0:T(8,128)} custom-call(bf16[336,336]{1,0:T(8,128)(2,1)S(1)} %get-tuple-element.308.integ_ref, bf16[32,336,512]{2,1,0:T(8,128)(2,1)} %bitcast.36, bf16[2,336,256]{2,1,0:T(8,128)(2,1)S(1)} %get-tuple-element.309.sign_ref, bf16[2,256,336]{2,1,0:T(8,128)(2,1)S(1)} %get-tuple-element.310.table_ref), custom_call_target="tpu_custom_call" | custom-call | tf_op jit(solution)/shard_map/while/body/pallas_call | solution.py:45
  128.5 1.5 reshape.127
  130.0 1.1 copy_dynamic-update-slice_fusion.2
  131.2 0.6 dynamic_slice.24
  132.3 0.8 constant_dynamic-slice_fusion.2
  133.1 0.1 reshape.126
  133.3 33.8 %gather_fusion = bf16[10752,512]{1,0:T(8,128)(2,1)} fusion(bf16[4112,512]{1,0:T(8,128)(2,1)} %get-tuple-element.307, s32[11264]{0:T(1024)S(1)} %pad_clamp_fusion.3), kind=kCustom, calls=%fused_computation.clone.1 | custom fusion | bytes 22063104 | tf_op jit(solution)/shard_map/while/body/gather | solution.py:276
  167.0 22.1 %body.3 = f32[32,64,64]{2,1,0:T(8,128)} custom-call(bf16[336,336]{1,0:T(8,128)(2,1)S(1)} %get-tuple-element.308.integ_ref, bf16[32,336,512]{2,1,0:T(8,128)(2,1)} %bitcast.36, bf16[2,336,256]{2,1,0:T(8,128)(2,1)S(1)} %get-tuple-element.309.sign_ref, bf16[2,256,336]{2,1,0:T(8,128)(2,1)S(1)} %get-tuple-element.310.table_ref), custom_call_target="tpu_custom_call" | custom-call | tf_op jit(solution)/shard_map/while/body/pallas_call | solution.py:45
  189.2 1.5 reshape.127
  190.7 1.1 copy_dynamic-update-slice_fusion.2
  191.8 35.2 %shard_map.83 = f32[16,4,32,256]{3,2,1,0:T(8,128)} custom-call(f32[16,4,32,256]{3,2,1,0:T(8,128)} %get-tuple-element.132.send_ref), custom_call_target="tpu_custom_call" | custom-call | tf_op jit(solution)/shard_map/pallas_call | solution.py:99
  227.0 0.0 copy-start.7
  227.0 0.0 copy-start.5
  227.0 0.0 copy-start
  227.0 0.0 copy-start.2
  227.1 1.8 reduce_sum.29
  228.9 0.7 copy.45
  229.6 39.6 %shard_map.84 = f32[8,4,64,256]{3,2,1,0:T(8,128)} custom-call(f32[4,64,256]{2,1,0:T(8,128)} %bitcast.47), custom_call_target="tpu_custom_call" | custom-call | tf_op jit(solution)/shard_map/pallas_call | solution.py:188
  269.2 0.1 compare_select_fusion
  269.3 2.2 gather_fusion.1
  271.5 0.1 dynamic-slice_compare_fusion
  271.6 0.1 broadcast_in_dim.58
  271.7 0.1 eq.70
  271.8 0.0 copy-done.2
  271.8 0.8 fusion.1
  (14 shorter events, 0.1 us)
Async XLA Ops:
  2.7 50.3 %copy-start.6 = (s32[32]{0:T(128)}, s32[32]{0:T(128)S(1)}, u32[]{:S(2)}) copy-start(s32[32]{0:T(128)S(1)} %get-tuple-element.194) | copy-start | bytes 388
  61.3 1.9 copy-start.1
  63.2 3.5 %copy-start.4 = (s32[4,324]{1,0:T(4,128)S(1)}, s32[4,324]{1,0:T(4,128)}, u32[]{:S(2)}) copy-start(s32[4,324]{1,0:T(4,128)} %param.15) | copy-start | bytes 15556
  65.7 3.2 %copy-start.3 = (bf16[324,324]{1,0:T(8,128)(2,1)S(1)}, bf16[324,324]{1,0:T(8,128)(2,1)}, u32[]{:S(2)}) copy-start(bf16[324,324]{1,0:T(8,128)(2,1)} %param.12) | copy-start | bytes 629860
  227.0 42.2 %copy-start.7 = (s32[32]{0:T(128)S(1)}, s32[32]{0:T(128)}, u32[]{:S(2)}) copy-start(s32[32]{0:T(128)} %copy-done.6) | copy-start | bytes 388
  227.0 44.5 %copy-start.5 = (s32[32]{0:T(128)S(1)}, s32[32]{0:T(128)}, u32[]{:S(2)}) copy-start(s32[32]{0:T(128)} %get-tuple-element.190) | copy-start | bytes 388
  227.0 44.7 %copy-start = (bf16[256,256]{1,0:T(8,128)(2,1)S(1)}, bf16[256,256]{1,0:T(8,128)(2,1)}, u32[]{:S(2)}) copy-start(bf16[256,256]{1,0:T(8,128)(2,1)} %own_ref.1) | copy-start | bytes 393220
  227.0 44.7 %copy-start.2 = (f32[256,256]{1,0:T(8,128)S(1)}, f32[256,256]{1,0:T(8,128)}, u32[]{:S(2)}) copy-start(f32[256,256]{1,0:T(8,128)} %param.11) | copy-start | bytes 786436

commit v10 on v9

--- a/solution.py
+++ b/solution.py
@@ -230,7 +230,7 @@
     row_ext = jnp.where(
         alpha_sign == 0, zero_row, jnp.where(alpha_sign < 0, alpha_row + window_rows, alpha_row)
     )
-    row_ext = jnp.pad(row_ext, ((0, extra), (0, 0)), constant_values=zero_row).T
+    row_ext = jnp.pad(row_ext, ((0, extra), (0, 0)), constant_values=zero_row)
 
     integ_pad = jnp.pad(integrals, ((0, extra), (0, extra)))
     beta_block2 = lax.all_gather(beta_block, "m", axis=0, tiled=True)
@@ -256,23 +256,32 @@
 
     block_count = live_flags.shape[0]
     block_iota = jnp.arange(block_count, dtype=jnp.int32)
-    live_rank = jnp.cumsum(live_flags) - live_flags
-    live_total = jnp.sum(live_flags)
-    block_of_rank = jnp.sum(
+    in_group = jnp.cumsum(live_flags.reshape(-1, per_device), axis=1).reshape(-1)
+    is_first = (live_flags == 1) & (in_group == 1)
+    is_extra = ((live_flags == 1) & jnp.logical_not(is_first)).astype(jnp.int32)
+    extra_rank = jnp.cumsum(is_extra) - is_extra
+    extra_total = jnp.sum(is_extra)
+    block_of_extra = jnp.sum(
         jnp.where(
-            (live_flags[None, :] == 1) & (live_rank[None, :] == block_iota[:, None]),
+            (is_extra[None, :] == 1) & (extra_rank[None, :] == block_iota[:, None]),
             block_iota[None, :],
             0,
         ),
         axis=1,
     )
-    my_count = jnp.maximum(live_total - alpha_rank + alpha_size - 1, 0) // alpha_size
+    own_first = lax.dynamic_slice_in_dim(is_first, alpha_rank * per_device, per_device, 0)
+    first_blk = alpha_rank * per_device + jnp.argmax(own_first).astype(jnp.int32)
+    my_count = 1 + jnp.maximum(extra_total - alpha_rank + alpha_size - 1, 0) // alpha_size
     beta_size = total_blocks // src_blocks
 
     def one_block(slot, buffer):
-        block_id = block_of_rank[slot * alpha_size + alpha_rank]
+        block_id = jnp.where(
+            slot == 0,
+            first_blk,
+            block_of_extra[jnp.maximum(slot - 1, 0) * alpha_size + alpha_rank],
+        )
         first_row = block_id * block_len + member * sub_rows
-        row_ids = lax.dynamic_slice_in_dim(row_ext, first_row, sub_rows, 0)
+        row_ids = lax.dynamic_slice_in_dim(row_ext, first_row, sub_rows, 1).T
         picked = lax.gather(
             coeff_ext,
             row_ids[:, :, None],
@@ -290,12 +299,15 @@
     groups = recv.shape[0] // PAIR
     recv = recv.reshape(groups, PAIR, per_device, sub_rows, local_cols).sum(axis=0)
     done = recv.transpose(1, 0, 2, 3).reshape(per_device, block_len, local_cols)
-    everyone = gather_alpha(done, alpha_size).reshape(
-        alpha_size * per_device, block_len, local_cols
-    )
-    own_rank = lax.dynamic_slice_in_dim(live_rank, alpha_rank * per_device, per_device, 0)
-    pick = (own_rank % alpha_size) * per_device + jnp.minimum(own_rank // alpha_size, per_device - 1)
-    placed = everyone[pick].reshape(local_rows, local_cols)
+    everyone = gather_alpha(done[1:], alpha_size).reshape(
+        alpha_size * (per_device - 1), block_len, local_cols
+    )
+    own_rank = lax.dynamic_slice_in_dim(extra_rank, alpha_rank * per_device, per_device, 0)
+    pick = (own_rank % alpha_size) * (per_device - 1) + jnp.minimum(
+        own_rank // alpha_size, per_device - 2
+    )
+    placed = jnp.where(own_first[:, None, None], done[0][None], everyone[pick])
+    placed = placed.reshape(local_rows, local_cols)
     own_live_rows = jnp.repeat(own_flags, block_len)
     total = diagonal * coefficients.astype(jnp.float32) + placed
     return jnp.where(own_live_rows[:, None] == 1, total, jnp.zeros_like(total))

time: 273 us -> 270 us (0.989)
  Pallas kernels: 157 us -> 151 us
    pallas_call x1, Pallas kernels: 39.6 us -> 34 us  [gather_alpha(): pl.pallas_call(gather_alpha_kernel, out_shape=jax.ShapeDtypeStruct((count...]
    unnamed x21 -> x27, local copies, waits for them, and re-layouts: 6.53 us -> 7.01 us
where the time goes in v10:
time: 270 us; the launch traced here: 269 us
  Pallas kernels  151 us (56%)
  local copies, waits for them, and re-layouts  94.5 us (35%)
  other arithmetic  16.3 us (6%)
  blocking collectives  4.21 us (2%)
    gather x2, local copies, waits for them, and re-layouts, one_block(): lax.gather(coeff_ext, row_ids[:, :, None], dims, slice_sizes=(1, wide_col...  67.6 us
    pallas_call x2, Pallas kernels, mix_block(): pl.pallas_call(mix_kernel, out_shape=jax.ShapeDtypeStruct((rows, targets,...  44.3 us
    pallas_call x1, Pallas kernels, spread(): pl.pallas_call(spread_kernel, out_shape=jax.ShapeDtypeStruct((count,) + o...  37.6 us
    pallas_call x1, Pallas kernels, exchange(): pl.pallas_call(exchange_kernel, out_shape=jax.ShapeDtypeStruct(send.shape...  35.2 us
    pallas_call x1, Pallas kernels, gather_alpha(): pl.pallas_call(gather_alpha_kernel, out_shape=jax.ShapeDtypeStruct((count...  34 us
    concatenate x1, other arithmetic, on_device(): jnp.concatenate([gathered, -gathered, jnp.zeros((16, wide_cols), jnp.bflo...  7.18 us
    unnamed x27, local copies, waits for them, and re-layouts  7.01 us

profile of v10, /device:TPU:1, one launch (start us, length us, event | category | flops | bytes accessed | tf_op | source)
XLA Modules:
  0.0 269.0 jit_solution(14397883659416847011)
XLA Ops:
  0.0 0.7 compare_convert_fusion
  0.7 0.5 copy-done.7
  1.1 0.1 reshape.92
  1.2 0.2 reduce_window_sum.18
  1.4 0.1 eq.89
  1.5 0.7 broadcast_compare_fusion.1
  2.1 0.1 copy.32
  2.2 0.1 reduce-window.9
  2.3 0.1 reduce.18
  2.4 0.6 fusion.8
  3.7 0.8 iota_reduce_fusion
  5.2 0.1 select_reduce_fusion
  5.3 0.1 broadcast_in_dim.94
  5.4 0.1 convert_element_type.32
  5.5 37.6 %shard_map.82 = bf16[16,256,256]{2,1,0:T(8,128)(2,1)} custom-call(bf16[256,256]{1,0:T(8,128)(2,1)} %own_ref.1), custom_call_target="tpu_custom_call" | custom-call | tf_op jit(solution)/shard_map/pallas_call | solution.py:143
  43.1 3.7 %copy.37 = bf16[8,256,2,256]{3,2,1,0:T(2,128)(2,1)S(1)} copy(bf16[8,256,2,256]{3,1,2,0:T(8,128)(2,1)} %bitcast.46) | data formatting | bytes 4194304 | tf_op jit(solution)/shard_map/transpose | solution.py:221
  46.9 0.5 copy.46
  47.5 0.3 fusion.7
  47.8 7.2 %maximum_maximum_fusion = bf16[4112,512]{1,0:T(8,128)(2,1)} fusion(bf16[2048,512]{1,0:T(8,128)(2,1)S(1)} %get-tuple-element.219, bf16[2048,512]{1,0:T(8,128)(2,1)S(1)} %get-tuple-element.220, bf16[4112]{0:T(1024)(128)(2,1)S(1)} %pad.27.clone), kind=kLoop, calls=%fused_computation.6 | loop fusion | flops 12632064 | bytes 8413216 | tf_op jit(solution)/shard_map/concatenate | solution.py:226
  55.0 2.3 copy.33
  57.3 3.5 %copy.35 = s32[324,2048]{0,1:T(8,128)} copy(s32[324,2048]{1,0:T(8,128)} %param.13) | data formatting | bytes 5308416 | tf_op args[3]
  60.8 2.4 fusion
  63.2 0.0 copy-start.1
  63.2 1.8 pad.20
  65.0 2.4 all-gather
  67.4 0.1 convert.10
  67.6 0.4 reshape.97
  68.0 0.3 copy.38
  68.3 0.2 copy.45
  68.5 1.8 all-gather.1
  70.4 0.1 eq.98
  70.4 0.1 eq.96
  70.5 0.2 bitcast_compare_fusion
  70.7 0.1 pad_convert_fusion
  70.8 1.6 broadcast_in_dim.90.clone
  72.4 121.3 %while.12 = (s32[]{:T(128)}, f32[16,4,32,256]{3,2,1,0:T(8,128)}, s32[]{:T(128)}, s32[]{:T(128)}, s32[32]{0:T(128)S(1)}, /*index=5*/s32[]{:T(128)}, s32[]{:T(128)...) while((s32[]{:T(128)}, f32[16,4,32,256]{3,2,1,0:T(8,128)}, ...), condition=%wide.region_6.7_spmd, body=%wide.region_5.6_spmd.sunk | while | flops 11283 | bytes 24420748 | solution.py:297
  72.4 0.6 dynamic_slice.31
  73.5 0.8 dynamic-slice_bitcast_fusion.2
  74.4 0.1 reshape.133
  74.5 33.8 %gather_fusion = bf16[10752,512]{1,0:T(8,128)(2,1)} fusion(bf16[4112,512]{1,0:T(8,128)(2,1)} %get-tuple-element.349, s32[11264]{0:T(1024)S(1)} %pad_clamp_fusion.3), kind=kCustom, calls=%fused_computation.clone.1 | custom fusion | bytes 22063104 | tf_op jit(solution)/shard_map/while/body/gather | solution.py:285
  108.3 22.1 %body.4 = f32[32,64,64]{2,1,0:T(8,128)} custom-call(bf16[336,336]{1,0:T(8,128)(2,1)S(1)} %get-tuple-element.350.integ_ref, bf16[32,336,512]{2,1,0:T(8,128)(2,1)} %bitcast.42, bf16[2,336,256]{2,1,0:T(8,128)(2,1)S(1)} %get-tuple-element.351.sign_ref, bf16[2,256,336]{2,1,0:T(8,128)(2,1)S(1)} %get-tuple-element.352.table_ref), custom_call_target="tpu_custom_call" | custom-call | tf_op jit(solution)/shard_map/while/body/pallas_call | solution.py:45
  130.4 1.5 reshape.134
  131.9 1.1 copy_dynamic-update-slice_fusion.2
  133.1 0.6 dynamic_slice.31
  134.2 0.8 dynamic-slice_bitcast_fusion.2
  135.0 0.1 reshape.133
  135.1 33.8 %gather_fusion = bf16[10752,512]{1,0:T(8,128)(2,1)} fusion(bf16[4112,512]{1,0:T(8,128)(2,1)} %get-tuple-element.349, s32[11264]{0:T(1024)S(1)} %pad_clamp_fusion.3), kind=kCustom, calls=%fused_computation.clone.1 | custom fusion | bytes 22063104 | tf_op jit(solution)/shard_map/while/body/gather | solution.py:285
  168.9 22.1 %body.4 = f32[32,64,64]{2,1,0:T(8,128)} custom-call(bf16[336,336]{1,0:T(8,128)(2,1)S(1)} %get-tuple-element.350.integ_ref, bf16[32,336,512]{2,1,0:T(8,128)(2,1)} %bitcast.42, bf16[2,336,256]{2,1,0:T(8,128)(2,1)S(1)} %get-tuple-element.351.sign_ref, bf16[2,256,336]{2,1,0:T(8,128)(2,1)S(1)} %get-tuple-element.352.table_ref), custom_call_target="tpu_custom_call" | custom-call | tf_op jit(solution)/shard_map/while/body/pallas_call | solution.py:45
  191.1 1.5 reshape.134
  192.6 1.1 copy_dynamic-update-slice_fusion.2
  193.7 35.2 %shard_map.83 = f32[16,4,32,256]{3,2,1,0:T(8,128)} custom-call(f32[16,4,32,256]{3,2,1,0:T(8,128)} %get-tuple-element.158.send_ref), custom_call_target="tpu_custom_call" | custom-call | tf_op jit(solution)/shard_map/pallas_call | solution.py:99
  228.9 0.0 copy-start
  229.0 1.8 reduce_sum.29
  230.8 0.7 copy.41
  231.5 34.0 %shard_map.84 = f32[8,3,64,256]{3,2,1,0:T(8,128)} custom-call(f32[3,64,256]{2,1,0:T(8,128)} %bitcast.54), custom_call_target="tpu_custom_call" | custom-call | tf_op jit(solution)/shard_map/pallas_call | solution.py:188
  265.5 0.1 compare_select_fusion
  265.6 2.0 gather_fusion.1
  267.6 0.1 dynamic_slice.22
  267.7 0.1 broadcast_in_dim.87
  267.8 0.1 broadcast_in_dim.88
  267.9 0.1 dynamic-slice_compare_fusion
  267.9 0.1 broadcast_in_dim.85
  268.0 0.1 eq.86
  268.1 0.8 fusion.2
  (31 shorter events, 0.2 us)
Async XLA Ops:
  0.7 0.5 copy-start.7
  2.1 44.8 %copy-start.5 = (pred[32]{0:T(512)(128)(4,1)}, pred[32]{0:T(512)(128)(4,1)S(1)}, u32[]{:S(2)}) copy-start(pred[32]{0:T(512)(128)(4,1)S(1)} %get-tuple-element.223) | copy-start | bytes 100
  3.0 43.9 %copy-start.9 = (s32[32]{0:T(128)}, s32[32]{0:T(128)S(1)}, u32[]{:S(2)}) copy-start(s32[32]{0:T(128)S(1)} %get-tuple-element.225) | copy-start | bytes 388
  63.2 1.9 copy-start.1
  65.0 3.5 %copy-start.4 = (s32[4,324]{1,0:T(4,128)S(1)}, s32[4,324]{1,0:T(4,128)}, u32[]{:S(2)}) copy-start(s32[4,324]{1,0:T(4,128)} %param.15) | copy-start | bytes 15556
  67.6 3.2 %copy-start.3 = (bf16[324,324]{1,0:T(8,128)(2,1)S(1)}, bf16[324,324]{1,0:T(8,128)(2,1)}, u32[]{:S(2)}) copy-start(bf16[324,324]{1,0:T(8,128)(2,1)} %param.12) | copy-start | bytes 629860
  228.9 36.6 %copy-start.10 = (s32[32]{0:T(128)S(1)}, s32[32]{0:T(128)}, u32[]{:S(2)}) copy-start(s32[32]{0:T(128)} %copy-done.9) | copy-start | bytes 388
  228.9 38.7 %copy-start.6 = (pred[32]{0:T(512)(128)(4,1)S(1)}, pred[32]{0:T(512)(128)(4,1)}, u32[]{:S(2)}) copy-start(pred[32]{0:T(512)(128)(4,1)} %copy-done.5) | copy-start | bytes 100
  228.9 38.9 %copy-start.8 = (s32[32]{0:T(128)S(1)}, s32[32]{0:T(128)}, u32[]{:S(2)}) copy-start(s32[32]{0:T(128)} %copy-done.7) | copy-start | bytes 388
  228.9 39.2 %copy-start = (bf16[256,256]{1,0:T(8,128)(2,1)S(1)}, bf16[256,256]{1,0:T(8,128)(2,1)}, u32[]{:S(2)}) copy-start(bf16[256,256]{1,0:T(8,128)(2,1)} %own_ref.1) | copy-start | bytes 393220
  228.9 39.2 %copy-start.2 = (f32[256,256]{1,0:T(8,128)S(1)}, f32[256,256]{1,0:T(8,128)}, u32[]{:S(2)}) copy-start(f32[256,256]{1,0:T(8,128)} %param.11) | copy-start | bytes 786436

commit v11 on v10

--- a/solution.py
+++ b/solution.py
@@ -112,13 +112,17 @@
 
 def spread_kernel(own_ref, out_ref, send_sem, recv_sem, local_sem):
     count = lax.axis_size("alpha") * PAIR
+    rows, cols = own_ref.shape
     group = lax.axis_index("g")
     me = lax.axis_index("alpha") * PAIR + lax.axis_index("m")
+
+    def window(slot):
+        return out_ref.at[pl.ds((slot // PAIR) * rows, rows), pl.ds((slot % PAIR) * cols, cols)]
 
     def remote(slot, sem_slot, peer):
         return pltpu.make_async_remote_copy(
             src_ref=own_ref,
-            dst_ref=out_ref.at[slot],
+            dst_ref=window(slot),
             send_sem=send_sem.at[sem_slot],
             recv_sem=recv_sem.at[slot],
             device_id=(peer // PAIR, group, peer % PAIR),
@@ -128,7 +132,7 @@
     for step in range(1, count):
         dest = lax.rem(me + step, count)
         remote(me, dest, dest).start()
-    local = pltpu.make_async_copy(own_ref, out_ref.at[me], local_sem)
+    local = pltpu.make_async_copy(own_ref, window(me), local_sem)
     local.start()
     local.wait()
     for step in range(1, count):
@@ -142,7 +146,9 @@
 def spread(own, count):
     return pl.pallas_call(
         spread_kernel,
-        out_shape=jax.ShapeDtypeStruct((count,) + own.shape, own.dtype),
+        out_shape=jax.ShapeDtypeStruct(
+            (count // PAIR * own.shape[0], PAIR * own.shape[1]), own.dtype
+        ),
         in_specs=[pl.BlockSpec(memory_space=pl.ANY)],
         out_specs=pl.BlockSpec(memory_space=pl.ANY),
         scratch_shapes=[
@@ -215,10 +221,7 @@
     sub_rows = block_len // PAIR
 
     alpha_size = lax.axis_size("alpha")
-    gathered = spread(coefficients, alpha_size * PAIR).reshape(
-        alpha_size, PAIR, local_rows, local_cols
-    )
-    gathered = gathered.transpose(0, 2, 1, 3).reshape(alpha_size * local_rows, PAIR * local_cols)
+    gathered = spread(coefficients, alpha_size * PAIR)
     live_flags = (block_irrep == 0).astype(jnp.int32)
     live_rows = jnp.repeat(live_flags, block_len)
     gathered = gathered * live_rows[:, None].astype(jnp.bfloat16)
@@ -227,14 +230,11 @@
         [gathered, -gathered, jnp.zeros((16, wide_cols), jnp.bfloat16)], axis=0
     )
     zero_row = 2 * window_rows
-    row_ext = jnp.where(
-        alpha_sign == 0, zero_row, jnp.where(alpha_sign < 0, alpha_row + window_rows, alpha_row)
-    )
-    row_ext = jnp.pad(row_ext, ((0, extra), (0, 0)), constant_values=zero_row)
 
     integ_pad = jnp.pad(integrals, ((0, extra), (0, extra)))
-    beta_block2 = lax.all_gather(beta_block, "m", axis=0, tiled=True)
-    beta_sign2 = lax.all_gather(beta_sign, "m", axis=0, tiled=True)
+    beta_block2 = lax.all_gather(beta_block.astype(jnp.bfloat16), "m", axis=0, tiled=True)
+    beta_block2 = beta_block2.astype(jnp.int32)
+    beta_sign2 = lax.all_gather(beta_sign.astype(jnp.bfloat16), "m", axis=0, tiled=True)
     sign_q = (
         beta_sign2.reshape(PAIR, src_blocks, pair_count, block_len)
         .transpose(0, 2, 1, 3)
@@ -281,7 +281,14 @@
             block_of_extra[jnp.maximum(slot - 1, 0) * alpha_size + alpha_rank],
         )
         first_row = block_id * block_len + member * sub_rows
-        row_ids = lax.dynamic_slice_in_dim(row_ext, first_row, sub_rows, 1).T
+        rows_src = lax.dynamic_slice_in_dim(alpha_row, first_row, sub_rows, 1)
+        signs_src = lax.dynamic_slice_in_dim(alpha_sign, first_row, sub_rows, 1)
+        row_ids = jnp.where(
+            signs_src == 0,
+            zero_row,
+            jnp.where(signs_src < 0, rows_src + window_rows, rows_src),
+        )
+        row_ids = jnp.pad(row_ids, ((0, extra), (0, 0)), constant_values=zero_row).T
         picked = lax.gather(
             coeff_ext,
             row_ids[:, :, None],

time: 270 us -> 323 us (1.20)
  local copies, waits for them, and re-layouts: 94.5 us -> 124 us
  Pallas kernels: 151 us -> 172 us
    gather x2 -> x3, local copies, waits for them, and re-layouts: 67.6 us -> 101 us  [one_block(): lax.gather(coeff_ext, row_ids[:, :, None], dims, slice_sizes=(1, wide_col...]
    pallas_call x2 -> x3, Pallas kernels: 44.3 us -> 66.3 us  [mix_block(): pl.pallas_call(mix_kernel, out_shape=jax.ShapeDtypeStruct((rows, targets,...]
    unnamed x27 -> x25, local copies, waits for them, and re-layouts: 7.01 us -> 0.8 us
    while x0 -> x2, local copies, waits for them, and re-layouts: none -> 5.8 us  [on_device(): send = lax.fori_loop(0, my_count, one_block, empty)]
    transpose x3, local copies, waits for them, and re-layouts: 5.36 us -> 0.02 us  [one_block(): row_ids = jnp.pad(row_ids, ((0, extra), (0, 0)), constant_values=zero_row).T]
where the time goes in v11:
time: 323 us; the launch traced here: 322 us
  Pallas kernels  172 us (53%)
  local copies, waits for them, and re-layouts  124 us (38%)
  other arithmetic  18 us (6%)
  blocking collectives  3.83 us (1%)
    gather x3, local copies, waits for them, and re-layouts, one_block(): lax.gather(coeff_ext, row_ids[:, :, None], dims, slice_sizes=(1, wide_col...  101 us
    pallas_call x3, Pallas kernels, mix_block(): pl.pallas_call(mix_kernel, out_shape=jax.ShapeDtypeStruct((rows, targets,...  66.3 us
    pallas_call x1, Pallas kernels, spread(): pl.pallas_call(spread_kernel, out_shape=jax.ShapeDtypeStruct((count // PA...  37.6 us
    pallas_call x1, Pallas kernels, gather_alpha(): pl.pallas_call(gather_alpha_kernel, out_shape=jax.ShapeDtypeStruct((count...  34 us
    pallas_call x1, Pallas kernels, exchange(): pl.pallas_call(exchange_kernel, out_shape=jax.ShapeDtypeStruct(send.shape...  33.8 us
    concatenate x1, other arithmetic, on_device(): jnp.concatenate([gathered, -gathered, jnp.zeros((16, wide_cols), jnp.bflo...  7.18 us

profile of v11, /device:TPU:1, one launch (start us, length us, event | category | flops | bytes accessed | tf_op | source)
XLA Modules:
  0.0 321.8 jit_solution(9881076756906810939)
XLA Ops:
  0.0 0.7 compare_convert_fusion
  0.7 0.6 copy-done.8
  1.2 0.1 reshape.84
  1.3 0.2 reduce_window_sum.18
  1.5 0.1 eq.92
  1.6 0.7 broadcast_compare_fusion.1
  2.2 0.1 copy.25
  2.3 0.1 reduce-window.9
  2.4 0.1 reduce.18
  2.5 0.6 fusion.8
  3.8 0.8 iota_reduce_fusion
  5.3 0.1 select_reduce_fusion
  5.4 0.1 broadcast_in_dim.96
  5.5 0.1 convert_element_type.42
  5.6 37.6 %shard_map.82 = bf16[2048,512]{1,0:T(8,128)(2,1)} custom-call(bf16[256,256]{1,0:T(8,128)(2,1)} %own_ref.1), custom_call_target="tpu_custom_call" | custom-call | tf_op jit(solution)/shard_map/pallas_call | solution.py:147
  43.2 1.9 fusion.7
  45.2 7.2 %maximum_maximum_fusion = bf16[4112,512]{1,0:T(8,128)(2,1)} fusion(bf16[2048,512]{1,0:T(8,128)(2,1)S(1)} %get-tuple-element.236, bf16[2048,512]{1,0:T(8,128)(2,1)S(1)} %get-tuple-element.237, bf16[4112]{0:T(1024)(128)(2,1)S(1)} %pad.28.clone), kind=kLoop, calls=%fused_computation.7 | loop fusion | flops 12632064 | bytes 8413216 | tf_op jit(solution)/shard_map/concatenate | solution.py:229
  52.4 2.3 copy.27
  54.7 3.5 %copy.28 = s32[324,2048]{0,1:T(8,128)} copy(s32[324,2048]{1,0:T(8,128)} %param.13) | data formatting | bytes 5308416 | tf_op jit(solution)/shard_map/while | solution.py:304
  58.2 0.1 convert_bitcast_fusion
  58.3 2.0 all-gather
  60.3 0.4 reshape.87
  60.8 0.3 copy.26
  61.1 0.2 copy.35
  61.3 1.8 all-gather.1
  63.2 0.1 eq.98
  63.3 0.2 bitcast_compare_fusion
  63.5 0.1 pad_convert_fusion
  63.6 1.6 broadcast_in_dim.93.clone
  65.2 182.7 %while.12 = (s32[]{:T(128)}, f32[16,4,32,256]{3,2,1,0:T(8,128)}, s32[]{:T(128)}, s32[]{:T(128)}, s32[32]{0:T(128)S(1)}, /*index=5*/s32[]{:T(128)}, s32[]{:T(128)...) while((s32[]{:T(128)}, f32[16,4,32,256]{3,2,1,0:T(8,128)}, ...), condition=%wide.region_6.7_spmd, body=%wide.region_5.6_spmd.sunk | while | flops 63123 | bytes 24543636 | solution.py:304
  65.2 0.7 dynamic_slice.40
  66.6 0.8 fusion.10
  67.4 0.1 reshape.123
  67.6 33.8 %gather_fusion = bf16[10752,512]{1,0:T(8,128)(2,1)} fusion(bf16[4112,512]{1,0:T(8,128)(2,1)} %get-tuple-element.375, s32[11264]{0:T(1024)S(1)} %pad_clamp_fusion.3), kind=kCustom, calls=%fused_computation.clone.1 | custom fusion | bytes 22063104 | tf_op jit(solution)/shard_map/while/body/gather | solution.py:292
  101.3 22.1 %body.4 = f32[32,64,64]{2,1,0:T(8,128)} custom-call(bf16[336,336]{1,0:T(8,128)(2,1)S(1)} %get-tuple-element.376.integ_ref, bf16[32,336,512]{2,1,0:T(8,128)(2,1)} %bitcast.38, bf16[2,336,256]{2,1,0:T(8,128)(2,1)S(1)} %get-tuple-element.377.sign_ref, bf16[2,256,336]{2,1,0:T(8,128)(2,1)S(1)} %get-tuple-element.378.table_ref), custom_call_target="tpu_custom_call" | custom-call | tf_op jit(solution)/shard_map/while/body/pallas_call | solution.py:45
  123.5 1.5 reshape.124
  125.0 1.1 copy_dynamic-update-slice_fusion.2
  126.1 0.7 dynamic_slice.40
  127.5 0.8 fusion.10
  128.3 0.1 reshape.123
  128.5 33.8 %gather_fusion = bf16[10752,512]{1,0:T(8,128)(2,1)} fusion(bf16[4112,512]{1,0:T(8,128)(2,1)} %get-tuple-element.375, s32[11264]{0:T(1024)S(1)} %pad_clamp_fusion.3), kind=kCustom, calls=%fused_computation.clone.1 | custom fusion | bytes 22063104 | tf_op jit(solution)/shard_map/while/body/gather | solution.py:292
  162.2 22.1 %body.4 = f32[32,64,64]{2,1,0:T(8,128)} custom-call(bf16[336,336]{1,0:T(8,128)(2,1)S(1)} %get-tuple-element.376.integ_ref, bf16[32,336,512]{2,1,0:T(8,128)(2,1)} %bitcast.38, bf16[2,336,256]{2,1,0:T(8,128)(2,1)S(1)} %get-tuple-element.377.sign_ref, bf16[2,256,336]{2,1,0:T(8,128)(2,1)S(1)} %get-tuple-element.378.table_ref), custom_call_target="tpu_custom_call" | custom-call | tf_op jit(solution)/shard_map/while/body/pallas_call | solution.py:45
  184.4 1.5 reshape.124
  185.9 1.1 copy_dynamic-update-slice_fusion.2
  187.0 0.7 dynamic_slice.40
  188.4 0.8 fusion.10
  189.2 0.1 reshape.123
  189.3 33.8 %gather_fusion = bf16[10752,512]{1,0:T(8,128)(2,1)} fusion(bf16[4112,512]{1,0:T(8,128)(2,1)} %get-tuple-element.375, s32[11264]{0:T(1024)S(1)} %pad_clamp_fusion.3), kind=kCustom, calls=%fused_computation.clone.1 | custom fusion | bytes 22063104 | tf_op jit(solution)/shard_map/while/body/gather | solution.py:292
  223.1 22.1 %body.4 = f32[32,64,64]{2,1,0:T(8,128)} custom-call(bf16[336,336]{1,0:T(8,128)(2,1)S(1)} %get-tuple-element.376.integ_ref, bf16[32,336,512]{2,1,0:T(8,128)(2,1)} %bitcast.38, bf16[2,336,256]{2,1,0:T(8,128)(2,1)S(1)} %get-tuple-element.377.sign_ref, bf16[2,256,336]{2,1,0:T(8,128)(2,1)S(1)} %get-tuple-element.378.table_ref), custom_call_target="tpu_custom_call" | custom-call | tf_op jit(solution)/shard_map/while/body/pallas_call | solution.py:45
  245.2 1.5 reshape.124
  246.8 1.1 copy_dynamic-update-slice_fusion.2
  247.9 33.8 %shard_map.83 = f32[16,4,32,256]{3,2,1,0:T(8,128)} custom-call(f32[16,4,32,256]{3,2,1,0:T(8,128)} %get-tuple-element.170.send_ref), custom_call_target="tpu_custom_call" | custom-call | tf_op jit(solution)/shard_map/pallas_call | solution.py:99
  281.8 1.8 reduce_sum.29
  283.6 0.7 copy.31
  284.3 34.0 %shard_map.84 = f32[8,3,64,256]{3,2,1,0:T(8,128)} custom-call(f32[3,64,256]{2,1,0:T(8,128)} %bitcast.47), custom_call_target="tpu_custom_call" | custom-call | tf_op jit(solution)/shard_map/pallas_call | solution.py:194
  318.3 0.1 compare_select_fusion
  318.4 2.0 gather_fusion.1
  320.4 0.1 dynamic_slice.28
  320.5 0.1 broadcast_in_dim.90
  320.6 0.1 broadcast_in_dim.91
  320.7 0.1 dynamic-slice_compare_fusion
  320.8 0.1 broadcast_in_dim.88
  320.8 0.1 eq.89
  320.9 0.8 fusion.2
  (42 shorter events, 0.3 us)
Async XLA Ops:
  0.7 0.6 copy-start.8
  2.2 42.9 %copy-start.6 = (pred[32]{0:T(512)(128)(4,1)}, pred[32]{0:T(512)(128)(4,1)S(1)}, u32[]{:S(2)}) copy-start(pred[32]{0:T(512)(128)(4,1)S(1)} %get-tuple-element.240) | copy-start | bytes 100
  3.1 42.0 %copy-start.10 = (s32[32]{0:T(128)}, s32[32]{0:T(128)S(1)}, u32[]{:S(2)}) copy-start(s32[32]{0:T(128)S(1)} %get-tuple-element.242) | copy-start | bytes 388
  45.2 7.2 %copy-start = (s32[324,2048]{1,0:T(8,128)S(1)}, s32[324,2048]{1,0:T(8,128)}, u32[]{:S(2)}) copy-start(s32[324,2048]{1,0:T(8,128)} %param.14) | copy-start | bytes 7962628
  54.7 3.5 %copy-start.2 = (s32[4,20736]{1,0:T(4,128)S(1)}, s32[4,20736]{1,0:T(4,128)}, u32[]{:S(2)}) copy-start(s32[4,20736]{1,0:T(4,128)} %param.16) | copy-start | bytes 995332
  58.2 3.1 copy-start.5
  60.8 2.8 copy-start.4
  281.7 36.6 %copy-start.11 = (s32[32]{0:T(128)S(1)}, s32[32]{0:T(128)}, u32[]{:S(2)}) copy-start(s32[32]{0:T(128)} %copy-done.10) | copy-start | bytes 388
  281.7 38.7 %copy-start.7 = (pred[32]{0:T(512)(128)(4,1)S(1)}, pred[32]{0:T(512)(128)(4,1)}, u32[]{:S(2)}) copy-start(pred[32]{0:T(512)(128)(4,1)} %copy-done.6) | copy-start | bytes 100
  281.7 38.9 %copy-start.9 = (s32[32]{0:T(128)S(1)}, s32[32]{0:T(128)}, u32[]{:S(2)}) copy-start(s32[32]{0:T(128)} %copy-done.8) | copy-start | bytes 388
  281.7 39.2 %copy-start.1 = (bf16[256,256]{1,0:T(8,128)(2,1)S(1)}, bf16[256,256]{1,0:T(8,128)(2,1)}, u32[]{:S(2)}) copy-start(bf16[256,256]{1,0:T(8,128)(2,1)} %own_ref.1) | copy-start | bytes 393220
  281.8 39.2 %copy-start.3 = (f32[256,256]{1,0:T(8,128)S(1)}, f32[256,256]{1,0:T(8,128)}, u32[]{:S(2)}) copy-start(f32[256,256]{1,0:T(8,128)} %param.11) | copy-start | bytes 786436

commit v12 on v11

--- a/solution.py
+++ b/solution.py
@@ -99,7 +99,7 @@
     return pl.pallas_call(
         exchange_kernel,
         out_shape=jax.ShapeDtypeStruct(send.shape, send.dtype),
-        in_specs=[pl.BlockSpec(memory_space=pl.ANY)],
+        in_specs=[pl.BlockSpec(memory_space=pltpu.VMEM)],
         out_specs=pl.BlockSpec(memory_space=pl.ANY),
         scratch_shapes=[
             pltpu.SemaphoreType.DMA((count,)),
@@ -149,7 +149,7 @@
         out_shape=jax.ShapeDtypeStruct(
             (count // PAIR * own.shape[0], PAIR * own.shape[1]), own.dtype
         ),
-        in_specs=[pl.BlockSpec(memory_space=pl.ANY)],
+        in_specs=[pl.BlockSpec(memory_space=pltpu.VMEM)],
         out_specs=pl.BlockSpec(memory_space=pl.ANY),
         scratch_shapes=[
             pltpu.SemaphoreType.DMA((count,)),
@@ -194,7 +194,7 @@
     return pl.pallas_call(
         gather_alpha_kernel,
         out_shape=jax.ShapeDtypeStruct((count,) + own.shape, own.dtype),
-        in_specs=[pl.BlockSpec(memory_space=pl.ANY)],
+        in_specs=[pl.BlockSpec(memory_space=pltpu.VMEM)],
         out_specs=pl.BlockSpec(memory_space=pl.ANY),
         scratch_shapes=[
             pltpu.SemaphoreType.DMA((count,)),

time: 323 us -> 266 us (0.82)
  local copies, waits for them, and re-layouts: 124 us -> 87.1 us
  Pallas kernels: 172 us -> 154 us
    gather x3 -> x2, local copies, waits for them, and re-layouts: 101 us -> 67.6 us  [one_block(): lax.gather(coeff_ext, row_ids[:, :, None], dims, slice_sizes=(1, wide_col...]
    pallas_call x3 -> x2, Pallas kernels: 66.3 us -> 44.2 us  [mix_block(): pl.pallas_call(mix_kernel, out_shape=jax.ShapeDtypeStruct((rows, targets,...]
where the time goes in v12:
time: 266 us; the launch traced here: 265 us
  Pallas kernels  154 us (58%)
  local copies, waits for them, and re-layouts  87.1 us (33%)
  other arithmetic  17.2 us (6%)
  blocking collectives  3.83 us (1%)
    gather x2, local copies, waits for them, and re-layouts, one_block(): lax.gather(coeff_ext, row_ids[:, :, None], dims, slice_sizes=(1, wide_col...  67.6 us
    pallas_call x2, Pallas kernels, mix_block(): pl.pallas_call(mix_kernel, out_shape=jax.ShapeDtypeStruct((rows, targets,...  44.2 us
    pallas_call x1, Pallas kernels, spread(): pl.pallas_call(spread_kernel, out_shape=jax.ShapeDtypeStruct((count // PA...  38.3 us
    pallas_call x1, Pallas kernels, exchange(): pl.pallas_call(exchange_kernel, out_shape=jax.ShapeDtypeStruct(send.shape...  36.5 us
    pallas_call x1, Pallas kernels, gather_alpha(): pl.pallas_call(gather_alpha_kernel, out_shape=jax.ShapeDtypeStruct((count...  34.8 us
    concatenate x1, other arithmetic, on_device(): jnp.concatenate([gathered, -gathered, jnp.zeros((16, wide_cols), jnp.bflo...  7.18 us
    while x2, local copies, waits for them, and re-layouts, on_device(): send = lax.fori_loop(0, my_count, one_block, empty)  5.8 us

profile of v12, /device:TPU:1, one launch (start us, length us, event | category | flops | bytes accessed | tf_op | source)
XLA Modules:
  0.0 265.0 jit_solution(9970495542810112202)
XLA Ops:
  0.0 0.7 compare_convert_fusion
  0.7 0.6 copy-done.8
  1.2 0.1 reshape.84
  1.3 0.2 reduce_window_sum.18
  1.5 0.1 eq.92
  1.6 0.7 broadcast_compare_fusion.1
  2.2 0.1 copy.25
  2.3 0.1 reduce-window.9
  2.4 0.1 reduce.18
  2.5 0.6 fusion.8
  3.8 0.8 iota_reduce_fusion
  5.3 0.1 select_reduce_fusion
  5.4 0.1 broadcast_in_dim.96
  5.5 0.1 convert_element_type.42
  5.6 38.3 %shard_map.82 = bf16[2048,512]{1,0:T(8,128)(2,1)} custom-call(bf16[256,256]{1,0:T(8,128)(2,1)} %own_ref.1), custom_call_target="tpu_custom_call" | custom-call | tf_op jit(solution)/shard_map/pallas_call | solution.py:147
  43.9 1.9 fusion.7
  45.8 0.0 copy-start
  45.9 7.2 %maximum_maximum_fusion = bf16[4112,512]{1,0:T(8,128)(2,1)} fusion(bf16[2048,512]{1,0:T(8,128)(2,1)S(1)} %get-tuple-element.236, bf16[2048,512]{1,0:T(8,128)(2,1)S(1)} %get-tuple-element.237, bf16[4112]{0:T(1024)(128)(2,1)S(1)} %pad.28.clone), kind=kLoop, calls=%fused_computation.7 | loop fusion | flops 12632064 | bytes 8413216 | tf_op jit(solution)/shard_map/concatenate | solution.py:229
  53.0 0.0 copy-done
  53.0 2.3 copy.27
  55.3 3.5 %copy.28 = s32[324,2048]{0,1:T(8,128)} copy(s32[324,2048]{1,0:T(8,128)} %param.13) | data formatting | bytes 5308416 | tf_op jit(solution)/shard_map/while | solution.py:304
  58.8 0.1 convert_bitcast_fusion
  58.9 2.0 all-gather
  60.9 0.4 reshape.87
  61.4 0.0 copy-start.4
  61.4 0.3 copy.26
  61.7 0.2 copy.35
  61.9 1.8 all-gather.1
  63.7 0.1 eq.100
  63.8 0.1 eq.98
  63.9 0.2 bitcast_compare_fusion
  64.1 0.1 pad_convert_fusion
  64.2 1.6 broadcast_in_dim.93.clone
  65.8 121.8 %while.12 = (s32[]{:T(128)}, f32[16,4,32,256]{3,2,1,0:T(8,128)}, s32[]{:T(128)}, s32[]{:T(128)}, s32[32]{0:T(128)S(1)}, /*index=5*/s32[]{:T(128)}, s32[]{:T(128)...) while((s32[]{:T(128)}, f32[16,4,32,256]{3,2,1,0:T(8,128)}, ...), condition=%wide.region_6.7_spmd, body=%wide.region_5.6_spmd.sunk | while | flops 63123 | bytes 24543636 | solution.py:304
  65.8 0.7 dynamic_slice.40
  67.2 0.8 fusion.10
  68.1 0.1 reshape.123
  68.2 33.8 %gather_fusion = bf16[10752,512]{1,0:T(8,128)(2,1)} fusion(bf16[4112,512]{1,0:T(8,128)(2,1)} %get-tuple-element.375, s32[11264]{0:T(1024)S(1)} %pad_clamp_fusion.3), kind=kCustom, calls=%fused_computation.clone.1 | custom fusion | bytes 22063104 | tf_op jit(solution)/shard_map/while/body/gather | solution.py:292
  102.0 22.1 %body.4 = f32[32,64,64]{2,1,0:T(8,128)} custom-call(bf16[336,336]{1,0:T(8,128)(2,1)S(1)} %get-tuple-element.376.integ_ref, bf16[32,336,512]{2,1,0:T(8,128)(2,1)} %bitcast.38, bf16[2,336,256]{2,1,0:T(8,128)(2,1)S(1)} %get-tuple-element.377.sign_ref, bf16[2,256,336]{2,1,0:T(8,128)(2,1)S(1)} %get-tuple-element.378.table_ref), custom_call_target="tpu_custom_call" | custom-call | tf_op jit(solution)/shard_map/while/body/pallas_call | solution.py:45
  124.1 1.5 reshape.124
  125.6 1.1 copy_dynamic-update-slice_fusion.2
  126.7 0.7 dynamic_slice.40
  128.1 0.8 fusion.10
  129.0 0.1 reshape.123
  129.1 33.8 %gather_fusion = bf16[10752,512]{1,0:T(8,128)(2,1)} fusion(bf16[4112,512]{1,0:T(8,128)(2,1)} %get-tuple-element.375, s32[11264]{0:T(1024)S(1)} %pad_clamp_fusion.3), kind=kCustom, calls=%fused_computation.clone.1 | custom fusion | bytes 22063104 | tf_op jit(solution)/shard_map/while/body/gather | solution.py:292
  162.9 22.1 %body.4 = f32[32,64,64]{2,1,0:T(8,128)} custom-call(bf16[336,336]{1,0:T(8,128)(2,1)S(1)} %get-tuple-element.376.integ_ref, bf16[32,336,512]{2,1,0:T(8,128)(2,1)} %bitcast.38, bf16[2,336,256]{2,1,0:T(8,128)(2,1)S(1)} %get-tuple-element.377.sign_ref, bf16[2,256,336]{2,1,0:T(8,128)(2,1)S(1)} %get-tuple-element.378.table_ref), custom_call_target="tpu_custom_call" | custom-call | tf_op jit(solution)/shard_map/while/body/pallas_call | solution.py:45
  185.0 1.5 reshape.124
  186.5 1.1 copy_dynamic-update-slice_fusion.2
  187.6 36.5 %shard_map.83 = f32[16,4,32,256]{3,2,1,0:T(8,128)} custom-call(f32[16,4,32,256]{3,2,1,0:T(8,128)} %get-tuple-element.170.send_ref), custom_call_target="tpu_custom_call" | custom-call | tf_op jit(solution)/shard_map/pallas_call | solution.py:99
  224.2 0.0 copy-start.1
  224.2 0.0 copy-start.3
  224.2 1.8 reduce_sum.29
  226.1 0.7 copy.31
  226.8 34.8 %shard_map.84 = f32[8,3,64,256]{3,2,1,0:T(8,128)} custom-call(f32[3,64,256]{2,1,0:T(8,128)} %bitcast.47), custom_call_target="tpu_custom_call" | custom-call | tf_op jit(solution)/shard_map/pallas_call | solution.py:194
  261.5 0.0 copy-done.11
  261.5 0.1 compare_select_fusion
  261.6 2.0 gather_fusion.1
  263.6 0.1 dynamic_slice.28
  263.7 0.1 broadcast_in_dim.90
  263.8 0.1 broadcast_in_dim.91
  263.9 0.1 dynamic-slice_compare_fusion
  264.0 0.1 broadcast_in_dim.88
  264.0 0.1 eq.89
  264.1 0.8 fusion.2
  (33 shorter events, 0.2 us)
Async XLA Ops:
  0.7 0.6 copy-start.8
  2.2 43.6 %copy-start.6 = (pred[32]{0:T(512)(128)(4,1)}, pred[32]{0:T(512)(128)(4,1)S(1)}, u32[]{:S(2)}) copy-start(pred[32]{0:T(512)(128)(4,1)S(1)} %get-tuple-element.240) | copy-start | bytes 100
  3.1 42.7 %copy-start.10 = (s32[32]{0:T(128)}, s32[32]{0:T(128)S(1)}, u32[]{:S(2)}) copy-start(s32[32]{0:T(128)S(1)} %get-tuple-element.242) | copy-start | bytes 388
  45.8 7.2 %copy-start = (s32[324,2048]{1,0:T(8,128)S(1)}, s32[324,2048]{1,0:T(8,128)}, u32[]{:S(2)}) copy-start(s32[324,2048]{1,0:T(8,128)} %param.14) | copy-start | bytes 7962628
  55.3 3.5 %copy-start.2 = (s32[4,20736]{1,0:T(4,128)S(1)}, s32[4,20736]{1,0:T(4,128)}, u32[]{:S(2)}) copy-start(s32[4,20736]{1,0:T(4,128)} %param.16) | copy-start | bytes 995332
  58.8 3.1 %copy-start.5 = (s32[4,324]{1,0:T(4,128)S(1)}, s32[4,324]{1,0:T(4,128)}, u32[]{:S(2)}) copy-start(s32[4,324]{1,0:T(4,128)} %param.15) | copy-start | bytes 15556
  61.4 2.8 %copy-start.4 = (bf16[324,324]{1,0:T(8,128)(2,1)S(1)}, bf16[324,324]{1,0:T(8,128)(2,1)}, u32[]{:S(2)}) copy-start(bf16[324,324]{1,0:T(8,128)(2,1)} %param.12) | copy-start | bytes 629860
  224.2 37.4 %copy-start.11 = (s32[32]{0:T(128)S(1)}, s32[32]{0:T(128)}, u32[]{:S(2)}) copy-start(s32[32]{0:T(128)} %copy-done.10) | copy-start | bytes 388
  224.2 39.5 %copy-start.7 = (pred[32]{0:T(512)(128)(4,1)S(1)}, pred[32]{0:T(512)(128)(4,1)}, u32[]{:S(2)}) copy-start(pred[32]{0:T(512)(128)(4,1)} %copy-done.6) | copy-start | bytes 100
  224.2 39.7 %copy-start.9 = (s32[32]{0:T(128)S(1)}, s32[32]{0:T(128)}, u32[]{:S(2)}) copy-start(s32[32]{0:T(128)} %copy-done.8) | copy-start | bytes 388
  224.2 39.9 %copy-start.1 = (bf16[256,256]{1,0:T(8,128)(2,1)S(1)}, bf16[256,256]{1,0:T(8,128)(2,1)}, u32[]{:S(2)}) copy-start(bf16[256,256]{1,0:T(8,128)(2,1)} %own_ref.1) | copy-start | bytes 393220
  224.2 39.9 %copy-start.3 = (f32[256,256]{1,0:T(8,128)S(1)}, f32[256,256]{1,0:T(8,128)}, u32[]{:S(2)}) copy-start(f32[256,256]{1,0:T(8,128)} %param.11) | copy-start | bytes 786436

commit v13 on v11

--- a/solution.py
+++ b/solution.py
@@ -63,35 +63,37 @@
     alpha = lax.axis_index("alpha")
     me = lax.axis_index("g") * PAIR + lax.axis_index("m")
 
-    def remote(slot, peer):
+    def remote(src_slot, dst_slot, sem_slot, peer):
         return pltpu.make_async_remote_copy(
-            src_ref=send_ref.at[slot],
-            dst_ref=recv_ref.at[slot],
-            send_sem=send_sem.at[slot],
-            recv_sem=recv_sem.at[slot],
+            src_ref=send_ref.at[src_slot],
+            dst_ref=recv_ref.at[dst_slot],
+            send_sem=send_sem.at[sem_slot],
+            recv_sem=recv_sem.at[dst_slot],
             device_id=(alpha, peer // PAIR, peer % PAIR),
             device_id_type=pl.DeviceIdType.MESH,
         )
 
-    for step in range(1, count):
-        dest = lax.rem(me + step, count)
-        pltpu.make_async_remote_copy(
-            src_ref=send_ref.at[dest],
-            dst_ref=recv_ref.at[me],
-            send_sem=send_sem.at[dest],
-            recv_sem=recv_sem.at[me],
-            device_id=(alpha, dest // PAIR, dest % PAIR),
+    barrier = pltpu.get_barrier_semaphore()
+    for step in range(1, count):
+        peer = lax.rem(me + step, count)
+        pl.semaphore_signal(
+            barrier, 1, device_id=(alpha, peer // PAIR, peer % PAIR),
             device_id_type=pl.DeviceIdType.MESH,
-        ).start()
+        )
+    pl.semaphore_wait(barrier, count - 1)
+
+    for step in range(1, count):
+        dest = lax.rem(me + step, count)
+        remote(dest, me, dest, dest).start()
     local = pltpu.make_async_copy(send_ref.at[me], recv_ref.at[me], local_sem)
     local.start()
     local.wait()
     for step in range(1, count):
         dest = lax.rem(me + step, count)
-        remote(dest, dest).wait_send()
+        remote(dest, me, dest, dest).wait_send()
     for step in range(1, count):
         src = lax.rem(me + count - step, count)
-        remote(src, src).wait_recv()
+        remote(src, src, src, src).wait_recv()
 
 
 def exchange(send):
@@ -106,7 +108,7 @@
             pltpu.SemaphoreType.DMA((count,)),
             pltpu.SemaphoreType.DMA,
         ],
-        compiler_params=pltpu.CompilerParams(has_side_effects=True),
+        compiler_params=pltpu.CompilerParams(collective_id=0, has_side_effects=True),
     )(send)
 
 
@@ -298,14 +300,13 @@
         )
         summed = mix_block(integ_pad, picked, sign_q, table_all, total_blocks, block_len)
         part = summed.reshape(sub_rows, beta_size, local_cols).transpose(1, 0, 2)
-        return lax.dynamic_update_slice(buffer, part[:, None], (0, slot, 0, 0))
-
-    empty = jnp.zeros((beta_size, per_device, sub_rows, local_cols), jnp.float32)
-    send = lax.fori_loop(0, my_count, one_block, empty)
-    recv = exchange(send)
-    groups = recv.shape[0] // PAIR
-    recv = recv.reshape(groups, PAIR, per_device, sub_rows, local_cols).sum(axis=0)
-    done = recv.transpose(1, 0, 2, 3).reshape(per_device, block_len, local_cols)
+        recv = exchange(part)
+        groups = recv.shape[0] // PAIR
+        rows = recv.reshape(groups, PAIR * sub_rows, local_cols).sum(axis=0)
+        return lax.dynamic_update_slice(buffer, rows[None], (slot, 0, 0))
+
+    empty = jnp.zeros((per_device, block_len, local_cols), jnp.float32)
+    done = lax.fori_loop(0, my_count, one_block, empty)
     everyone = gather_alpha(done[1:], alpha_size).reshape(
         alpha_size * (per_device - 1), block_len, local_cols
     )

time: 323 us -> 248 us (0.77)
  local copies, waits for them, and re-layouts: 124 us -> 85.2 us
  Pallas kernels: 172 us -> 138 us
    gather x3 -> x2, local copies, waits for them, and re-layouts: 101 us -> 67.6 us  [one_block(): lax.gather(coeff_ext, row_ids[:, :, None], dims, slice_sizes=(1, wide_col...]
    pallas_call x3 -> x2, Pallas kernels: 66.3 us -> 44.3 us  [mix_block(): pl.pallas_call(mix_kernel, out_shape=jax.ShapeDtypeStruct((rows, targets,...]
    pallas_call x1 -> x2, Pallas kernels: 33.8 us -> 26.7 us  [exchange(): pl.pallas_call(exchange_kernel, out_shape=jax.ShapeDtypeStruct(send.shape...]
    pallas_call x1, Pallas kernels: 34 us -> 28.8 us  [gather_alpha(): pl.pallas_call(gather_alpha_kernel, out_shape=jax.ShapeDtypeStruct((count...]
    dynamic_update_slice x3 -> x2, local copies, waits for them, and re-layouts: 3.41 us -> 0.02 us  [one_block(): return lax.dynamic_update_slice(buffer, rows[None], (slot, 0, 0))]
where the time goes in v13:
time: 248 us; the launch traced here: 247 us
  Pallas kernels  138 us (56%)
  local copies, waits for them, and re-layouts  85.2 us (34%)
  other arithmetic  17.5 us (7%)
  blocking collectives  3.96 us (2%)
    gather x2, local copies, waits for them, and re-layouts, one_block(): lax.gather(coeff_ext, row_ids[:, :, None], dims, slice_sizes=(1, wide_col...  67.6 us
    pallas_call x2, Pallas kernels, mix_block(): pl.pallas_call(mix_kernel, out_shape=jax.ShapeDtypeStruct((rows, targets,...  44.3 us
    pallas_call x1, Pallas kernels, spread(): pl.pallas_call(spread_kernel, out_shape=jax.ShapeDtypeStruct((count // PA...  37.6 us
    pallas_call x1, Pallas kernels, gather_alpha(): pl.pallas_call(gather_alpha_kernel, out_shape=jax.ShapeDtypeStruct((count...  28.8 us
    pallas_call x2, Pallas kernels, exchange(): pl.pallas_call(exchange_kernel, out_shape=jax.ShapeDtypeStruct(send.shape...  26.7 us
    concatenate x1, other arithmetic, on_device(): jnp.concatenate([gathered, -gathered, jnp.zeros((16, wide_cols), jnp.bflo...  7.18 us
    while x2, local copies, waits for them, and re-layouts, on_device(): done = lax.fori_loop(0, my_count, one_block, empty)  5.8 us
    reshape x4, local copies, waits for them, and re-layouts, one_block(): part = summed.reshape(sub_rows, beta_size, local_cols).transpose(1, 0, 2)  5.22 us

profile of v13, /device:TPU:1, one launch (start us, length us, event | category | flops | bytes accessed | tf_op | source)
XLA Modules:
  0.0 247.3 jit_solution(12247033914023760202)
XLA Ops:
  0.0 0.7 compare_convert_fusion
  0.7 0.6 copy-done.8
  1.2 0.1 reshape.83
  1.3 0.2 reduce_window_sum.18
  1.5 0.1 eq.92
  1.6 0.7 broadcast_compare_fusion.1
  2.3 0.1 copy.24
  2.3 0.1 reduce-window.9
  2.4 0.1 reduce.18
  2.5 0.6 fusion.8
  3.8 0.8 iota_reduce_fusion
  5.3 0.1 select_reduce_fusion
  5.4 0.1 broadcast_in_dim.96
  5.5 0.1 convert_element_type.42
  5.6 37.6 %shard_map.82 = bf16[2048,512]{1,0:T(8,128)(2,1)} custom-call(bf16[256,256]{1,0:T(8,128)(2,1)} %own_ref.1), custom_call_target="tpu_custom_call" | custom-call | tf_op jit(solution)/shard_map/pallas_call | solution.py:149
  43.3 1.9 fusion.7
  45.2 0.0 copy-done.6
  45.2 0.0 copy-start
  45.3 7.2 %maximum_maximum_fusion = bf16[4112,512]{1,0:T(8,128)(2,1)} fusion(bf16[2048,512]{1,0:T(8,128)(2,1)S(1)} %get-tuple-element.236, bf16[2048,512]{1,0:T(8,128)(2,1)S(1)} %get-tuple-element.237, bf16[4112]{0:T(1024)(128)(2,1)S(1)} %pad.28.clone), kind=kLoop, calls=%fused_computation.9 | loop fusion | flops 12632064 | bytes 8413216 | tf_op jit(solution)/shard_map/concatenate | solution.py:231
  52.4 2.3 copy.26
  54.7 3.5 %copy.27 = s32[324,2048]{0,1:T(8,128)} copy(s32[324,2048]{1,0:T(8,128)} %param.13) | data formatting | bytes 5308416 | tf_op jit(solution)/shard_map/while | solution.py:309
  58.2 0.1 convert_bitcast_fusion
  58.3 0.0 copy-start.4
  58.3 2.2 all-gather
  60.5 0.4 reshape.86
  60.9 0.3 copy.25
  61.2 0.2 copy.29
  61.5 1.8 all-gather.1
  63.3 0.1 eq.100
  63.4 0.1 eq.98
  63.4 0.2 bitcast_compare_fusion
  63.6 0.1 pad_convert_fusion
  63.8 0.0 copy-start.1
  63.8 0.0 copy-start.3
  63.8 150.5 %while.12 = (s32[]{:T(128)}, f32[4,64,256]{2,1,0:T(8,128)S(1)}, s32[]{:T(128)}, s32[]{:T(128)}, s32[32]{0:T(128)S(1)}, /*index=5*/s32[]{:T(128)}, s32[]{:T(128)}...) while((s32[]{:T(128)}, f32[4,64,256]{2,1,0:T(8,128)S(1)}, ...), condition=%wide.region_7.8_spmd, body=%wide.region_5.7_spmd.sunk | while | flops 177811 | bytes 25264532 | solution.py:309
  64.0 0.6 dynamic_slice.40
  65.2 0.8 fusion.10
  66.0 0.1 reshape.121
  66.1 33.8 %gather_fusion = bf16[10752,512]{1,0:T(8,128)(2,1)} fusion(bf16[4112,512]{1,0:T(8,128)(2,1)} %get-tuple-element.375, s32[11264]{0:T(1024)S(1)} %pad_clamp_fusion.3), kind=kCustom, calls=%fused_computation.clone.1 | custom fusion | bytes 22063104 | tf_op jit(solution)/shard_map/while/body/gather | solution.py:294
  99.9 22.2 %body.8 = f32[32,64,64]{2,1,0:T(8,128)} custom-call(bf16[336,336]{1,0:T(8,128)(2,1)S(1)} %get-tuple-element.376.integ_ref, bf16[32,336,512]{2,1,0:T(8,128)(2,1)} %bitcast.45, bf16[2,336,256]{2,1,0:T(8,128)(2,1)S(1)} %get-tuple-element.377.sign_ref, bf16[2,256,336]{2,1,0:T(8,128)(2,1)S(1)} %get-tuple-element.378.table_ref), custom_call_target="tpu_custom_call" | custom-call | tf_op jit(solution)/shard_map/while/body/pallas_call | solution.py:45
  122.1 1.5 reshape.122
  123.6 1.1 copy.33
  124.7 13.6 %body.9 = f32[16,32,256]{2,1,0:T(8,128)} custom-call(f32[16,32,256]{2,1,0:T(8,128)} %bitcast.46), custom_call_target="tpu_custom_call" | custom-call | tf_op jit(solution)/shard_map/while/body/pallas_call | solution.py:101
  138.2 1.1 bitcast_reduce_fusion.2
  139.4 0.6 dynamic_slice.40
  140.5 0.8 fusion.10
  141.4 0.1 reshape.121
  141.5 33.8 %gather_fusion = bf16[10752,512]{1,0:T(8,128)(2,1)} fusion(bf16[4112,512]{1,0:T(8,128)(2,1)} %get-tuple-element.375, s32[11264]{0:T(1024)S(1)} %pad_clamp_fusion.3), kind=kCustom, calls=%fused_computation.clone.1 | custom fusion | bytes 22063104 | tf_op jit(solution)/shard_map/while/body/gather | solution.py:294
  175.3 22.2 %body.8 = f32[32,64,64]{2,1,0:T(8,128)} custom-call(bf16[336,336]{1,0:T(8,128)(2,1)S(1)} %get-tuple-element.376.integ_ref, bf16[32,336,512]{2,1,0:T(8,128)(2,1)} %bitcast.45, bf16[2,336,256]{2,1,0:T(8,128)(2,1)S(1)} %get-tuple-element.377.sign_ref, bf16[2,256,336]{2,1,0:T(8,128)(2,1)S(1)} %get-tuple-element.378.table_ref), custom_call_target="tpu_custom_call" | custom-call | tf_op jit(solution)/shard_map/while/body/pallas_call | solution.py:45
  197.4 1.5 reshape.122
  198.9 1.1 copy.33
  200.0 13.2 %body.9 = f32[16,32,256]{2,1,0:T(8,128)} custom-call(f32[16,32,256]{2,1,0:T(8,128)} %bitcast.46), custom_call_target="tpu_custom_call" | custom-call | tf_op jit(solution)/shard_map/while/body/pallas_call | solution.py:101
  213.2 1.1 bitcast_reduce_fusion.2
  214.3 0.7 slice.7.own_ref
  215.0 28.8 %shard_map.83 = f32[8,3,64,256]{3,2,1,0:T(8,128)} custom-call(f32[3,64,256]{2,1,0:T(8,128)} %slice.7.own_ref), custom_call_target="tpu_custom_call" | custom-call | tf_op jit(solution)/shard_map/pallas_call | solution.py:196
  243.9 0.1 compare_select_fusion
  244.0 2.0 gather_fusion.1
  246.0 0.1 dynamic_slice.28
  246.1 0.1 broadcast_in_dim.90
  246.1 0.1 broadcast_in_dim.91
  246.2 0.1 dynamic-slice_compare_fusion
  246.3 0.1 broadcast_in_dim.88
  246.4 0.1 eq.89
  246.5 0.8 fusion.2
  (36 shorter events, 0.2 us)
Async XLA Ops:
  0.7 0.6 copy-start.8
  2.3 42.9 %copy-start.6 = (pred[32]{0:T(512)(128)(4,1)}, pred[32]{0:T(512)(128)(4,1)S(1)}, u32[]{:S(2)}) copy-start(pred[32]{0:T(512)(128)(4,1)S(1)} %get-tuple-element.240) | copy-start | bytes 100
  3.2 42.0 %copy-start.10 = (s32[32]{0:T(128)}, s32[32]{0:T(128)S(1)}, u32[]{:S(2)}) copy-start(s32[32]{0:T(128)S(1)} %get-tuple-element.242) | copy-start | bytes 388
  45.2 7.2 %copy-start = (s32[324,2048]{1,0:T(8,128)S(1)}, s32[324,2048]{1,0:T(8,128)}, u32[]{:S(2)}) copy-start(s32[324,2048]{1,0:T(8,128)} %param.14) | copy-start | bytes 7962628
  54.7 3.5 %copy-start.2 = (s32[4,20736]{1,0:T(4,128)S(1)}, s32[4,20736]{1,0:T(4,128)}, u32[]{:S(2)}) copy-start(s32[4,20736]{1,0:T(4,128)} %param.16) | copy-start | bytes 995332
  58.2 3.2 %copy-start.5 = (s32[4,324]{1,0:T(4,128)S(1)}, s32[4,324]{1,0:T(4,128)}, u32[]{:S(2)}) copy-start(s32[4,324]{1,0:T(4,128)} %param.15) | copy-start | bytes 15556
  58.3 5.4 %copy-start.4 = (bf16[324,324]{1,0:T(8,128)(2,1)S(1)}, bf16[324,324]{1,0:T(8,128)(2,1)}, u32[]{:S(2)}) copy-start(bf16[324,324]{1,0:T(8,128)(2,1)} %param.12) | copy-start | bytes 629860
  63.8 180.1 %copy-start.11 = (s32[32]{0:T(128)S(1)}, s32[32]{0:T(128)}, u32[]{:S(2)}) copy-start(s32[32]{0:T(128)} %copy-done.10) | copy-start | bytes 388
  63.8 182.2 %copy-start.7 = (pred[32]{0:T(512)(128)(4,1)S(1)}, pred[32]{0:T(512)(128)(4,1)}, u32[]{:S(2)}) copy-start(pred[32]{0:T(512)(128)(4,1)} %copy-done.6) | copy-start | bytes 100
  63.8 182.4 %copy-start.9 = (s32[32]{0:T(128)S(1)}, s32[32]{0:T(128)}, u32[]{:S(2)}) copy-start(s32[32]{0:T(128)} %copy-done.8) | copy-start | bytes 388
  63.8 182.7 %copy-start.1 = (bf16[256,256]{1,0:T(8,128)(2,1)S(1)}, bf16[256,256]{1,0:T(8,128)(2,1)}, u32[]{:S(2)}) copy-start(bf16[256,256]{1,0:T(8,128)(2,1)} %own_ref.1) | copy-start | bytes 393220
  63.8 182.7 %copy-start.3 = (f32[256,256]{1,0:T(8,128)S(1)}, f32[256,256]{1,0:T(8,128)}, u32[]{:S(2)}) copy-start(f32[256,256]{1,0:T(8,128)} %param.11) | copy-start | bytes 786436

commit v14 on v13

--- a/solution.py
+++ b/solution.py
@@ -178,6 +178,14 @@
             device_id_type=pl.DeviceIdType.MESH,
         )
 
+    barrier = pltpu.get_barrier_semaphore()
+    for step in range(1, count):
+        peer = lax.rem(me + step, count)
+        pl.semaphore_signal(
+            barrier, 1, device_id=(peer, group, member), device_id_type=pl.DeviceIdType.MESH
+        )
+    pl.semaphore_wait(barrier, count - 1)
+
     for step in range(1, count):
         dest = lax.rem(me + step, count)
         remote(me, dest, dest).start()
@@ -203,7 +211,7 @@
             pltpu.SemaphoreType.DMA((count,)),
             pltpu.SemaphoreType.DMA,
         ],
-        compiler_params=pltpu.CompilerParams(has_side_effects=True),
+        compiler_params=pltpu.CompilerParams(collective_id=1, has_side_effects=True),
     )(own)
 
 
@@ -307,13 +315,17 @@
 
     empty = jnp.zeros((per_device, block_len, local_cols), jnp.float32)
     done = lax.fori_loop(0, my_count, one_block, empty)
-    everyone = gather_alpha(done[1:], alpha_size).reshape(
-        alpha_size * (per_device - 1), block_len, local_cols
-    )
+    pushes = jnp.maximum(extra_total + alpha_size - 1, 0) // alpha_size
+
+    def push(step, held):
+        arrived = gather_alpha(done[step + 1], alpha_size)
+        return lax.dynamic_update_slice(held, arrived[None], (step, 0, 0, 0))
+
+    everyone = lax.fori_loop(
+        0, pushes, push, jnp.zeros((per_device - 1, alpha_size, block_len, local_cols), jnp.float32)
+    ).reshape((per_device - 1) * alpha_size, block_len, local_cols)
     own_rank = lax.dynamic_slice_in_dim(extra_rank, alpha_rank * per_device, per_device, 0)
-    pick = (own_rank % alpha_size) * (per_device - 1) + jnp.minimum(
-        own_rank // alpha_size, per_device - 2
-    )
+    pick = jnp.minimum(own_rank // alpha_size, per_device - 2) * alpha_size + own_rank % alpha_size
     placed = jnp.where(own_first[:, None, None], done[0][None], everyone[pick])
     placed = placed.reshape(local_rows, local_cols)
     own_live_rows = jnp.repeat(own_flags, block_len)

time: 248 us -> 230 us (0.927)
  Pallas kernels: 138 us -> 119 us
    pallas_call x1, Pallas kernels: 28.8 us -> 9.9 us  [gather_alpha(): pl.pallas_call(gather_alpha_kernel, out_shape=jax.ShapeDtypeStruct((count...]
where the time goes in v14:
time: 230 us; the launch traced here: 229 us
  Pallas kernels  119 us (52%)
  local copies, waits for them, and re-layouts  85 us (37%)
  other arithmetic  17.5 us (8%)
  blocking collectives  3.96 us (2%)
    gather x2, local copies, waits for them, and re-layouts, one_block(): lax.gather(coeff_ext, row_ids[:, :, None], dims, slice_sizes=(1, wide_col...  67.6 us
    pallas_call x2, Pallas kernels, mix_block(): pl.pallas_call(mix_kernel, out_shape=jax.ShapeDtypeStruct((rows, targets,...  44.3 us
    pallas_call x1, Pallas kernels, spread(): pl.pallas_call(spread_kernel, out_shape=jax.ShapeDtypeStruct((count // PA...  37.6 us
    pallas_call x2, Pallas kernels, exchange(): pl.pallas_call(exchange_kernel, out_shape=jax.ShapeDtypeStruct(send.shape...  26.7 us
    pallas_call x1, Pallas kernels, gather_alpha(): pl.pallas_call(gather_alpha_kernel, out_shape=jax.ShapeDtypeStruct((count...  9.9 us
    concatenate x1, other arithmetic, on_device(): jnp.concatenate([gathered, -gathered, jnp.zeros((16, wide_cols), jnp.bflo...  7.18 us
    while x2, local copies, waits for them, and re-layouts, on_device(): done = lax.fori_loop(0, my_count, one_block, empty)  5.8 us
    reshape x4, local copies, waits for them, and re-layouts, one_block(): part = summed.reshape(sub_rows, beta_size, local_cols).transpose(1, 0, 2)  5.22 us

profile of v14, /device:TPU:1, one launch (start us, length us, event | category | flops | bytes accessed | tf_op | source)
XLA Modules:
  0.0 228.9 jit_solution(14976765088612290196)
XLA Ops:
  0.0 0.7 compare_convert_fusion
  0.7 0.6 copy-done.8
  1.2 0.1 reshape.83
  1.3 0.2 reduce_window_sum.18
  1.5 0.1 eq.92
  1.6 0.7 broadcast_compare_fusion.1
  2.3 0.1 copy.24
  2.3 0.1 reduce-window.9
  2.4 0.1 reduce.18
  2.5 0.6 fusion.7
  3.8 0.8 iota_reduce_fusion
  5.3 0.1 select_reduce_fusion
  5.4 0.1 broadcast_in_dim.105
  5.5 0.1 convert_element_type.42
  5.6 37.6 %shard_map.82 = bf16[2048,512]{1,0:T(8,128)(2,1)} custom-call(bf16[256,256]{1,0:T(8,128)(2,1)} %own_ref.1), custom_call_target="tpu_custom_call" | custom-call | tf_op jit(solution)/shard_map/pallas_call | solution.py:149
  43.3 1.9 fusion.6
  45.2 0.0 copy-start
  45.3 7.2 %maximum_maximum_fusion = bf16[4112,512]{1,0:T(8,128)(2,1)} fusion(bf16[2048,512]{1,0:T(8,128)(2,1)S(1)} %get-tuple-element.301, bf16[2048,512]{1,0:T(8,128)(2,1)S(1)} %get-tuple-element.302, bf16[4112]{0:T(1024)(128)(2,1)S(1)} %pad.28.clone), kind=kLoop, calls=%fused_computation.11 | loop fusion | flops 12632064 | bytes 8413216 | tf_op jit(solution)/shard_map/concatenate | solution.py:239
  52.4 2.3 %copy.26 = s32[324,2048]{0,1:T(8,128)} copy(s32[324,2048]{1,0:T(8,128)S(1)} %copy-done) | data formatting | bytes 5308416 | tf_op jit(solution)/shard_map/while | solution.py:317
  54.7 3.5 %copy.27 = s32[324,2048]{0,1:T(8,128)} copy(s32[324,2048]{1,0:T(8,128)} %param.15) | data formatting | bytes 5308416 | tf_op jit(solution)/shard_map/while | solution.py:317
  58.2 0.1 convert_bitcast_fusion
  58.3 2.2 all-gather
  60.5 0.4 reshape.86
  60.9 0.3 copy.25
  61.2 0.2 copy.29
  61.5 1.8 all-gather.1
  63.3 0.1 eq.100
  63.4 0.1 eq.98
  63.4 0.2 bitcast_compare_fusion
  63.6 0.1 pad_convert_fusion
  63.8 150.5 %while.24 = (s32[]{:T(128)}, f32[4,64,256]{2,1,0:T(8,128)S(1)}, s32[]{:T(128)}, s32[]{:T(128)}, s32[32]{0:T(128)S(1)}, /*index=5*/s32[]{:T(128)}, s32[]{:T(128)}...) while((s32[]{:T(128)}, f32[4,64,256]{2,1,0:T(8,128)S(1)}, ...), condition=%wide.region_7.8_spmd, body=%wide.region_5.7_spmd.sunk | while | flops 177811 | bytes 25264532 | solution.py:317
  64.0 0.6 dynamic_slice.48
  65.1 0.8 fusion.9
  66.0 0.1 reshape.121
  66.1 33.8 %gather_fusion = bf16[10752,512]{1,0:T(8,128)(2,1)} fusion(bf16[4112,512]{1,0:T(8,128)(2,1)} %get-tuple-element.466, s32[11264]{0:T(1024)S(1)} %pad_clamp_fusion.3), kind=kCustom, calls=%fused_computation.clone.1 | custom fusion | bytes 22063104 | tf_op jit(solution)/shard_map/while/body/gather | solution.py:302
  99.9 22.2 %body.12 = f32[32,64,64]{2,1,0:T(8,128)} custom-call(bf16[336,336]{1,0:T(8,128)(2,1)S(1)} %get-tuple-element.467.integ_ref, bf16[32,336,512]{2,1,0:T(8,128)(2,1)} %bitcast.53, bf16[2,336,256]{2,1,0:T(8,128)(2,1)S(1)} %get-tuple-element.468.sign_ref, bf16[2,256,336]{2,1,0:T(8,128)(2,1)S(1)} %get-tuple-element.469.table_ref), custom_call_target="tpu_custom_call" | custom-call | tf_op jit(solution)/shard_map/while/body/pallas_call | solution.py:45
  122.0 1.5 reshape.122
  123.5 1.1 copy.33
  124.6 13.6 %body.13 = f32[16,32,256]{2,1,0:T(8,128)} custom-call(f32[16,32,256]{2,1,0:T(8,128)} %bitcast.54), custom_call_target="tpu_custom_call" | custom-call | tf_op jit(solution)/shard_map/while/body/pallas_call | solution.py:101
  138.2 1.1 bitcast_reduce_fusion.2
  139.3 0.6 dynamic_slice.48
  140.4 0.8 fusion.9
  141.3 0.1 reshape.121
  141.4 33.8 %gather_fusion = bf16[10752,512]{1,0:T(8,128)(2,1)} fusion(bf16[4112,512]{1,0:T(8,128)(2,1)} %get-tuple-element.466, s32[11264]{0:T(1024)S(1)} %pad_clamp_fusion.3), kind=kCustom, calls=%fused_computation.clone.1 | custom fusion | bytes 22063104 | tf_op jit(solution)/shard_map/while/body/gather | solution.py:302
  175.2 22.2 %body.12 = f32[32,64,64]{2,1,0:T(8,128)} custom-call(bf16[336,336]{1,0:T(8,128)(2,1)S(1)} %get-tuple-element.467.integ_ref, bf16[32,336,512]{2,1,0:T(8,128)(2,1)} %bitcast.53, bf16[2,336,256]{2,1,0:T(8,128)(2,1)S(1)} %get-tuple-element.468.sign_ref, bf16[2,256,336]{2,1,0:T(8,128)(2,1)S(1)} %get-tuple-element.469.table_ref), custom_call_target="tpu_custom_call" | custom-call | tf_op jit(solution)/shard_map/while/body/pallas_call | solution.py:45
  197.4 1.5 reshape.122
  198.9 1.1 copy.33
  200.0 13.2 %body.13 = f32[16,32,256]{2,1,0:T(8,128)} custom-call(f32[16,32,256]{2,1,0:T(8,128)} %bitcast.54), custom_call_target="tpu_custom_call" | custom-call | tf_op jit(solution)/shard_map/while/body/pallas_call | solution.py:101
  213.2 1.1 bitcast_reduce_fusion.2
  214.9 0.2 broadcast_in_dim.110
  215.2 0.0 copy-start.3
  215.2 11.7 %while.25 = (s32[]{:T(128)}, f32[3,8,64,256]{3,2,1,0:T(8,128)S(1)}, s32[]{:T(128)}, f32[4,64,256]{2,1,0:T(8,128)S(1)}, s32[]{:T(128)}, /*index=5*/s32[]{:T(128)}, s32[]{:T(128)}, s32[]{:T(128)}) while((s32[]{:T(128)}, f32[3,8,64,256]{3,2,1,0:T(8,128)S(1)}, s32[]{:T(128)}, f32[4,64,256]{2,1,0:T(8,128)S(1)}, s32[]{:T(128)}, ...), condition=%wide.region_9.10_spmd, body=%wide.region_8.9_spmd.sunk | while | flops 8 | bytes 1179817 | solution.py:324
  215.2 0.6 dynamic-slice_bitcast_fusion.2.own_ref
  215.8 9.9 %body.14 = f32[8,64,256]{2,1,0:T(8,128)} custom-call(f32[64,256]{1,0:T(8,128)} %dynamic-slice_bitcast_fusion.2.own_ref), custom_call_target="tpu_custom_call" | custom-call | tf_op jit(solution)/shard_map/while/body/pallas_call | solution.py:204
  225.8 1.1 bitcast_dynamic-update-slice_fusion.5
  226.9 0.1 compare_select_fusion
  227.0 0.6 gather_fusion.1
  227.6 0.1 dynamic_slice.34
  227.7 0.1 broadcast_in_dim.99
  227.7 0.1 broadcast_in_dim.100
  227.8 0.1 dynamic-slice_compare_fusion
  227.9 0.1 broadcast_in_dim.97
  228.0 0.1 eq.89
  228.1 0.8 fusion.2
  (39 shorter events, 0.2 us)
Async XLA Ops:
  0.7 0.6 copy-start.8
  2.3 42.9 %copy-start.6 = (pred[32]{0:T(512)(128)(4,1)}, pred[32]{0:T(512)(128)(4,1)S(1)}, u32[]{:S(2)}) copy-start(pred[32]{0:T(512)(128)(4,1)S(1)} %get-tuple-element.305) | copy-start | bytes 100
  3.2 42.0 %copy-start.10 = (s32[32]{0:T(128)}, s32[32]{0:T(128)S(1)}, u32[]{:S(2)}) copy-start(s32[32]{0:T(128)S(1)} %get-tuple-element.307) | copy-start | bytes 388
  45.2 7.2 %copy-start = (s32[324,2048]{1,0:T(8,128)S(1)}, s32[324,2048]{1,0:T(8,128)}, u32[]{:S(2)}) copy-start(s32[324,2048]{1,0:T(8,128)} %param.16) | copy-start | bytes 7962628
  54.7 3.5 %copy-start.2 = (s32[4,20736]{1,0:T(4,128)S(1)}, s32[4,20736]{1,0:T(4,128)}, u32[]{:S(2)}) copy-start(s32[4,20736]{1,0:T(4,128)} %param.18) | copy-start | bytes 995332
  58.2 3.2 %copy-start.5 = (s32[4,324]{1,0:T(4,128)S(1)}, s32[4,324]{1,0:T(4,128)}, u32[]{:S(2)}) copy-start(s32[4,324]{1,0:T(4,128)} %param.17) | copy-start | bytes 15556
  58.3 5.4 %copy-start.4 = (bf16[324,324]{1,0:T(8,128)(2,1)S(1)}, bf16[324,324]{1,0:T(8,128)(2,1)}, u32[]{:S(2)}) copy-start(bf16[324,324]{1,0:T(8,128)(2,1)} %param.14) | copy-start | bytes 629860
  215.1 11.7 %copy-start.11 = (s32[32]{0:T(128)S(1)}, s32[32]{0:T(128)}, u32[]{:S(2)}) copy-start(s32[32]{0:T(128)} %copy-done.10) | copy-start | bytes 388
  215.1 12.4 %copy-start.7 = (pred[32]{0:T(512)(128)(4,1)S(1)}, pred[32]{0:T(512)(128)(4,1)}, u32[]{:S(2)}) copy-start(pred[32]{0:T(512)(128)(4,1)} %copy-done.6) | copy-start | bytes 100
  215.1 12.7 %copy-start.9 = (s32[32]{0:T(128)S(1)}, s32[32]{0:T(128)}, u32[]{:S(2)}) copy-start(s32[32]{0:T(128)} %copy-done.8) | copy-start | bytes 388
  215.1 12.9 %copy-start.1 = (bf16[256,256]{1,0:T(8,128)(2,1)S(1)}, bf16[256,256]{1,0:T(8,128)(2,1)}, u32[]{:S(2)}) copy-start(bf16[256,256]{1,0:T(8,128)(2,1)} %own_ref.1) | copy-start | bytes 393220
  215.2 12.9 %copy-start.3 = (f32[256,256]{1,0:T(8,128)S(1)}, f32[256,256]{1,0:T(8,128)}, u32[]{:S(2)}) copy-start(f32[256,256]{1,0:T(8,128)} %param.13) | copy-start | bytes 786436

commit v15 on v14

--- a/solution.py
+++ b/solution.py
@@ -112,14 +112,16 @@
     )(send)
 
 
-def spread_kernel(own_ref, out_ref, send_sem, recv_sem, local_sem):
-    count = lax.axis_size("alpha") * PAIR
+def spread_kernel(own_ref, out_ref, send_sem, recv_sem, local_sem, pair_send, pair_recv):
+    count = lax.axis_size("alpha")
     rows, cols = own_ref.shape
     group = lax.axis_index("g")
-    me = lax.axis_index("alpha") * PAIR + lax.axis_index("m")
+    member = lax.axis_index("m")
+    me = lax.axis_index("alpha")
+    other = 1 - member
 
     def window(slot):
-        return out_ref.at[pl.ds((slot // PAIR) * rows, rows), pl.ds((slot % PAIR) * cols, cols)]
+        return out_ref.at[pl.ds(slot * rows, rows), pl.ds(member * cols, cols)]
 
     def remote(slot, sem_slot, peer):
         return pltpu.make_async_remote_copy(
@@ -127,7 +129,7 @@
             dst_ref=window(slot),
             send_sem=send_sem.at[sem_slot],
             recv_sem=recv_sem.at[slot],
-            device_id=(peer // PAIR, group, peer % PAIR),
+            device_id=(peer, group, member),
             device_id_type=pl.DeviceIdType.MESH,
         )
 
@@ -143,6 +145,23 @@
     for step in range(1, count):
         src = lax.rem(me + count - step, count)
         remote(src, src, src).wait_recv()
+
+    def half(col):
+        return out_ref.at[:, pl.ds(col * cols, cols)]
+
+    def pair(col):
+        return pltpu.make_async_remote_copy(
+            src_ref=half(col),
+            dst_ref=half(col),
+            send_sem=pair_send,
+            recv_sem=pair_recv,
+            device_id=(me, group, other),
+            device_id_type=pl.DeviceIdType.MESH,
+        )
+
+    pair(member).start()
+    pair(member).wait_send()
+    pair(other).wait_recv()
 
 
 def spread(own, count):
@@ -154,8 +173,10 @@
         in_specs=[pl.BlockSpec(memory_space=pl.ANY)],
         out_specs=pl.BlockSpec(memory_space=pl.ANY),
         scratch_shapes=[
-            pltpu.SemaphoreType.DMA((count,)),
-            pltpu.SemaphoreType.DMA((count,)),
+            pltpu.SemaphoreType.DMA((count // PAIR,)),
+            pltpu.SemaphoreType.DMA((count // PAIR,)),
+            pltpu.SemaphoreType.DMA,
+            pltpu.SemaphoreType.DMA,
             pltpu.SemaphoreType.DMA,
         ],
         compiler_params=pltpu.CompilerParams(has_side_effects=True),

time: 230 us -> 221 us (0.961)
  Pallas kernels: 119 us -> 110 us
    pallas_call x1, Pallas kernels: 37.6 us -> 29.4 us  [spread(): pl.pallas_call(spread_kernel, out_shape=jax.ShapeDtypeStruct((count // PA...]
where the time goes in v15:
time: 221 us
  Pallas kernels  110 us (50%)
  local copies, waits for them, and re-layouts  85 us (38%)
  other arithmetic  17.5 us (8%)
  blocking collectives  3.96 us (2%)
  between operations  2.3 us (1%)
    gather x2, local copies, waits for them, and re-layouts, one_block(): lax.gather(coeff_ext, row_ids[:, :, None], dims, slice_sizes=(1, wide_col...  67.6 us
    pallas_call x2, Pallas kernels, mix_block(): pl.pallas_call(mix_kernel, out_shape=jax.ShapeDtypeStruct((rows, targets,...  44.3 us
    pallas_call x1, Pallas kernels, spread(): pl.pallas_call(spread_kernel, out_shape=jax.ShapeDtypeStruct((count // PA...  29.4 us
    pallas_call x2, Pallas kernels, exchange(): pl.pallas_call(exchange_kernel, out_shape=jax.ShapeDtypeStruct(send.shape...  26.8 us
    pallas_call x1, Pallas kernels, gather_alpha(): pl.pallas_call(gather_alpha_kernel, out_shape=jax.ShapeDtypeStruct((count...  9.9 us
    concatenate x1, other arithmetic, on_device(): jnp.concatenate([gathered, -gathered, jnp.zeros((16, wide_cols), jnp.bflo...  7.18 us
    while x2, local copies, waits for them, and re-layouts, on_device(): done = lax.fori_loop(0, my_count, one_block, empty)  5.8 us
    reshape x4, local copies, waits for them, and re-layouts, one_block(): part = summed.reshape(sub_rows, beta_size, local_cols).transpose(1, 0, 2)  5.22 us

profile of v15, /device:TPU:1, one launch (start us, length us, event | category | flops | bytes accessed | tf_op | source)
XLA Modules:
  0.0 220.7 jit_solution(8141745195592378824)
XLA Ops:
  0.0 0.7 compare_convert_fusion
  0.7 0.6 copy-done.8
  1.2 0.1 reshape.83
  1.3 0.2 reduce_window_sum.18
  1.5 0.1 eq.92
  1.6 0.7 broadcast_compare_fusion.1
  2.3 0.1 copy.24
  2.3 0.1 reduce-window.9
  2.4 0.1 reduce.18
  2.5 0.6 fusion.7
  3.8 0.8 iota_reduce_fusion
  5.3 0.1 select_reduce_fusion
  5.4 0.1 broadcast_in_dim.105
  5.5 0.1 convert_element_type.42
  5.6 29.4 %shard_map.82 = bf16[2048,512]{1,0:T(8,128)(2,1)} custom-call(bf16[256,256]{1,0:T(8,128)(2,1)} %own_ref.1), custom_call_target="tpu_custom_call" | custom-call | tf_op jit(solution)/shard_map/pallas_call | solution.py:168
  35.0 1.9 fusion.6
  37.0 0.0 copy-start
  37.0 7.2 %maximum_maximum_fusion = bf16[4112,512]{1,0:T(8,128)(2,1)} fusion(bf16[2048,512]{1,0:T(8,128)(2,1)S(1)} %get-tuple-element.301, bf16[2048,512]{1,0:T(8,128)(2,1)S(1)} %get-tuple-element.302, bf16[4112]{0:T(1024)(128)(2,1)S(1)} %pad.28.clone), kind=kLoop, calls=%fused_computation.11 | loop fusion | flops 12632064 | bytes 8413216 | tf_op jit(solution)/shard_map/concatenate | solution.py:260
  44.2 2.3 %copy.26 = s32[324,2048]{0,1:T(8,128)} copy(s32[324,2048]{1,0:T(8,128)S(1)} %copy-done) | data formatting | bytes 5308416 | tf_op jit(solution)/shard_map/while | solution.py:338
  46.5 3.5 %copy.27 = s32[324,2048]{0,1:T(8,128)} copy(s32[324,2048]{1,0:T(8,128)} %param.15) | data formatting | bytes 5308416 | tf_op jit(solution)/shard_map/while | solution.py:338
  50.0 0.1 convert_bitcast_fusion
  50.1 0.0 copy-start.4
  50.1 2.2 all-gather
  52.3 0.4 reshape.86
  52.7 0.3 copy.25
  53.0 0.2 copy.29
  53.2 1.8 all-gather.1
  55.1 0.1 eq.100
  55.1 0.1 eq.98
  55.2 0.2 bitcast_compare_fusion
  55.4 0.1 pad_convert_fusion
  55.6 150.5 %while.24 = (s32[]{:T(128)}, f32[4,64,256]{2,1,0:T(8,128)S(1)}, s32[]{:T(128)}, s32[]{:T(128)}, s32[32]{0:T(128)S(1)}, /*index=5*/s32[]{:T(128)}, s32[]{:T(128)}...) while((s32[]{:T(128)}, f32[4,64,256]{2,1,0:T(8,128)S(1)}, ...), condition=%wide.region_7.8_spmd, body=%wide.region_5.7_spmd.sunk | while | flops 177811 | bytes 25264532 | solution.py:338
  55.8 0.6 dynamic_slice.48
  56.9 0.8 fusion.9
  57.7 0.1 reshape.121
  57.9 33.8 %gather_fusion = bf16[10752,512]{1,0:T(8,128)(2,1)} fusion(bf16[4112,512]{1,0:T(8,128)(2,1)} %get-tuple-element.466, s32[11264]{0:T(1024)S(1)} %pad_clamp_fusion.3), kind=kCustom, calls=%fused_computation.clone.1 | custom fusion | bytes 22063104 | tf_op jit(solution)/shard_map/while/body/gather | solution.py:323
  91.6 22.1 %body.12 = f32[32,64,64]{2,1,0:T(8,128)} custom-call(bf16[336,336]{1,0:T(8,128)(2,1)S(1)} %get-tuple-element.467.integ_ref, bf16[32,336,512]{2,1,0:T(8,128)(2,1)} %bitcast.53, bf16[2,336,256]{2,1,0:T(8,128)(2,1)S(1)} %get-tuple-element.468.sign_ref, bf16[2,256,336]{2,1,0:T(8,128)(2,1)S(1)} %get-tuple-element.469.table_ref), custom_call_target="tpu_custom_call" | custom-call | tf_op jit(solution)/shard_map/while/body/pallas_call | solution.py:45
  113.8 1.5 reshape.122
  115.3 1.1 copy.33
  116.4 13.6 %body.13 = f32[16,32,256]{2,1,0:T(8,128)} custom-call(f32[16,32,256]{2,1,0:T(8,128)} %bitcast.54), custom_call_target="tpu_custom_call" | custom-call | tf_op jit(solution)/shard_map/while/body/pallas_call | solution.py:101
  130.0 1.1 bitcast_reduce_fusion.2
  131.1 0.6 dynamic_slice.48
  132.2 0.8 fusion.9
  133.1 0.1 reshape.121
  133.2 33.8 %gather_fusion = bf16[10752,512]{1,0:T(8,128)(2,1)} fusion(bf16[4112,512]{1,0:T(8,128)(2,1)} %get-tuple-element.466, s32[11264]{0:T(1024)S(1)} %pad_clamp_fusion.3), kind=kCustom, calls=%fused_computation.clone.1 | custom fusion | bytes 22063104 | tf_op jit(solution)/shard_map/while/body/gather | solution.py:323
  167.0 22.2 %body.12 = f32[32,64,64]{2,1,0:T(8,128)} custom-call(bf16[336,336]{1,0:T(8,128)(2,1)S(1)} %get-tuple-element.467.integ_ref, bf16[32,336,512]{2,1,0:T(8,128)(2,1)} %bitcast.53, bf16[2,336,256]{2,1,0:T(8,128)(2,1)S(1)} %get-tuple-element.468.sign_ref, bf16[2,256,336]{2,1,0:T(8,128)(2,1)S(1)} %get-tuple-element.469.table_ref), custom_call_target="tpu_custom_call" | custom-call | tf_op jit(solution)/shard_map/while/body/pallas_call | solution.py:45
  189.1 1.5 reshape.122
  190.7 1.1 copy.33
  191.8 13.2 %body.13 = f32[16,32,256]{2,1,0:T(8,128)} custom-call(f32[16,32,256]{2,1,0:T(8,128)} %bitcast.54), custom_call_target="tpu_custom_call" | custom-call | tf_op jit(solution)/shard_map/while/body/pallas_call | solution.py:101
  204.9 1.1 bitcast_reduce_fusion.2
  206.7 0.2 broadcast_in_dim.110
  207.0 11.7 %while.25 = (s32[]{:T(128)}, f32[3,8,64,256]{3,2,1,0:T(8,128)S(1)}, s32[]{:T(128)}, f32[4,64,256]{2,1,0:T(8,128)S(1)}, s32[]{:T(128)}, /*index=5*/s32[]{:T(128)}, s32[]{:T(128)}, s32[]{:T(128)}) while((s32[]{:T(128)}, f32[3,8,64,256]{3,2,1,0:T(8,128)S(1)}, s32[]{:T(128)}, f32[4,64,256]{2,1,0:T(8,128)S(1)}, s32[]{:T(128)}, ...), condition=%wide.region_9.10_spmd, body=%wide.region_8.9_spmd.sunk | while | flops 8 | bytes 1179817 | solution.py:345
  207.0 0.6 dynamic-slice_bitcast_fusion.2.own_ref
  207.6 9.9 %body.14 = f32[8,64,256]{2,1,0:T(8,128)} custom-call(f32[64,256]{1,0:T(8,128)} %dynamic-slice_bitcast_fusion.2.own_ref), custom_call_target="tpu_custom_call" | custom-call | tf_op jit(solution)/shard_map/while/body/pallas_call | solution.py:225
  217.5 1.1 bitcast_dynamic-update-slice_fusion.5
  218.7 0.1 compare_select_fusion
  218.8 0.6 gather_fusion.1
  219.4 0.1 dynamic_slice.34
  219.4 0.1 broadcast_in_dim.99
  219.5 0.1 broadcast_in_dim.100
  219.6 0.1 dynamic-slice_compare_fusion
  219.7 0.1 broadcast_in_dim.97
  219.8 0.1 eq.89
  219.9 0.8 fusion.2
  (39 shorter events, 0.2 us)
Async XLA Ops:
  0.7 0.6 copy-start.8
  2.3 34.7 %copy-start.6 = (pred[32]{0:T(512)(128)(4,1)}, pred[32]{0:T(512)(128)(4,1)S(1)}, u32[]{:S(2)}) copy-start(pred[32]{0:T(512)(128)(4,1)S(1)} %get-tuple-element.305) | copy-start | bytes 100
  3.2 33.8 %copy-start.10 = (s32[32]{0:T(128)}, s32[32]{0:T(128)S(1)}, u32[]{:S(2)}) copy-start(s32[32]{0:T(128)S(1)} %get-tuple-element.307) | copy-start | bytes 388
  37.0 7.2 %copy-start = (s32[324,2048]{1,0:T(8,128)S(1)}, s32[324,2048]{1,0:T(8,128)}, u32[]{:S(2)}) copy-start(s32[324,2048]{1,0:T(8,128)} %param.16) | copy-start | bytes 7962628
  46.5 3.5 %copy-start.2 = (s32[4,20736]{1,0:T(4,128)S(1)}, s32[4,20736]{1,0:T(4,128)}, u32[]{:S(2)}) copy-start(s32[4,20736]{1,0:T(4,128)} %param.18) | copy-start | bytes 995332
  50.0 3.2 %copy-start.5 = (s32[4,324]{1,0:T(4,128)S(1)}, s32[4,324]{1,0:T(4,128)}, u32[]{:S(2)}) copy-start(s32[4,324]{1,0:T(4,128)} %param.17) | copy-start | bytes 15556
  50.1 5.4 %copy-start.4 = (bf16[324,324]{1,0:T(8,128)(2,1)S(1)}, bf16[324,324]{1,0:T(8,128)(2,1)}, u32[]{:S(2)}) copy-start(bf16[324,324]{1,0:T(8,128)(2,1)} %param.14) | copy-start | bytes 629860
  206.9 11.7 %copy-start.11 = (s32[32]{0:T(128)S(1)}, s32[32]{0:T(128)}, u32[]{:S(2)}) copy-start(s32[32]{0:T(128)} %copy-done.10) | copy-start | bytes 388
  206.9 12.4 %copy-start.7 = (pred[32]{0:T(512)(128)(4,1)S(1)}, pred[32]{0:T(512)(128)(4,1)}, u32[]{:S(2)}) copy-start(pred[32]{0:T(512)(128)(4,1)} %copy-done.6) | copy-start | bytes 100
  206.9 12.7 %copy-start.9 = (s32[32]{0:T(128)S(1)}, s32[32]{0:T(128)}, u32[]{:S(2)}) copy-start(s32[32]{0:T(128)} %copy-done.8) | copy-start | bytes 388
  206.9 12.9 %copy-start.1 = (bf16[256,256]{1,0:T(8,128)(2,1)S(1)}, bf16[256,256]{1,0:T(8,128)(2,1)}, u32[]{:S(2)}) copy-start(bf16[256,256]{1,0:T(8,128)(2,1)} %own_ref.1) | copy-start | bytes 393220
  206.9 12.9 %copy-start.3 = (f32[256,256]{1,0:T(8,128)S(1)}, f32[256,256]{1,0:T(8,128)}, u32[]{:S(2)}) copy-start(f32[256,256]{1,0:T(8,128)} %param.13) | copy-start | bytes 786436

commit v16 on v15

--- a/solution.py
+++ b/solution.py
@@ -27,10 +27,8 @@
             )
             high = weighted.astype(jnp.bfloat16)
             low = (weighted - high.astype(jnp.float32)).astype(jnp.bfloat16)
-            table = table_ref[half]
-            res = jnp.dot(table, high, preferred_element_type=jnp.float32) + jnp.dot(
-                table, low, preferred_element_type=jnp.float32
-            )
+            stacked = jnp.concatenate([high, low], axis=0)
+            res = jnp.dot(table_ref[half], stacked, preferred_element_type=jnp.float32)
             for s in range(src_blocks):
                 lanes = (s // 2) * 2 * block_len
                 piece = res[s * targets : (s + 1) * targets, lanes : lanes + 2 * block_len]
@@ -278,6 +276,7 @@
         table_all.reshape(PAIR, src_blocks * total_blocks, pair_count),
         ((0, 0), (0, 0), (0, extra)),
     )
+    table_all = jnp.concatenate([table_all, table_all], axis=2)
 
     own_flags = lax.dynamic_slice_in_dim(live_flags, alpha_rank * per_device, per_device, 0)
 

time: 221 us -> 217 us (0.982)
  Pallas kernels: 110 us -> 106 us
    pallas_call x2, Pallas kernels: 44.3 us -> 39.7 us  [mix_block(): pl.pallas_call(mix_kernel, out_shape=jax.ShapeDtypeStruct((rows, targets,...]
where the time goes in v16:
time: 217 us; the launch traced here: 216 us
  Pallas kernels  106 us (49%)
  local copies, waits for them, and re-layouts  85 us (39%)
  other arithmetic  17.8 us (8%)
  blocking collectives  3.83 us (2%)
  between operations  2.3 us (1%)
    gather x2, local copies, waits for them, and re-layouts, one_block(): lax.gather(coeff_ext, row_ids[:, :, None], dims, slice_sizes=(1, wide_col...  67.6 us
    pallas_call x2, Pallas kernels, mix_block(): pl.pallas_call(mix_kernel, out_shape=jax.ShapeDtypeStruct((rows, targets,...  39.7 us
    pallas_call x1, Pallas kernels, spread(): pl.pallas_call(spread_kernel, out_shape=jax.ShapeDtypeStruct((count // PA...  29.4 us
    pallas_call x2, Pallas kernels, exchange(): pl.pallas_call(exchange_kernel, out_shape=jax.ShapeDtypeStruct(send.shape...  26.7 us
    pallas_call x1, Pallas kernels, gather_alpha(): pl.pallas_call(gather_alpha_kernel, out_shape=jax.ShapeDtypeStruct((count...  9.92 us
    concatenate x1, other arithmetic, on_device(): jnp.concatenate([gathered, -gathered, jnp.zeros((16, wide_cols), jnp.bflo...  7.18 us
    while x2, local copies, waits for them, and re-layouts, on_device(): done = lax.fori_loop(0, my_count, one_block, empty)  5.8 us
    reshape x4, local copies, waits for them, and re-layouts, one_block(): part = summed.reshape(sub_rows, beta_size, local_cols).transpose(1, 0, 2)  5.22 us

profile of v16, /device:TPU:1, one launch (start us, length us, event | category | flops | bytes accessed | tf_op | source)
XLA Modules:
  0.0 216.3 jit_solution(15221699463699202134)
XLA Ops:
  0.0 0.7 compare_convert_fusion
  0.7 0.6 copy-done.8
  1.2 0.1 reshape.83
  1.3 0.2 reduce_window_sum.18
  1.5 0.1 eq.92
  1.6 0.7 broadcast_compare_fusion.1
  2.3 0.1 copy.24
  2.3 0.1 reduce-window.9
  2.4 0.1 reduce.18
  2.5 0.6 fusion.7
  3.8 0.8 iota_reduce_fusion
  5.3 0.1 select_reduce_fusion
  5.4 0.1 broadcast_in_dim.105
  5.5 0.1 convert_element_type.42
  5.6 29.4 %shard_map.82 = bf16[2048,512]{1,0:T(8,128)(2,1)} custom-call(bf16[256,256]{1,0:T(8,128)(2,1)} %own_ref.1), custom_call_target="tpu_custom_call" | custom-call | tf_op jit(solution)/shard_map/pallas_call | solution.py:166
  35.0 1.9 fusion.6
  37.0 0.0 copy-start
  37.0 7.2 %maximum_maximum_fusion = bf16[4112,512]{1,0:T(8,128)(2,1)} fusion(bf16[2048,512]{1,0:T(8,128)(2,1)S(1)} %get-tuple-element.301, bf16[2048,512]{1,0:T(8,128)(2,1)S(1)} %get-tuple-element.302, bf16[4112]{0:T(1024)(128)(2,1)S(1)} %pad.27.clone), kind=kLoop, calls=%fused_computation.11 | loop fusion | flops 12632064 | bytes 8413216 | tf_op jit(solution)/shard_map/concatenate | solution.py:258
  44.2 2.3 %copy.26 = s32[324,2048]{0,1:T(8,128)} copy(s32[324,2048]{1,0:T(8,128)S(1)} %copy-done) | data formatting | bytes 5308416 | tf_op jit(solution)/shard_map/while | solution.py:337
  46.5 3.5 %copy.27 = s32[324,2048]{0,1:T(8,128)} copy(s32[324,2048]{1,0:T(8,128)} %param.15) | data formatting | bytes 5308416 | tf_op jit(solution)/shard_map/while | solution.py:337
  50.0 0.1 convert_bitcast_fusion
  50.1 2.0 all-gather
  52.1 0.4 reshape.86
  52.6 0.3 copy.25
  52.9 0.2 copy.29
  53.1 1.8 all-gather.1
  54.9 0.1 eq.100
  55.0 0.1 eq.98
  55.1 0.2 bitcast_compare_fusion
  55.3 0.1 pad.22
  55.3 0.4 add_convert_fusion
  55.8 145.9 %while.24 = (s32[]{:T(128)}, f32[4,64,256]{2,1,0:T(8,128)S(1)}, s32[]{:T(128)}, s32[]{:T(128)}, s32[32]{0:T(128)S(1)}, /*index=5*/s32[]{:T(128)}, s32[]{:T(128)}...) while((s32[]{:T(128)}, f32[4,64,256]{2,1,0:T(8,128)S(1)}, ...), condition=%wide.region_7.8_spmd, body=%wide.region_5.7_spmd.sunk | while | flops 177811 | bytes 25264532 | solution.py:337
  56.0 0.6 dynamic_slice.48
  57.1 0.8 fusion.9
  58.0 0.1 reshape.121
  58.1 33.8 %gather_fusion = bf16[10752,512]{1,0:T(8,128)(2,1)} fusion(bf16[4112,512]{1,0:T(8,128)(2,1)} %get-tuple-element.466, s32[11264]{0:T(1024)S(1)} %pad_clamp_fusion.3), kind=kCustom, calls=%fused_computation.clone.1 | custom fusion | bytes 22063104 | tf_op jit(solution)/shard_map/while/body/gather | solution.py:322
  91.9 19.9 %body.12 = f32[32,64,64]{2,1,0:T(8,128)} custom-call(bf16[336,336]{1,0:T(8,128)(2,1)S(1)} %get-tuple-element.467.integ_ref, bf16[32,336,512]{2,1,0:T(8,128)(2,1)} %bitcast.53, bf16[2,336,256]{2,1,0:T(8,128)(2,1)S(1)} %get-tuple-element.468.sign_ref, bf16[2,256,672]{2,1,0:T(8,128)(2,1)S(1)} %get-tuple-element.469.table_ref), custom_call_target="tpu_custom_call" | custom-call | tf_op jit(solution)/shard_map/while/body/pallas_call | solution.py:43
  111.7 1.5 reshape.122
  113.2 1.1 copy.33
  114.3 13.6 %body.13 = f32[16,32,256]{2,1,0:T(8,128)} custom-call(f32[16,32,256]{2,1,0:T(8,128)} %bitcast.54), custom_call_target="tpu_custom_call" | custom-call | tf_op jit(solution)/shard_map/while/body/pallas_call | solution.py:99
  127.9 1.1 bitcast_reduce_fusion.2
  129.0 0.6 dynamic_slice.48
  130.2 0.8 fusion.9
  131.0 0.1 reshape.121
  131.1 33.8 %gather_fusion = bf16[10752,512]{1,0:T(8,128)(2,1)} fusion(bf16[4112,512]{1,0:T(8,128)(2,1)} %get-tuple-element.466, s32[11264]{0:T(1024)S(1)} %pad_clamp_fusion.3), kind=kCustom, calls=%fused_computation.clone.1 | custom fusion | bytes 22063104 | tf_op jit(solution)/shard_map/while/body/gather | solution.py:322
  164.9 19.9 %body.12 = f32[32,64,64]{2,1,0:T(8,128)} custom-call(bf16[336,336]{1,0:T(8,128)(2,1)S(1)} %get-tuple-element.467.integ_ref, bf16[32,336,512]{2,1,0:T(8,128)(2,1)} %bitcast.53, bf16[2,336,256]{2,1,0:T(8,128)(2,1)S(1)} %get-tuple-element.468.sign_ref, bf16[2,256,672]{2,1,0:T(8,128)(2,1)S(1)} %get-tuple-element.469.table_ref), custom_call_target="tpu_custom_call" | custom-call | tf_op jit(solution)/shard_map/while/body/pallas_call | solution.py:43
  184.8 1.5 reshape.122
  186.3 1.1 copy.33
  187.4 13.2 %body.13 = f32[16,32,256]{2,1,0:T(8,128)} custom-call(f32[16,32,256]{2,1,0:T(8,128)} %bitcast.54), custom_call_target="tpu_custom_call" | custom-call | tf_op jit(solution)/shard_map/while/body/pallas_call | solution.py:99
  200.6 1.1 bitcast_reduce_fusion.2
  202.4 0.2 broadcast_in_dim.110
  202.6 11.7 %while.25 = (s32[]{:T(128)}, f32[3,8,64,256]{3,2,1,0:T(8,128)S(1)}, s32[]{:T(128)}, f32[4,64,256]{2,1,0:T(8,128)S(1)}, s32[]{:T(128)}, /*index=5*/s32[]{:T(128)}, s32[]{:T(128)}, s32[]{:T(128)}) while((s32[]{:T(128)}, f32[3,8,64,256]{3,2,1,0:T(8,128)S(1)}, s32[]{:T(128)}, f32[4,64,256]{2,1,0:T(8,128)S(1)}, s32[]{:T(128)}, ...), condition=%wide.region_9.10_spmd, body=%wide.region_8.9_spmd.sunk | while | flops 8 | bytes 1179817 | solution.py:344
  202.6 0.6 dynamic-slice_bitcast_fusion.2.own_ref
  203.3 9.9 %body.14 = f32[8,64,256]{2,1,0:T(8,128)} custom-call(f32[64,256]{1,0:T(8,128)} %dynamic-slice_bitcast_fusion.2.own_ref), custom_call_target="tpu_custom_call" | custom-call | tf_op jit(solution)/shard_map/while/body/pallas_call | solution.py:223
  213.2 1.1 bitcast_dynamic-update-slice_fusion.5
  214.3 0.1 compare_select_fusion
  214.4 0.6 gather_fusion.1
  215.0 0.1 dynamic_slice.34
  215.1 0.1 broadcast_in_dim.99
  215.2 0.1 broadcast_in_dim.100
  215.3 0.1 dynamic-slice_compare_fusion
  215.3 0.1 broadcast_in_dim.97
  215.4 0.1 eq.89
  215.5 0.8 fusion.2
  (40 shorter events, 0.2 us)
Async XLA Ops:
  0.7 0.6 copy-start.8
  2.3 34.7 %copy-start.6 = (pred[32]{0:T(512)(128)(4,1)}, pred[32]{0:T(512)(128)(4,1)S(1)}, u32[]{:S(2)}) copy-start(pred[32]{0:T(512)(128)(4,1)S(1)} %get-tuple-element.305) | copy-start | bytes 100
  3.2 33.8 %copy-start.10 = (s32[32]{0:T(128)}, s32[32]{0:T(128)S(1)}, u32[]{:S(2)}) copy-start(s32[32]{0:T(128)S(1)} %get-tuple-element.307) | copy-start | bytes 388
  37.0 7.2 %copy-start = (s32[324,2048]{1,0:T(8,128)S(1)}, s32[324,2048]{1,0:T(8,128)}, u32[]{:S(2)}) copy-start(s32[324,2048]{1,0:T(8,128)} %param.16) | copy-start | bytes 7962628
  46.5 3.5 %copy-start.2 = (s32[4,20736]{1,0:T(4,128)S(1)}, s32[4,20736]{1,0:T(4,128)}, u32[]{:S(2)}) copy-start(s32[4,20736]{1,0:T(4,128)} %param.18) | copy-start | bytes 995332
  50.0 3.1 %copy-start.5 = (s32[4,324]{1,0:T(4,128)S(1)}, s32[4,324]{1,0:T(4,128)}, u32[]{:S(2)}) copy-start(s32[4,324]{1,0:T(4,128)} %param.17) | copy-start | bytes 15556
  52.1 3.6 %copy-start.4 = (bf16[324,324]{1,0:T(8,128)(2,1)S(1)}, bf16[324,324]{1,0:T(8,128)(2,1)}, u32[]{:S(2)}) copy-start(bf16[324,324]{1,0:T(8,128)(2,1)} %param.14) | copy-start | bytes 629860
  202.5 11.8 %copy-start.11 = (s32[32]{0:T(128)S(1)}, s32[32]{0:T(128)}, u32[]{:S(2)}) copy-start(s32[32]{0:T(128)} %copy-done.10) | copy-start | bytes 388
  202.5 12.5 %copy-start.7 = (pred[32]{0:T(512)(128)(4,1)S(1)}, pred[32]{0:T(512)(128)(4,1)}, u32[]{:S(2)}) copy-start(pred[32]{0:T(512)(128)(4,1)} %copy-done.6) | copy-start | bytes 100
  202.6 12.7 %copy-start.9 = (s32[32]{0:T(128)S(1)}, s32[32]{0:T(128)}, u32[]{:S(2)}) copy-start(s32[32]{0:T(128)} %copy-done.8) | copy-start | bytes 388
  202.6 12.9 %copy-start.1 = (bf16[256,256]{1,0:T(8,128)(2,1)S(1)}, bf16[256,256]{1,0:T(8,128)(2,1)}, u32[]{:S(2)}) copy-start(bf16[256,256]{1,0:T(8,128)(2,1)} %own_ref.1) | copy-start | bytes 393220
  202.6 12.9 %copy-start.3 = (f32[256,256]{1,0:T(8,128)S(1)}, f32[256,256]{1,0:T(8,128)}, u32[]{:S(2)}) copy-start(f32[256,256]{1,0:T(8,128)} %param.13) | copy-start | bytes 786436

commit v17 on v16

--- a/solution.py
+++ b/solution.py
@@ -20,20 +20,23 @@
     integ = integ_ref[...]
     for row in range(picked_ref.shape[0]):
         mixed = jnp.dot(integ, picked_ref[row], preferred_element_type=jnp.float32)
-        folded = jnp.zeros((targets, 2 * block_len), jnp.float32)
+        parts = []
         for half in range(halves):
             weighted = mixed[:, half * width : (half + 1) * width] * sign_ref[half].astype(
                 jnp.float32
             )
             high = weighted.astype(jnp.bfloat16)
             low = (weighted - high.astype(jnp.float32)).astype(jnp.bfloat16)
-            stacked = jnp.concatenate([high, low], axis=0)
-            res = jnp.dot(table_ref[half], stacked, preferred_element_type=jnp.float32)
-            for s in range(src_blocks):
-                lanes = (s // 2) * 2 * block_len
-                piece = res[s * targets : (s + 1) * targets, lanes : lanes + 2 * block_len]
-                keep = upper if s % 2 else jnp.logical_not(upper)
-                folded = folded + jnp.where(keep, piece, 0.0)
+            parts += [high, low]
+        res = jnp.dot(
+            table_ref[...], jnp.concatenate(parts, axis=0), preferred_element_type=jnp.float32
+        )
+        folded = jnp.zeros((targets, 2 * block_len), jnp.float32)
+        for s in range(src_blocks):
+            lanes = (s // 2) * 2 * block_len
+            piece = res[s * targets : (s + 1) * targets, lanes : lanes + 2 * block_len]
+            keep = upper if s % 2 else jnp.logical_not(upper)
+            folded = folded + jnp.where(keep, piece, 0.0)
         folded = folded + pltpu.roll(folded, block_len, 1)
         out_ref[row] = folded[:, :block_len]
 
@@ -48,7 +51,7 @@
             pl.BlockSpec((pairs, pairs), lambda i: (0, 0)),
             pl.BlockSpec((ROWS, pairs, width), lambda i: (i, 0, 0)),
             pl.BlockSpec(sign_q.shape, lambda i: (0, 0, 0)),
-            pl.BlockSpec(table_all.shape, lambda i: (0, 0, 0)),
+            pl.BlockSpec(table_all.shape, lambda i: (0, 0)),
         ],
         out_specs=pl.BlockSpec((ROWS, targets, block_len), lambda i: (i, 0, 0)),
         compiler_params=pltpu.CompilerParams(dimension_semantics=("arbitrary",)),
@@ -276,7 +279,7 @@
         table_all.reshape(PAIR, src_blocks * total_blocks, pair_count),
         ((0, 0), (0, 0), (0, extra)),
     )
-    table_all = jnp.concatenate([table_all, table_all], axis=2)
+    table_all = jnp.concatenate([table_all[h] for h in range(PAIR) for _ in range(2)], axis=1)
 
     own_flags = lax.dynamic_slice_in_dim(live_flags, alpha_rank * per_device, per_device, 0)
 

time: 217 us -> 214 us (0.986)
  Pallas kernels: 106 us -> 101 us
    pallas_call x2, Pallas kernels: 39.7 us -> 35.4 us  [mix_block(): pl.pallas_call(mix_kernel, out_shape=jax.ShapeDtypeStruct((rows, targets,...]
where the time goes in v17:
time: 214 us
  Pallas kernels  101 us (47%)
  local copies, waits for them, and re-layouts  86.8 us (41%)
  other arithmetic  17.5 us (8%)
  blocking collectives  3.95 us (2%)
  between operations  2.3 us (1%)
    gather x2, local copies, waits for them, and re-layouts, one_block(): lax.gather(coeff_ext, row_ids[:, :, None], dims, slice_sizes=(1, wide_col...  67.6 us
    pallas_call x2, Pallas kernels, mix_block(): pl.pallas_call(mix_kernel, out_shape=jax.ShapeDtypeStruct((rows, targets,...  35.4 us
    pallas_call x1, Pallas kernels, spread(): pl.pallas_call(spread_kernel, out_shape=jax.ShapeDtypeStruct((count // PA...  29.4 us
    pallas_call x2, Pallas kernels, exchange(): pl.pallas_call(exchange_kernel, out_shape=jax.ShapeDtypeStruct(send.shape...  26.7 us
    pallas_call x1, Pallas kernels, gather_alpha(): pl.pallas_call(gather_alpha_kernel, out_shape=jax.ShapeDtypeStruct((count...  9.91 us
    concatenate x1, other arithmetic, on_device(): jnp.concatenate([gathered, -gathered, jnp.zeros((16, wide_cols), jnp.bflo...  7.18 us
    while x2, local copies, waits for them, and re-layouts, on_device(): done = lax.fori_loop(0, my_count, one_block, empty)  6.94 us
    reshape x4, local copies, waits for them, and re-layouts, one_block(): part = summed.reshape(sub_rows, beta_size, local_cols).transpose(1, 0, 2)  5.21 us

profile of v17, /device:TPU:1, one launch (start us, length us, event | category | flops | bytes accessed | tf_op | source)
XLA Modules:
  0.0 213.6 jit_solution(10001906353501282865)
XLA Ops:
  0.0 0.7 compare_convert_fusion
  0.7 0.6 copy-done.7
  1.2 0.1 reshape.83
  1.3 0.2 reduce_window_sum.18
  1.5 0.1 eq.92
  1.6 0.7 broadcast_compare_fusion.1
  2.3 0.1 copy.24
  2.3 0.1 reduce-window.9
  2.4 0.1 reduce.18
  2.5 0.6 fusion.7
  3.8 0.8 iota_reduce_fusion
  5.3 0.1 select_reduce_fusion
  5.4 0.1 broadcast_in_dim.105
  5.5 0.1 convert_element_type.42
  5.6 29.4 %shard_map.82 = bf16[2048,512]{1,0:T(8,128)(2,1)} custom-call(bf16[256,256]{1,0:T(8,128)(2,1)} %own_ref.1), custom_call_target="tpu_custom_call" | custom-call | tf_op jit(solution)/shard_map/pallas_call | solution.py:169
  35.0 1.9 fusion.6
  37.0 7.2 %maximum_maximum_fusion = bf16[4112,512]{1,0:T(8,128)(2,1)} fusion(bf16[2048,512]{1,0:T(8,128)(2,1)S(1)} %get-tuple-element.301, bf16[2048,512]{1,0:T(8,128)(2,1)S(1)} %get-tuple-element.302, bf16[4112]{0:T(1024)(128)(2,1)S(1)} %pad.28.clone), kind=kLoop, calls=%fused_computation.11 | loop fusion | flops 12632064 | bytes 8413216 | tf_op jit(solution)/shard_map/concatenate | solution.py:261
  44.2 1.8 all-gather.1
  46.0 0.1 eq.100
  46.1 0.1 eq.98
  46.2 0.2 bitcast_compare_fusion
  46.4 0.1 pad_convert_fusion
  46.5 0.6 concatenate.7
  47.1 3.5 %copy.26 = s32[324,2048]{0,1:T(8,128)} copy(s32[324,2048]{1,0:T(8,128)} %param.16) | data formatting | bytes 5308416 | tf_op jit(solution)/shard_map/while | solution.py:340
  50.6 3.5 %copy.27 = s32[324,2048]{0,1:T(8,128)} copy(s32[324,2048]{1,0:T(8,128)} %param.15) | data formatting | bytes 5308416 | tf_op jit(solution)/shard_map/while | solution.py:340
  54.0 0.1 convert_bitcast_fusion
  54.1 2.2 %all-gather = bf16[2,4,20736]{2,1,0:T(4,128)(2,1)S(1)} all-gather(bf16[1,4,20736]{2,1,0:T(4,128)(2,1)S(1)} %convert_bitcast_fusion), channel_id=1, replica_groups=mesh['alpha'=8,'g'=8,'m'=2] {'m'}, dimensions={0}, use_global_device_ids=true | all-gather | bytes 497664 | tf_op jit(solution)/shard_map/all_gather | solution.py:269
  56.3 0.4 reshape.86
  56.7 0.3 copy.25
  57.0 0.2 copy.29
  57.3 141.6 %while.24 = (s32[]{:T(128)}, f32[4,64,256]{2,1,0:T(8,128)S(1)}, s32[]{:T(128)}, s32[]{:T(128)}, s32[32]{0:T(128)S(1)}, /*index=5*/s32[]{:T(128)}, s32[]{:T(128)}...) while((s32[]{:T(128)}, f32[4,64,256]{2,1,0:T(8,128)S(1)}, ...), condition=%wide.region_7.8_spmd, body=%wide.region_5.7_spmd.sunk | while | flops 177811 | bytes 25264532 | solution.py:340
  57.5 0.6 dynamic_slice.48
  58.7 0.8 fusion.9
  59.5 0.1 reshape.121
  59.6 33.8 %gather_fusion = bf16[10752,512]{1,0:T(8,128)(2,1)} fusion(bf16[4112,512]{1,0:T(8,128)(2,1)} %get-tuple-element.468, s32[11264]{0:T(1024)S(1)} %pad_clamp_fusion.3), kind=kCustom, calls=%fused_computation.clone.1 | custom fusion | bytes 22063104 | tf_op jit(solution)/shard_map/while/body/gather | solution.py:325
  93.4 17.7 %body.12 = f32[32,64,64]{2,1,0:T(8,128)} custom-call(bf16[336,336]{1,0:T(8,128)(2,1)S(1)} %get-tuple-element.469.integ_ref, bf16[32,336,512]{2,1,0:T(8,128)(2,1)} %bitcast.57, bf16[2,336,256]{2,1,0:T(8,128)(2,1)S(1)} %get-tuple-element.470.sign_ref, bf16[256,1344]{1,0:T(8,128)(2,1)S(1)} %get-tuple-element.471.table_ref), custom_call_target="tpu_custom_call" | custom-call | tf_op jit(solution)/shard_map/while/body/pallas_call | solution.py:46
  111.1 1.5 reshape.122
  112.6 1.1 copy.33
  113.7 13.6 %body.13 = f32[16,32,256]{2,1,0:T(8,128)} custom-call(f32[16,32,256]{2,1,0:T(8,128)} %bitcast.58), custom_call_target="tpu_custom_call" | custom-call | tf_op jit(solution)/shard_map/while/body/pallas_call | solution.py:102
  127.3 1.1 bitcast_reduce_fusion.2
  128.4 0.6 dynamic_slice.48
  129.6 0.8 fusion.9
  130.4 0.1 reshape.121
  130.5 33.8 %gather_fusion = bf16[10752,512]{1,0:T(8,128)(2,1)} fusion(bf16[4112,512]{1,0:T(8,128)(2,1)} %get-tuple-element.468, s32[11264]{0:T(1024)S(1)} %pad_clamp_fusion.3), kind=kCustom, calls=%fused_computation.clone.1 | custom fusion | bytes 22063104 | tf_op jit(solution)/shard_map/while/body/gather | solution.py:325
  164.3 17.7 %body.12 = f32[32,64,64]{2,1,0:T(8,128)} custom-call(bf16[336,336]{1,0:T(8,128)(2,1)S(1)} %get-tuple-element.469.integ_ref, bf16[32,336,512]{2,1,0:T(8,128)(2,1)} %bitcast.57, bf16[2,336,256]{2,1,0:T(8,128)(2,1)S(1)} %get-tuple-element.470.sign_ref, bf16[256,1344]{1,0:T(8,128)(2,1)S(1)} %get-tuple-element.471.table_ref), custom_call_target="tpu_custom_call" | custom-call | tf_op jit(solution)/shard_map/while/body/pallas_call | solution.py:46
  182.0 1.5 reshape.122
  183.5 1.1 copy.33
  184.6 13.2 %body.13 = f32[16,32,256]{2,1,0:T(8,128)} custom-call(f32[16,32,256]{2,1,0:T(8,128)} %bitcast.58), custom_call_target="tpu_custom_call" | custom-call | tf_op jit(solution)/shard_map/while/body/pallas_call | solution.py:102
  197.8 1.1 bitcast_reduce_fusion.2
  199.6 0.2 broadcast_in_dim.110
  199.8 0.0 copy-start
  199.8 11.7 %while.25 = (s32[]{:T(128)}, f32[3,8,64,256]{3,2,1,0:T(8,128)S(1)}, s32[]{:T(128)}, f32[4,64,256]{2,1,0:T(8,128)S(1)}, s32[]{:T(128)}, /*index=5*/s32[]{:T(128)}, s32[]{:T(128)}, s32[]{:T(128)}) while((s32[]{:T(128)}, f32[3,8,64,256]{3,2,1,0:T(8,128)S(1)}, s32[]{:T(128)}, f32[4,64,256]{2,1,0:T(8,128)S(1)}, s32[]{:T(128)}, ...), condition=%wide.region_9.10_spmd, body=%wide.region_8.9_spmd.sunk | while | flops 8 | bytes 1179817 | solution.py:347
  199.8 0.6 dynamic-slice_bitcast_fusion.2.own_ref
  200.5 9.9 %body.14 = f32[8,64,256]{2,1,0:T(8,128)} custom-call(f32[64,256]{1,0:T(8,128)} %dynamic-slice_bitcast_fusion.2.own_ref), custom_call_target="tpu_custom_call" | custom-call | tf_op jit(solution)/shard_map/while/body/pallas_call | solution.py:226
  210.4 1.1 bitcast_dynamic-update-slice_fusion.5
  211.5 0.1 compare_select_fusion
  211.6 0.6 gather_fusion.1
  212.2 0.1 dynamic_slice.34
  212.3 0.1 broadcast_in_dim.99
  212.4 0.1 broadcast_in_dim.100
  212.5 0.1 dynamic-slice_compare_fusion
  212.6 0.1 broadcast_in_dim.97
  212.6 0.1 eq.89
  212.7 0.8 fusion.2
  (39 shorter events, 0.3 us)
Async XLA Ops:
  0.7 0.6 copy-start.7
  2.3 34.7 %copy-start.5 = (pred[32]{0:T(512)(128)(4,1)}, pred[32]{0:T(512)(128)(4,1)S(1)}, u32[]{:S(2)}) copy-start(pred[32]{0:T(512)(128)(4,1)S(1)} %get-tuple-element.307) | copy-start | bytes 100
  3.2 33.8 %copy-start.9 = (s32[32]{0:T(128)}, s32[32]{0:T(128)S(1)}, u32[]{:S(2)}) copy-start(s32[32]{0:T(128)S(1)} %get-tuple-element.309) | copy-start | bytes 388
  37.0 7.2 %copy-start.4 = (s32[4,324]{1,0:T(4,128)S(1)}, s32[4,324]{1,0:T(4,128)}, u32[]{:S(2)}) copy-start(s32[4,324]{1,0:T(4,128)} %param.17) | copy-start | bytes 15556
  50.6 3.5 %copy-start.1 = (s32[4,20736]{1,0:T(4,128)S(1)}, s32[4,20736]{1,0:T(4,128)}, u32[]{:S(2)}) copy-start(s32[4,20736]{1,0:T(4,128)} %param.18) | copy-start | bytes 995332
  54.0 3.2 %copy-start.3 = (bf16[324,324]{1,0:T(8,128)(2,1)S(1)}, bf16[324,324]{1,0:T(8,128)(2,1)}, u32[]{:S(2)}) copy-start(bf16[324,324]{1,0:T(8,128)(2,1)} %param.14) | copy-start | bytes 629860
  199.8 11.8 %copy-start.10 = (s32[32]{0:T(128)S(1)}, s32[32]{0:T(128)}, u32[]{:S(2)}) copy-start(s32[32]{0:T(128)} %copy-done.9) | copy-start | bytes 388
  199.8 12.5 %copy-start.6 = (pred[32]{0:T(512)(128)(4,1)S(1)}, pred[32]{0:T(512)(128)(4,1)}, u32[]{:S(2)}) copy-start(pred[32]{0:T(512)(128)(4,1)} %copy-done.5) | copy-start | bytes 100
  199.8 12.7 %copy-start.8 = (s32[32]{0:T(128)S(1)}, s32[32]{0:T(128)}, u32[]{:S(2)}) copy-start(s32[32]{0:T(128)} %copy-done.7) | copy-start | bytes 388
  199.8 12.9 %copy-start = (bf16[256,256]{1,0:T(8,128)(2,1)S(1)}, bf16[256,256]{1,0:T(8,128)(2,1)}, u32[]{:S(2)}) copy-start(bf16[256,256]{1,0:T(8,128)(2,1)} %own_ref.1) | copy-start | bytes 393220
  199.8 12.9 %copy-start.2 = (f32[256,256]{1,0:T(8,128)S(1)}, f32[256,256]{1,0:T(8,128)}, u32[]{:S(2)}) copy-start(f32[256,256]{1,0:T(8,128)} %param.13) | copy-start | bytes 786436

commit v18 on v17

--- a/solution.py
+++ b/solution.py
@@ -349,7 +349,10 @@
     ).reshape((per_device - 1) * alpha_size, block_len, local_cols)
     own_rank = lax.dynamic_slice_in_dim(extra_rank, alpha_rank * per_device, per_device, 0)
     pick = jnp.minimum(own_rank // alpha_size, per_device - 2) * alpha_size + own_rank % alpha_size
-    placed = jnp.where(own_first[:, None, None], done[0][None], everyone[pick])
+    chosen = jnp.stack(
+        [lax.dynamic_index_in_dim(everyone, pick[b], 0, keepdims=False) for b in range(per_device)]
+    )
+    placed = jnp.where(own_first[:, None, None], done[0][None], chosen)
     placed = placed.reshape(local_rows, local_cols)
     own_live_rows = jnp.repeat(own_flags, block_len)
     total = diagonal * coefficients.astype(jnp.float32) + placed

time: 214 us -> 222 us (1.037)
  between operations: 2.3 us -> 9.9 us
where the time goes in v18:
time: 222 us; the launch traced here: 221 us
  Pallas kernels  101 us (45%)
  local copies, waits for them, and re-layouts  86.9 us (39%)
  other arithmetic  17.5 us (8%)
  between operations  9.9 us (4%)
  blocking collectives  3.95 us (2%)
    gather x2, local copies, waits for them, and re-layouts, one_block(): lax.gather(coeff_ext, row_ids[:, :, None], dims, slice_sizes=(1, wide_col...  67.6 us
    pallas_call x2, Pallas kernels, mix_block(): pl.pallas_call(mix_kernel, out_shape=jax.ShapeDtypeStruct((rows, targets,...  35.4 us
    pallas_call x1, Pallas kernels, spread(): pl.pallas_call(spread_kernel, out_shape=jax.ShapeDtypeStruct((count // PA...  29.4 us
    pallas_call x2, Pallas kernels, exchange(): pl.pallas_call(exchange_kernel, out_shape=jax.ShapeDtypeStruct(send.shape...  26.7 us
    pallas_call x1, Pallas kernels, gather_alpha(): pl.pallas_call(gather_alpha_kernel, out_shape=jax.ShapeDtypeStruct((count...  9.91 us
    concatenate x1, other arithmetic, on_device(): jnp.concatenate([gathered, -gathered, jnp.zeros((16, wide_cols), jnp.bflo...  7.18 us
    while x2, local copies, waits for them, and re-layouts, on_device(): done = lax.fori_loop(0, my_count, one_block, empty)  6.94 us
    reshape x4, local copies, waits for them, and re-layouts, one_block(): part = summed.reshape(sub_rows, beta_size, local_cols).transpose(1, 0, 2)  5.21 us

profile of v18, /device:TPU:1, one launch (start us, length us, event | category | flops | bytes accessed | tf_op | source)
XLA Modules:
  0.0 221.3 jit_solution(231088117835412784)
XLA Ops:
  0.0 0.7 compare_convert_fusion
  0.7 0.6 copy-done.7
  1.2 0.1 reshape.83
  1.3 0.2 reduce_window_sum.18
  1.5 0.1 eq.92
  1.6 0.7 broadcast_compare_fusion.1
  2.3 0.1 copy.24
  2.3 0.1 reduce-window.9
  2.4 0.1 reduce.18
  2.5 0.6 fusion.8
  3.8 0.8 iota_reduce_fusion
  5.3 0.1 select_reduce_fusion
  5.4 0.1 broadcast_in_dim.102
  5.5 0.1 convert_element_type.42
  5.6 29.4 %shard_map.82 = bf16[2048,512]{1,0:T(8,128)(2,1)} custom-call(bf16[256,256]{1,0:T(8,128)(2,1)} %own_ref.1), custom_call_target="tpu_custom_call" | custom-call | tf_op jit(solution)/shard_map/pallas_call | solution.py:169
  35.0 1.9 fusion.6
  37.0 7.2 %maximum_maximum_fusion = bf16[4112,512]{1,0:T(8,128)(2,1)} fusion(bf16[2048,512]{1,0:T(8,128)(2,1)S(1)} %get-tuple-element.301, bf16[2048,512]{1,0:T(8,128)(2,1)S(1)} %get-tuple-element.302, bf16[4112]{0:T(1024)(128)(2,1)S(1)} %pad.32.clone), kind=kLoop, calls=%fused_computation.10 | loop fusion | flops 12632064 | bytes 8413216 | tf_op jit(solution)/shard_map/concatenate | solution.py:261
  44.2 1.8 all-gather.1
  46.0 0.1 eq.100
  46.1 0.1 eq.98
  46.2 0.2 bitcast_compare_fusion
  46.4 0.1 pad_convert_fusion
  46.5 0.6 concatenate.7
  47.1 3.5 %copy.26 = s32[324,2048]{0,1:T(8,128)} copy(s32[324,2048]{1,0:T(8,128)} %param.16) | data formatting | bytes 5308416 | tf_op jit(solution)/shard_map/while | solution.py:340
  50.6 3.5 %copy.27 = s32[324,2048]{0,1:T(8,128)} copy(s32[324,2048]{1,0:T(8,128)} %param.15) | data formatting | bytes 5308416 | tf_op jit(solution)/shard_map/while | solution.py:340
  54.0 0.1 convert_bitcast_fusion
  54.1 2.2 all-gather
  56.3 0.4 reshape.86
  56.7 0.3 copy.25
  57.0 0.2 copy.29
  57.3 141.6 %while.24 = (s32[]{:T(128)}, f32[4,64,256]{2,1,0:T(8,128)S(1)}, s32[]{:T(128)}, s32[]{:T(128)}, s32[32]{0:T(128)S(1)}, /*index=5*/s32[]{:T(128)}, s32[]{:T(128)}...) while((s32[]{:T(128)}, f32[4,64,256]{2,1,0:T(8,128)S(1)}, ...), condition=%wide.region_7.8_spmd, body=%wide.region_5.7_spmd.sunk | while | flops 177811 | bytes 25264532 | solution.py:340
  57.5 0.6 dynamic_slice.69
  58.7 0.8 fusion.10
  59.5 0.1 reshape.112
  59.6 33.8 %gather_fusion = bf16[10752,512]{1,0:T(8,128)(2,1)} fusion(bf16[4112,512]{1,0:T(8,128)(2,1)} %get-tuple-element.476, s32[11264]{0:T(1024)S(1)} %pad_clamp_fusion.2), kind=kCustom, calls=%fused_computation.clone.1 | custom fusion | bytes 22063104 | tf_op jit(solution)/shard_map/while/body/gather | solution.py:325
  93.4 17.7 %body.12 = f32[32,64,64]{2,1,0:T(8,128)} custom-call(bf16[336,336]{1,0:T(8,128)(2,1)S(1)} %get-tuple-element.477.integ_ref, bf16[32,336,512]{2,1,0:T(8,128)(2,1)} %bitcast.61, bf16[2,336,256]{2,1,0:T(8,128)(2,1)S(1)} %get-tuple-element.478.sign_ref, bf16[256,1344]{1,0:T(8,128)(2,1)S(1)} %get-tuple-element.479.table_ref), custom_call_target="tpu_custom_call" | custom-call | tf_op jit(solution)/shard_map/while/body/pallas_call | solution.py:46
  111.1 1.5 reshape.113
  112.6 1.1 copy.33
  113.7 13.6 %body.13 = f32[16,32,256]{2,1,0:T(8,128)} custom-call(f32[16,32,256]{2,1,0:T(8,128)} %bitcast.62), custom_call_target="tpu_custom_call" | custom-call | tf_op jit(solution)/shard_map/while/body/pallas_call | solution.py:102
  127.3 1.1 bitcast_reduce_fusion.2
  128.4 0.6 dynamic_slice.69
  129.6 0.8 fusion.10
  130.4 0.1 reshape.112
  130.5 33.8 %gather_fusion = bf16[10752,512]{1,0:T(8,128)(2,1)} fusion(bf16[4112,512]{1,0:T(8,128)(2,1)} %get-tuple-element.476, s32[11264]{0:T(1024)S(1)} %pad_clamp_fusion.2), kind=kCustom, calls=%fused_computation.clone.1 | custom fusion | bytes 22063104 | tf_op jit(solution)/shard_map/while/body/gather | solution.py:325
  164.3 17.7 %body.12 = f32[32,64,64]{2,1,0:T(8,128)} custom-call(bf16[336,336]{1,0:T(8,128)(2,1)S(1)} %get-tuple-element.477.integ_ref, bf16[32,336,512]{2,1,0:T(8,128)(2,1)} %bitcast.61, bf16[2,336,256]{2,1,0:T(8,128)(2,1)S(1)} %get-tuple-element.478.sign_ref, bf16[256,1344]{1,0:T(8,128)(2,1)S(1)} %get-tuple-element.479.table_ref), custom_call_target="tpu_custom_call" | custom-call | tf_op jit(solution)/shard_map/while/body/pallas_call | solution.py:46
  182.0 1.5 reshape.113
  183.5 1.1 copy.33
  184.6 13.2 %body.13 = f32[16,32,256]{2,1,0:T(8,128)} custom-call(f32[16,32,256]{2,1,0:T(8,128)} %bitcast.62), custom_call_target="tpu_custom_call" | custom-call | tf_op jit(solution)/shard_map/while/body/pallas_call | solution.py:102
  197.8 1.1 bitcast_reduce_fusion.2
  199.6 0.2 broadcast_in_dim.107
  199.8 0.0 copy-start
  199.8 11.7 %while.25 = (s32[]{:T(128)}, f32[3,8,64,256]{3,2,1,0:T(8,128)S(1)}, s32[]{:T(128)}, f32[4,64,256]{2,1,0:T(8,128)S(1)}, s32[]{:T(128)}, /*index=5*/s32[]{:T(128)}, s32[]{:T(128)}, s32[]{:T(128)}) while((s32[]{:T(128)}, f32[3,8,64,256]{3,2,1,0:T(8,128)S(1)}, s32[]{:T(128)}, f32[4,64,256]{2,1,0:T(8,128)S(1)}, s32[]{:T(128)}, ...), condition=%wide.region_9.10_spmd, body=%wide.region_8.9_spmd.sunk | while | flops 8 | bytes 1179817 | solution.py:347
  199.8 0.6 dynamic-slice_bitcast_fusion.2.own_ref
  200.5 9.9 %body.14 = f32[8,64,256]{2,1,0:T(8,128)} custom-call(f32[64,256]{1,0:T(8,128)} %dynamic-slice_bitcast_fusion.2.own_ref), custom_call_target="tpu_custom_call" | custom-call | tf_op jit(solution)/shard_map/while/body/pallas_call | solution.py:226
  210.4 1.1 bitcast_dynamic-update-slice_fusion.5
  211.5 0.1 fusion.4
  211.6 0.7 fusion.7
  220.0 0.1 dynamic_slice.47
  220.0 0.1 broadcast_in_dim.96
  220.1 0.1 broadcast_in_dim.97
  220.2 0.1 dynamic-slice_compare_fusion
  220.3 0.1 broadcast_in_dim.94
  220.4 0.1 eq.89
  220.5 0.8 fusion.2
  (40 shorter events, 0.3 us)
Async XLA Ops:
  0.7 0.6 copy-start.7
  2.3 34.7 %copy-start.5 = (pred[32]{0:T(512)(128)(4,1)}, pred[32]{0:T(512)(128)(4,1)S(1)}, u32[]{:S(2)}) copy-start(pred[32]{0:T(512)(128)(4,1)S(1)} %get-tuple-element.311) | copy-start | bytes 100
  3.2 33.8 %copy-start.9 = (s32[32]{0:T(128)}, s32[32]{0:T(128)S(1)}, u32[]{:S(2)}) copy-start(s32[32]{0:T(128)S(1)} %get-tuple-element.317) | copy-start | bytes 388
  37.0 7.2 %copy-start.4 = (s32[4,324]{1,0:T(4,128)S(1)}, s32[4,324]{1,0:T(4,128)}, u32[]{:S(2)}) copy-start(s32[4,324]{1,0:T(4,128)} %param.17) | copy-start | bytes 15556
  50.6 3.5 %copy-start.1 = (s32[4,20736]{1,0:T(4,128)S(1)}, s32[4,20736]{1,0:T(4,128)}, u32[]{:S(2)}) copy-start(s32[4,20736]{1,0:T(4,128)} %param.18) | copy-start | bytes 995332
  54.0 3.2 %copy-start.3 = (bf16[324,324]{1,0:T(8,128)(2,1)S(1)}, bf16[324,324]{1,0:T(8,128)(2,1)}, u32[]{:S(2)}) copy-start(bf16[324,324]{1,0:T(8,128)(2,1)} %param.14) | copy-start | bytes 629860
  199.8 11.8 %copy-start.10 = (s32[32]{0:T(128)S(1)}, s32[32]{0:T(128)}, u32[]{:S(2)}) copy-start(s32[32]{0:T(128)} %copy-done.9) | copy-start | bytes 388
  199.8 20.2 %copy-start.6 = (pred[32]{0:T(512)(128)(4,1)S(1)}, pred[32]{0:T(512)(128)(4,1)}, u32[]{:S(2)}) copy-start(pred[32]{0:T(512)(128)(4,1)} %copy-done.5) | copy-start | bytes 100
  199.8 20.4 %copy-start.8 = (s32[32]{0:T(128)S(1)}, s32[32]{0:T(128)}, u32[]{:S(2)}) copy-start(s32[32]{0:T(128)} %copy-done.7) | copy-start | bytes 388
  199.8 20.7 %copy-start = (bf16[256,256]{1,0:T(8,128)(2,1)S(1)}, bf16[256,256]{1,0:T(8,128)(2,1)}, u32[]{:S(2)}) copy-start(bf16[256,256]{1,0:T(8,128)(2,1)} %own_ref.1) | copy-start | bytes 393220
  199.8 20.7 %copy-start.2 = (f32[256,256]{1,0:T(8,128)S(1)}, f32[256,256]{1,0:T(8,128)}, u32[]{:S(2)}) copy-start(f32[256,256]{1,0:T(8,128)} %param.13) | copy-start | bytes 786436

commit v19 on v17

--- a/solution.py
+++ b/solution.py
@@ -264,9 +264,10 @@
     zero_row = 2 * window_rows
 
     integ_pad = jnp.pad(integrals, ((0, extra), (0, extra)))
-    beta_block2 = lax.all_gather(beta_block.astype(jnp.bfloat16), "m", axis=0, tiled=True)
-    beta_block2 = beta_block2.astype(jnp.int32)
-    beta_sign2 = lax.all_gather(beta_sign.astype(jnp.bfloat16), "m", axis=0, tiled=True)
+    tables_both = jnp.concatenate([beta_sign, beta_block], axis=1).astype(jnp.bfloat16)
+    tables_both = lax.all_gather(tables_both, "m", axis=0, tiled=True)
+    beta_sign2 = tables_both[:, : beta_sign.shape[1]]
+    beta_block2 = tables_both[:, beta_sign.shape[1] :].astype(jnp.int32)
     sign_q = (
         beta_sign2.reshape(PAIR, src_blocks, pair_count, block_len)
         .transpose(0, 2, 1, 3)

time: 214 us -> 213 us (level)
  no operation moved by 1% of the time
where the time goes in v19:
time: 213 us; the launch traced here: 212 us
  Pallas kernels  101 us (47%)
  local copies, waits for them, and re-layouts  86.8 us (41%)
  other arithmetic  17.6 us (8%)
  between operations  2.34 us (1%)
    gather x2, local copies, waits for them, and re-layouts, one_block(): lax.gather(coeff_ext, row_ids[:, :, None], dims, slice_sizes=(1, wide_col...  67.6 us
    pallas_call x2, Pallas kernels, mix_block(): pl.pallas_call(mix_kernel, out_shape=jax.ShapeDtypeStruct((rows, targets,...  35.4 us
    pallas_call x1, Pallas kernels, spread(): pl.pallas_call(spread_kernel, out_shape=jax.ShapeDtypeStruct((count // PA...  29.4 us
    pallas_call x2, Pallas kernels, exchange(): pl.pallas_call(exchange_kernel, out_shape=jax.ShapeDtypeStruct(send.shape...  26.7 us
    pallas_call x1, Pallas kernels, gather_alpha(): pl.pallas_call(gather_alpha_kernel, out_shape=jax.ShapeDtypeStruct((count...  9.91 us
    concatenate x1, other arithmetic, on_device(): jnp.concatenate([gathered, -gathered, jnp.zeros((16, wide_cols), jnp.bflo...  7.18 us
    while x2, local copies, waits for them, and re-layouts, on_device(): done = lax.fori_loop(0, my_count, one_block, empty)  6.94 us
    reshape x4, local copies, waits for them, and re-layouts, one_block(): part = summed.reshape(sub_rows, beta_size, local_cols).transpose(1, 0, 2)  5.21 us

profile of v19, /device:TPU:1, one launch (start us, length us, event | category | flops | bytes accessed | tf_op | source)
XLA Modules:
  0.0 211.8 jit_solution(6000224421130743779)
XLA Ops:
  0.0 0.7 compare_convert_fusion
  0.7 0.6 copy-done.7
  1.2 0.1 reshape.83
  1.3 0.2 reduce_window_sum.18
  1.5 0.1 eq.92
  1.6 0.7 broadcast_compare_fusion.1
  2.3 0.1 copy.23
  2.3 0.1 reduce-window.9
  2.4 0.1 reduce.18
  2.5 0.6 fusion.7
  3.8 0.8 iota_reduce_fusion
  5.3 0.1 select_reduce_fusion
  5.4 0.1 broadcast_in_dim.105
  5.5 0.1 convert_element_type.37
  5.6 29.4 %shard_map.82 = bf16[2048,512]{1,0:T(8,128)(2,1)} custom-call(bf16[256,256]{1,0:T(8,128)(2,1)} %own_ref.1), custom_call_target="tpu_custom_call" | custom-call | tf_op jit(solution)/shard_map/pallas_call | solution.py:169
  35.0 1.9 fusion.6
  37.0 7.2 %maximum_maximum_fusion = bf16[4112,512]{1,0:T(8,128)(2,1)} fusion(bf16[2048,512]{1,0:T(8,128)(2,1)S(1)} %get-tuple-element.301, bf16[2048,512]{1,0:T(8,128)(2,1)S(1)} %get-tuple-element.302, bf16[4112]{0:T(1024)(128)(2,1)S(1)} %pad.30.clone), kind=kLoop, calls=%fused_computation.11 | loop fusion | flops 12632064 | bytes 8413216 | tf_op jit(solution)/shard_map/concatenate | solution.py:261
  44.2 0.1 convert.8
  44.3 0.1 maximum_bitcast_fusion
  44.4 2.0 all-gather
  46.4 0.1 reshape.109
  46.6 0.1 eq.100
  46.6 0.1 eq.98
  46.7 0.2 bitcast_compare_fusion
  46.9 0.1 pad_convert_fusion
  47.0 0.6 concatenate.12
  47.7 0.4 reshape.86
  48.1 0.3 copy.24
  48.4 0.2 copy.28
  48.6 3.5 %copy.25 = s32[324,2048]{0,1:T(8,128)} copy(s32[324,2048]{1,0:T(8,128)} %param.16) | data formatting | bytes 5308416 | tf_op jit(solution)/shard_map/while | solution.py:341
  52.1 3.5 %copy.26 = s32[324,2048]{0,1:T(8,128)} copy(s32[324,2048]{1,0:T(8,128)} %param.15) | data formatting | bytes 5308416 | tf_op jit(solution)/shard_map/while | solution.py:341
  55.6 141.5 %while.24 = (s32[]{:T(128)}, f32[4,64,256]{2,1,0:T(8,128)S(1)}, s32[]{:T(128)}, s32[]{:T(128)}, s32[32]{0:T(128)S(1)}, /*index=5*/s32[]{:T(128)}, s32[]{:T(128)}...) while((s32[]{:T(128)}, f32[4,64,256]{2,1,0:T(8,128)S(1)}, ...), condition=%wide.region_7.8_spmd, body=%wide.region_5.7_spmd.sunk | while | flops 177811 | bytes 25264532 | solution.py:341
  55.8 0.6 dynamic_slice.48
  56.9 0.8 fusion.9
  57.8 0.1 reshape.117
  57.9 33.8 %gather_fusion = bf16[10752,512]{1,0:T(8,128)(2,1)} fusion(bf16[4112,512]{1,0:T(8,128)(2,1)} %get-tuple-element.468, s32[11264]{0:T(1024)S(1)} %pad_clamp_fusion.3), kind=kCustom, calls=%fused_computation.clone.1 | custom fusion | bytes 22063104 | tf_op jit(solution)/shard_map/while/body/gather | solution.py:326
  91.7 17.7 %body.12 = f32[32,64,64]{2,1,0:T(8,128)} custom-call(bf16[336,336]{1,0:T(8,128)(2,1)S(1)} %get-tuple-element.469.integ_ref, bf16[32,336,512]{2,1,0:T(8,128)(2,1)} %bitcast.55, bf16[2,336,256]{2,1,0:T(8,128)(2,1)S(1)} %get-tuple-element.470.sign_ref, bf16[256,1344]{1,0:T(8,128)(2,1)S(1)} %get-tuple-element.471.table_ref), custom_call_target="tpu_custom_call" | custom-call | tf_op jit(solution)/shard_map/while/body/pallas_call | solution.py:46
  109.4 1.5 reshape.118
  110.9 1.1 copy.32
  112.0 13.5 %body.13 = f32[16,32,256]{2,1,0:T(8,128)} custom-call(f32[16,32,256]{2,1,0:T(8,128)} %bitcast.56), custom_call_target="tpu_custom_call" | custom-call | tf_op jit(solution)/shard_map/while/body/pallas_call | solution.py:102
  125.5 1.1 bitcast_reduce_fusion.2
  126.7 0.6 dynamic_slice.48
  127.8 0.8 fusion.9
  128.6 0.1 reshape.117
  128.8 33.8 %gather_fusion = bf16[10752,512]{1,0:T(8,128)(2,1)} fusion(bf16[4112,512]{1,0:T(8,128)(2,1)} %get-tuple-element.468, s32[11264]{0:T(1024)S(1)} %pad_clamp_fusion.3), kind=kCustom, calls=%fused_computation.clone.1 | custom fusion | bytes 22063104 | tf_op jit(solution)/shard_map/while/body/gather | solution.py:326
  162.5 17.7 %body.12 = f32[32,64,64]{2,1,0:T(8,128)} custom-call(bf16[336,336]{1,0:T(8,128)(2,1)S(1)} %get-tuple-element.469.integ_ref, bf16[32,336,512]{2,1,0:T(8,128)(2,1)} %bitcast.55, bf16[2,336,256]{2,1,0:T(8,128)(2,1)S(1)} %get-tuple-element.470.sign_ref, bf16[256,1344]{1,0:T(8,128)(2,1)S(1)} %get-tuple-element.471.table_ref), custom_call_target="tpu_custom_call" | custom-call | tf_op jit(solution)/shard_map/while/body/pallas_call | solution.py:46
  180.2 1.5 reshape.118
  181.8 1.1 copy.32
  182.9 13.1 %body.13 = f32[16,32,256]{2,1,0:T(8,128)} custom-call(f32[16,32,256]{2,1,0:T(8,128)} %bitcast.56), custom_call_target="tpu_custom_call" | custom-call | tf_op jit(solution)/shard_map/while/body/pallas_call | solution.py:102
  196.0 1.1 bitcast_reduce_fusion.2
  197.8 0.2 broadcast_in_dim.110
  198.0 11.7 %while.25 = (s32[]{:T(128)}, f32[3,8,64,256]{3,2,1,0:T(8,128)S(1)}, s32[]{:T(128)}, f32[4,64,256]{2,1,0:T(8,128)S(1)}, s32[]{:T(128)}, /*index=5*/s32[]{:T(128)}, s32[]{:T(128)}, s32[]{:T(128)}) while((s32[]{:T(128)}, f32[3,8,64,256]{3,2,1,0:T(8,128)S(1)}, s32[]{:T(128)}, f32[4,64,256]{2,1,0:T(8,128)S(1)}, s32[]{:T(128)}, ...), condition=%wide.region_9.10_spmd, body=%wide.region_8.9_spmd.sunk | while | flops 8 | bytes 1179817 | solution.py:348
  198.0 0.6 dynamic-slice_bitcast_fusion.2.own_ref
  198.7 9.9 %body.14 = f32[8,64,256]{2,1,0:T(8,128)} custom-call(f32[64,256]{1,0:T(8,128)} %dynamic-slice_bitcast_fusion.2.own_ref), custom_call_target="tpu_custom_call" | custom-call | tf_op jit(solution)/shard_map/while/body/pallas_call | solution.py:226
  208.6 1.1 bitcast_dynamic-update-slice_fusion.5
  209.7 0.1 compare_select_fusion
  209.8 0.6 gather_fusion.1
  210.4 0.1 dynamic_slice.34
  210.5 0.1 broadcast_in_dim.99
  210.6 0.1 broadcast_in_dim.100
  210.7 0.1 dynamic-slice_compare_fusion
  210.7 0.1 broadcast_in_dim.97
  210.8 0.1 eq.89
  210.9 0.8 fusion.2
  (40 shorter events, 0.3 us)
Async XLA Ops:
  0.7 0.6 copy-start.7
  2.3 34.7 %copy-start.5 = (pred[32]{0:T(512)(128)(4,1)}, pred[32]{0:T(512)(128)(4,1)S(1)}, u32[]{:S(2)}) copy-start(pred[32]{0:T(512)(128)(4,1)S(1)} %get-tuple-element.307) | copy-start | bytes 100
  3.2 33.8 %copy-start.9 = (s32[32]{0:T(128)}, s32[32]{0:T(128)S(1)}, u32[]{:S(2)}) copy-start(s32[32]{0:T(128)S(1)} %get-tuple-element.309) | copy-start | bytes 388
  37.0 7.2 %copy-start.1 = (s32[4,20736]{1,0:T(4,128)S(1)}, s32[4,20736]{1,0:T(4,128)}, u32[]{:S(2)}) copy-start(s32[4,20736]{1,0:T(4,128)} %param.18) | copy-start | bytes 995332
  37.0 7.3 %copy-start.4 = (s32[4,324]{1,0:T(4,128)S(1)}, s32[4,324]{1,0:T(4,128)}, u32[]{:S(2)}) copy-start(s32[4,324]{1,0:T(4,128)} %param.17) | copy-start | bytes 15556
  52.1 3.5 %copy-start.3 = (bf16[324,324]{1,0:T(8,128)(2,1)S(1)}, bf16[324,324]{1,0:T(8,128)(2,1)}, u32[]{:S(2)}) copy-start(bf16[324,324]{1,0:T(8,128)(2,1)} %param.14) | copy-start | bytes 629860
  198.0 11.8 %copy-start.10 = (s32[32]{0:T(128)S(1)}, s32[32]{0:T(128)}, u32[]{:S(2)}) copy-start(s32[32]{0:T(128)} %copy-done.9) | copy-start | bytes 388
  198.0 12.4 %copy-start.6 = (pred[32]{0:T(512)(128)(4,1)S(1)}, pred[32]{0:T(512)(128)(4,1)}, u32[]{:S(2)}) copy-start(pred[32]{0:T(512)(128)(4,1)} %copy-done.5) | copy-start | bytes 100
  198.0 12.7 %copy-start.8 = (s32[32]{0:T(128)S(1)}, s32[32]{0:T(128)}, u32[]{:S(2)}) copy-start(s32[32]{0:T(128)} %copy-done.7) | copy-start | bytes 388
  198.0 12.9 %copy-start = (bf16[256,256]{1,0:T(8,128)(2,1)S(1)}, bf16[256,256]{1,0:T(8,128)(2,1)}, u32[]{:S(2)}) copy-start(bf16[256,256]{1,0:T(8,128)(2,1)} %own_ref.1) | copy-start | bytes 393220
  198.0 12.9 %copy-start.2 = (f32[256,256]{1,0:T(8,128)S(1)}, f32[256,256]{1,0:T(8,128)}, u32[]{:S(2)}) copy-start(f32[256,256]{1,0:T(8,128)} %param.13) | copy-start | bytes 786436

commit v20 on v19

--- a/solution.py
+++ b/solution.py
@@ -22,9 +22,7 @@
         mixed = jnp.dot(integ, picked_ref[row], preferred_element_type=jnp.float32)
         parts = []
         for half in range(halves):
-            weighted = mixed[:, half * width : (half + 1) * width] * sign_ref[half].astype(
-                jnp.float32
-            )
+            weighted = mixed[:, half * width : (half + 1) * width] * sign_ref[half]
             high = weighted.astype(jnp.bfloat16)
             low = (weighted - high.astype(jnp.float32)).astype(jnp.bfloat16)
             parts += [high, low]
@@ -273,7 +271,7 @@
         .transpose(0, 2, 1, 3)
         .reshape(PAIR, pair_count, local_cols)
     )
-    sign_q = jnp.pad(sign_q, ((0, 0), (0, extra), (0, 0))).astype(jnp.bfloat16)
+    sign_q = jnp.pad(sign_q, ((0, 0), (0, extra), (0, 0))).astype(jnp.float32)
     target_iota = jnp.arange(total_blocks, dtype=jnp.int32)
     table_all = (target_iota[None, :, None] == beta_block2[:, None, :]).astype(jnp.bfloat16)
     table_all = jnp.pad(

time: 213 us -> 213 us (level)
    while x2 -> x3, local copies, waits for them, and re-layouts: 6.94 us -> 7.19 us  [on_device(): done = lax.fori_loop(0, my_count, one_block, empty)]
where the time goes in v20:
time: 213 us; the launch traced here: 212 us
  Pallas kernels  101 us (47%)
  local copies, waits for them, and re-layouts  86.9 us (41%)
  other arithmetic  17.7 us (8%)
  between operations  2.34 us (1%)
    gather x2, local copies, waits for them, and re-layouts, one_block(): lax.gather(coeff_ext, row_ids[:, :, None], dims, slice_sizes=(1, wide_col...  67.6 us
    pallas_call x2, Pallas kernels, mix_block(): pl.pallas_call(mix_kernel, out_shape=jax.ShapeDtypeStruct((rows, targets,...  35.4 us
    pallas_call x1, Pallas kernels, spread(): pl.pallas_call(spread_kernel, out_shape=jax.ShapeDtypeStruct((count // PA...  29.4 us
    pallas_call x2, Pallas kernels, exchange(): pl.pallas_call(exchange_kernel, out_shape=jax.ShapeDtypeStruct(send.shape...  26.7 us
    pallas_call x1, Pallas kernels, gather_alpha(): pl.pallas_call(gather_alpha_kernel, out_shape=jax.ShapeDtypeStruct((count...  9.92 us
    while x3, local copies, waits for them, and re-layouts, on_device(): done = lax.fori_loop(0, my_count, one_block, empty)  7.19 us
    concatenate x1, other arithmetic, on_device(): jnp.concatenate([gathered, -gathered, jnp.zeros((16, wide_cols), jnp.bflo...  7.18 us
    reshape x4, local copies, waits for them, and re-layouts, one_block(): part = summed.reshape(sub_rows, beta_size, local_cols).transpose(1, 0, 2)  5.21 us

profile of v20, /device:TPU:1, one launch (start us, length us, event | category | flops | bytes accessed | tf_op | source)
XLA Modules:
  0.0 211.9 jit_solution(9555940836080012597)
XLA Ops:
  0.0 0.7 compare_convert_fusion
  0.7 0.6 copy-done.7
  1.2 0.1 reshape.83
  1.3 0.2 reduce_window_sum.18
  1.5 0.1 eq.92
  1.6 0.7 broadcast_compare_fusion.1
  2.3 0.1 copy.23
  2.3 0.1 reduce-window.9
  2.4 0.1 reduce.18
  2.5 0.6 fusion.7
  3.8 0.8 iota_reduce_fusion
  5.3 0.1 select_reduce_fusion
  5.4 0.1 broadcast_in_dim.105
  5.5 0.1 convert_element_type.40
  5.6 29.4 %shard_map.82 = bf16[2048,512]{1,0:T(8,128)(2,1)} custom-call(bf16[256,256]{1,0:T(8,128)(2,1)} %own_ref.1), custom_call_target="tpu_custom_call" | custom-call | tf_op jit(solution)/shard_map/pallas_call | solution.py:167
  35.0 1.9 fusion.6
  37.0 7.2 %maximum_maximum_fusion = bf16[4112,512]{1,0:T(8,128)(2,1)} fusion(bf16[2048,512]{1,0:T(8,128)(2,1)S(1)} %get-tuple-element.301, bf16[2048,512]{1,0:T(8,128)(2,1)S(1)} %get-tuple-element.302, bf16[4112]{0:T(1024)(128)(2,1)S(1)} %pad.30.clone), kind=kLoop, calls=%fused_computation.11 | loop fusion | flops 12632064 | bytes 8413216 | tf_op jit(solution)/shard_map/concatenate | solution.py:259
  44.2 0.1 convert.8
  44.3 0.1 maximum_bitcast_fusion
  44.4 2.0 all-gather
  46.4 0.1 reshape.109
  46.6 0.1 eq.98
  46.7 0.2 bitcast_compare_fusion
  46.9 0.1 pad_convert_fusion
  47.0 0.6 concatenate.12
  47.7 0.4 reshape.86
  48.1 0.3 copy.24
  48.4 0.1 pad_convert_fusion.1
  48.4 0.3 copy.27
  48.7 3.5 %copy.25 = s32[324,2048]{0,1:T(8,128)} copy(s32[324,2048]{1,0:T(8,128)} %param.16) | data formatting | bytes 5308416 | tf_op jit(solution)/shard_map/while | solution.py:339
  52.2 3.5 %copy.26 = s32[324,2048]{0,1:T(8,128)} copy(s32[324,2048]{1,0:T(8,128)} %param.15) | data formatting | bytes 5308416 | tf_op jit(solution)/shard_map/while | solution.py:339
  55.7 141.6 %while.24 = (s32[]{:T(128)}, f32[4,64,256]{2,1,0:T(8,128)S(1)}, s32[]{:T(128)}, s32[]{:T(128)}, s32[32]{0:T(128)S(1)}, /*index=5*/s32[]{:T(128)}, s32[]{:T(128)}...) while((s32[]{:T(128)}, f32[4,64,256]{2,1,0:T(8,128)S(1)}, ...), condition=%wide.region_7.8_spmd, body=%wide.region_5.7_spmd.sunk | while | flops 177811 | bytes 25264532 | solution.py:339
  55.9 0.6 dynamic_slice.48
  57.0 0.8 fusion.9
  57.9 0.1 reshape.117
  58.0 33.8 %gather_fusion = bf16[10752,512]{1,0:T(8,128)(2,1)} fusion(bf16[4112,512]{1,0:T(8,128)(2,1)} %get-tuple-element.468, s32[11264]{0:T(1024)S(1)} %pad_clamp_fusion.3), kind=kCustom, calls=%fused_computation.clone.1 | custom fusion | bytes 22063104 | tf_op jit(solution)/shard_map/while/body/gather | solution.py:324
  91.8 17.7 %body.12 = f32[32,64,64]{2,1,0:T(8,128)} custom-call(bf16[336,336]{1,0:T(8,128)(2,1)S(1)} %get-tuple-element.469.integ_ref, bf16[32,336,512]{2,1,0:T(8,128)(2,1)} %bitcast.55, f32[2,336,256]{2,1,0:T(8,128)S(1)} %get-tuple-element.470.sign_ref, bf16[256,1344]{1,0:T(8,128)(2,1)S(1)} %get-tuple-element.471.table_ref), custom_call_target="tpu_custom_call" | custom-call | tf_op jit(solution)/shard_map/while/body/pallas_call | solution.py:44
  109.5 1.5 reshape.118
  111.0 1.1 copy.31
  112.1 13.5 %body.13 = f32[16,32,256]{2,1,0:T(8,128)} custom-call(f32[16,32,256]{2,1,0:T(8,128)} %bitcast.56), custom_call_target="tpu_custom_call" | custom-call | tf_op jit(solution)/shard_map/while/body/pallas_call | solution.py:100
  125.6 1.1 bitcast_reduce_fusion.2
  126.8 0.6 dynamic_slice.48
  127.9 0.8 fusion.9
  128.8 0.1 reshape.117
  128.9 33.8 %gather_fusion = bf16[10752,512]{1,0:T(8,128)(2,1)} fusion(bf16[4112,512]{1,0:T(8,128)(2,1)} %get-tuple-element.468, s32[11264]{0:T(1024)S(1)} %pad_clamp_fusion.3), kind=kCustom, calls=%fused_computation.clone.1 | custom fusion | bytes 22063104 | tf_op jit(solution)/shard_map/while/body/gather | solution.py:324
  162.7 17.7 %body.12 = f32[32,64,64]{2,1,0:T(8,128)} custom-call(bf16[336,336]{1,0:T(8,128)(2,1)S(1)} %get-tuple-element.469.integ_ref, bf16[32,336,512]{2,1,0:T(8,128)(2,1)} %bitcast.55, f32[2,336,256]{2,1,0:T(8,128)S(1)} %get-tuple-element.470.sign_ref, bf16[256,1344]{1,0:T(8,128)(2,1)S(1)} %get-tuple-element.471.table_ref), custom_call_target="tpu_custom_call" | custom-call | tf_op jit(solution)/shard_map/while/body/pallas_call | solution.py:44
  180.4 1.5 reshape.118
  181.9 1.1 copy.31
  183.0 13.2 %body.13 = f32[16,32,256]{2,1,0:T(8,128)} custom-call(f32[16,32,256]{2,1,0:T(8,128)} %bitcast.56), custom_call_target="tpu_custom_call" | custom-call | tf_op jit(solution)/shard_map/while/body/pallas_call | solution.py:100
  196.2 1.1 bitcast_reduce_fusion.2
  197.9 0.2 broadcast_in_dim.110
  198.2 11.7 %while.25 = (s32[]{:T(128)}, f32[3,8,64,256]{3,2,1,0:T(8,128)S(1)}, s32[]{:T(128)}, f32[4,64,256]{2,1,0:T(8,128)S(1)}, s32[]{:T(128)}, /*index=5*/s32[]{:T(128)}, s32[]{:T(128)}, s32[]{:T(128)}) while((s32[]{:T(128)}, f32[3,8,64,256]{3,2,1,0:T(8,128)S(1)}, s32[]{:T(128)}, f32[4,64,256]{2,1,0:T(8,128)S(1)}, s32[]{:T(128)}, ...), condition=%wide.region_9.10_spmd, body=%wide.region_8.9_spmd.sunk | while | flops 8 | bytes 1179817 | solution.py:346
  198.2 0.6 dynamic-slice_bitcast_fusion.2.own_ref
  198.8 9.9 %body.14 = f32[8,64,256]{2,1,0:T(8,128)} custom-call(f32[64,256]{1,0:T(8,128)} %dynamic-slice_bitcast_fusion.2.own_ref), custom_call_target="tpu_custom_call" | custom-call | tf_op jit(solution)/shard_map/while/body/pallas_call | solution.py:224
  208.8 1.1 bitcast_dynamic-update-slice_fusion.5
  209.9 0.1 compare_select_fusion
  210.0 0.6 gather_fusion.1
  210.6 0.1 dynamic_slice.34
  210.7 0.1 broadcast_in_dim.99
  210.7 0.1 broadcast_in_dim.100
  210.8 0.1 dynamic-slice_compare_fusion
  210.9 0.1 broadcast_in_dim.97
  211.0 0.1 eq.89
  211.1 0.8 fusion.2
  (40 shorter events, 0.3 us)
Async XLA Ops:
  0.7 0.6 copy-start.7
  2.3 34.7 %copy-start.5 = (pred[32]{0:T(512)(128)(4,1)}, pred[32]{0:T(512)(128)(4,1)S(1)}, u32[]{:S(2)}) copy-start(pred[32]{0:T(512)(128)(4,1)S(1)} %get-tuple-element.307) | copy-start | bytes 100
  3.2 33.8 %copy-start.9 = (s32[32]{0:T(128)}, s32[32]{0:T(128)S(1)}, u32[]{:S(2)}) copy-start(s32[32]{0:T(128)S(1)} %get-tuple-element.309) | copy-start | bytes 388
  37.0 7.2 %copy-start.1 = (s32[4,20736]{1,0:T(4,128)S(1)}, s32[4,20736]{1,0:T(4,128)}, u32[]{:S(2)}) copy-start(s32[4,20736]{1,0:T(4,128)} %param.18) | copy-start | bytes 995332
  37.0 7.3 %copy-start.4 = (s32[4,324]{1,0:T(4,128)S(1)}, s32[4,324]{1,0:T(4,128)}, u32[]{:S(2)}) copy-start(s32[4,324]{1,0:T(4,128)} %param.17) | copy-start | bytes 15556
  52.2 3.5 %copy-start.3 = (bf16[324,324]{1,0:T(8,128)(2,1)S(1)}, bf16[324,324]{1,0:T(8,128)(2,1)}, u32[]{:S(2)}) copy-start(bf16[324,324]{1,0:T(8,128)(2,1)} %param.14) | copy-start | bytes 629860
  198.1 11.8 %copy-start.10 = (s32[32]{0:T(128)S(1)}, s32[32]{0:T(128)}, u32[]{:S(2)}) copy-start(s32[32]{0:T(128)} %copy-done.9) | copy-start | bytes 388
  198.1 12.4 %copy-start.6 = (pred[32]{0:T(512)(128)(4,1)S(1)}, pred[32]{0:T(512)(128)(4,1)}, u32[]{:S(2)}) copy-start(pred[32]{0:T(512)(128)(4,1)} %copy-done.5) | copy-start | bytes 100
  198.1 12.7 %copy-start.8 = (s32[32]{0:T(128)S(1)}, s32[32]{0:T(128)}, u32[]{:S(2)}) copy-start(s32[32]{0:T(128)} %copy-done.7) | copy-start | bytes 388
  198.1 12.9 %copy-start = (bf16[256,256]{1,0:T(8,128)(2,1)S(1)}, bf16[256,256]{1,0:T(8,128)(2,1)}, u32[]{:S(2)}) copy-start(bf16[256,256]{1,0:T(8,128)(2,1)} %own_ref.1) | copy-start | bytes 393220
  198.2 12.9 %copy-start.2 = (f32[256,256]{1,0:T(8,128)S(1)}, f32[256,256]{1,0:T(8,128)}, u32[]{:S(2)}) copy-start(f32[256,256]{1,0:T(8,128)} %param.13) | copy-start | bytes 786436
